TPU v7x, 128 devices: a whole 4x4x4 slice. The times are simulated.
128 devices in a mesh: row: 8 (over y_hi, x), col: 16 (over z, y_lo, core).
Axes of the slice: x: 4, y: 4 (y_hi: 2, y_lo: 2; y = y_hi * 2 + y_lo), z: 4, core: 2. Of those that a mesh axis runs over, the one named last changes fastest.
Arguments:
- features: bfloat16 [64, 1024, 1024], P(None, 'col', 'row'), may hold values from -120 to 120
- conv_first: bfloat16 [9, 64, 64], replicated, may hold values from -0.25 to 0.25
- conv_second: bfloat16 [9, 64, 64], replicated, may hold values from -0.25 to 0.25
- head_weight: bfloat16 [37, 64], replicated, may hold values from -0.75 to 0.75
- head_bias: float32 [37], replicated, may hold values from -4 to 4
- cotangent: bfloat16 [37, 1024, 1024], P(None, 'col', 'row'), may hold values from -6 to 6
Outputs:
- logits: bfloat16 [37, 1024, 1024], P(None, 'col', 'row')
- input_grad: bfloat16 [64, 1024, 1024], P(None, 'col', 'row')
- grad_first: float32 [9, 64, 64], replicated
- grad_second: float32 [9, 64, 64], replicated
- grad_head: float32 [37, 64], replicated
- grad_bias: float32 [37], replicated
All inputs are finite; a program needn't handle non-finite values.
Results may differ from a plain program's by a relative error of at most 0.007.
Values may be sent and summed in bfloat16 or wider, within the bound.
No kernel may reach another device: no remote copies, remote signals or barrier semaphores. Data moves between devices by JAX's collectives and lax.ppermute only.
A program may use at most 128 MiB of HBM per device.

v0:
```python
import jax
import jax.numpy as jnp
from jax import lax
from jax.sharding import PartitionSpec as P

DILATION_STEP = 16


epsilon = 1e-05


def with_halo(block, sides, width):
    for axis, dim in sides:
        count = lax.axis_size(axis)
        forward = [(i, i + 1) for i in range(count - 1)]
        backward = [(target, source) for source, target in forward]
        low = lax.ppermute(
            lax.slice_in_dim(block, block.shape[dim] - width, None, axis=dim), axis, forward
        )
        high = lax.ppermute(lax.slice_in_dim(block, 0, width, axis=dim), axis, backward)
        block = jnp.concatenate([low, block, high], axis=dim)
    return block


def as_sent(shard):

    def short(part):
        return part.astype(jnp.bfloat16) if part.dtype == jnp.float32 else part

    return jax.tree.map(short, shard)


def elu_apply(value_entries):
    return jnp.where(
        value_entries > 0, value_entries, jnp.exp(jnp.minimum(value_entries, 0.0)) - 1.0
    )


def elu_slope(value_entries):
    return jnp.where(value_entries > 0, 1.0, jnp.exp(jnp.minimum(value_entries, 0.0)))


def widen(value_entries):
    return with_halo(value_entries, (("row", 2), ("col", 1)), DILATION_STEP)


def widen_grad(value_entries):
    return with_halo(value_entries, (("row", 2), ("col", 1)), DILATION_STEP)


def tap_window(padded, kernel_row, kernel_column, adjoint, col_count, row_count):
    shift_direction = -1 if adjoint else 1
    column_shift = DILATION_STEP + shift_direction * DILATION_STEP * (kernel_column - 1)
    row_shift = DILATION_STEP + shift_direction * DILATION_STEP * (kernel_row - 1)
    window = padded[:, column_shift : column_shift + col_count, row_shift : row_shift + row_count]
    return window.reshape(padded.shape[0], col_count * row_count)


def convolve(padded, weights, col_count, row_count, adjoint):
    running = jnp.zeros((weights.shape[1], col_count * row_count), jnp.float32)
    for kernel_row in range(3):
        for kernel_column in range(3):
            window = tap_window(padded, kernel_row, kernel_column, adjoint, col_count, row_count)
            matrix = weights[3 * kernel_row + kernel_column]
            if adjoint:
                matrix = matrix.T
            running = running + jnp.dot(matrix, window, preferred_element_type=jnp.float32)
    return running.reshape(-1, col_count, row_count)


def weight_terms(gradient, padded, col_count, row_count):
    flattened = gradient.reshape(gradient.shape[0], -1)
    collected = []
    for kernel_row in range(3):
        for kernel_column in range(3):
            window = tap_window(padded, kernel_row, kernel_column, False, col_count, row_count)
            collected.append(
                lax.dot_general(
                    flattened, window, (((1,), (1,)), ((), ())), preferred_element_type=jnp.float32
                )
            )
    return jnp.stack(collected, 0)


def normalize(activation, cell_count):
    totals = lax.psum(jnp.sum(activation, axis=(1, 2)), ("row", "col"))
    average = totals / cell_count
    centered = activation - average[:, None, None]
    spread = lax.psum(jnp.sum(centered * centered, axis=(1, 2)), ("row", "col")) / cell_count
    inverse_std = lax.rsqrt(spread + epsilon)
    return (centered * inverse_std[:, None, None], inverse_std)


def norm_back(gradient, normed, inverse_std, cell_count):
    first_sum, second_sum = lax.psum(
        (jnp.sum(gradient, axis=(1, 2)), jnp.sum(gradient * normed, axis=(1, 2))), ("row", "col")
    )
    first_mean = first_sum / cell_count
    second_mean = second_sum / cell_count
    return inverse_std[:, None, None] * (
        gradient - first_mean[:, None, None] - normed * second_mean[:, None, None]
    )


def mirror_prepare(tensor, col_devices):
    planes, col_count, row_count = tensor.shape
    slab_rows = row_count // col_devices
    shaped = tensor.reshape(planes, col_count, col_devices, slab_rows).transpose(2, 1, 0, 3)
    return shaped.reshape(col_devices, col_count, planes * slab_rows)


def mirror_middle(received):
    return received.reshape(received.shape[1], 1, received.shape[2])


def mirror_tail(received, col_devices, row_devices):
    return received.reshape(received.shape[0], col_devices, row_devices, received.shape[2])


def mirror_finish(received, planes, row_devices):
    row_count = received.shape[0]
    slab_rows = received.shape[3] // planes
    shaped = received.reshape(row_count, row_devices, planes, slab_rows).transpose(2, 1, 3, 0)
    return shaped.reshape(planes, row_devices * slab_rows, row_count)


def mirror_half(tensors):
    col_devices = lax.axis_size("col")
    row_devices = lax.axis_size("row")
    planes = tuple((member.shape[0] for member in tensors))
    first = lax.all_to_all(
        as_sent(tuple((mirror_prepare(member, col_devices) for member in tensors))),
        "col",
        split_axis=0,
        concat_axis=1,
        tiled=True,
    )
    second = lax.all_to_all(
        as_sent(tuple((mirror_middle(member) for member in first))),
        ("row", "col"),
        split_axis=0,
        concat_axis=1,
        tiled=True,
    )
    third = lax.all_to_all(
        as_sent(tuple((mirror_tail(member, col_devices, row_devices) for member in second))),
        "col",
        split_axis=1,
        concat_axis=0,
        tiled=True,
    )
    return tuple(
        (
            mirror_finish(member, count_planes, row_devices)
            for member, count_planes in zip(third, planes)
        )
    )


def mirror_full(tensors):
    col_devices = lax.axis_size("col")
    row_devices = lax.axis_size("row")
    planes = tuple((member.shape[0] for member in tensors))
    first = lax.all_to_all(
        tuple((mirror_prepare(member, col_devices) for member in tensors)),
        "col",
        split_axis=0,
        concat_axis=1,
        tiled=True,
    )
    second = lax.all_to_all(
        tuple((mirror_middle(member) for member in first)),
        ("row", "col"),
        split_axis=0,
        concat_axis=1,
        tiled=True,
    )
    third = lax.all_to_all(
        tuple((mirror_tail(member, col_devices, row_devices) for member in second)),
        "col",
        split_axis=1,
        concat_axis=0,
        tiled=True,
    )
    return tuple(
        (
            mirror_finish(member, count_planes, row_devices)
            for member, count_planes in zip(third, planes)
        )
    )


def on_device(features, conv_first, conv_second, head_weight, head_bias, cotangent):
    channels, col_count, row_count = features.shape
    length = col_count * lax.axis_size("col")
    cell_count = float(length * length)
    cot_mirror = mirror_half((cotangent,))[0]
    wide_in = widen(features)
    act_first = convolve(wide_in, conv_first, col_count, row_count, False)
    normed_first, inverse_first = normalize(act_first, cell_count)
    hidden_first = elu_apply(normed_first).astype(jnp.bfloat16)
    wide_hidden = widen(hidden_first)
    act_second = convolve(wide_hidden, conv_second, col_count, row_count, False)
    normed_second, inverse_second = normalize(act_second, cell_count)
    summed = normed_second + features.astype(jnp.float32)
    hidden = elu_apply(summed).astype(jnp.bfloat16)
    flat_hidden = hidden.reshape(channels, -1)
    raw_logits = (
        jnp.dot(head_weight, flat_hidden, preferred_element_type=jnp.float32) + head_bias[:, None]
    ).reshape(-1, col_count, row_count)
    logit_mirror = mirror_full((raw_logits,))[0]
    logits = (0.5 * (raw_logits + logit_mirror)).astype(jnp.bfloat16)
    grad_sym = (0.5 * (cotangent.astype(jnp.float32) + cot_mirror.astype(jnp.float32))).astype(
        jnp.bfloat16
    )
    flat_sym = grad_sym.reshape(grad_sym.shape[0], -1)
    bias_term = jnp.sum(flat_sym, axis=1, dtype=jnp.float32)
    head_term = lax.dot_general(
        flat_sym, flat_hidden, (((1,), (1,)), ((), ())), preferred_element_type=jnp.float32
    )
    grad_hidden = jnp.dot(head_weight.T, flat_sym, preferred_element_type=jnp.float32).reshape(
        channels, col_count, row_count
    )
    grad_summed = grad_hidden * elu_slope(summed)
    grad_act_second = norm_back(grad_summed, normed_second, inverse_second, cell_count).astype(
        jnp.bfloat16
    )
    second_term = weight_terms(grad_act_second, wide_hidden, col_count, row_count)
    grad_hidden_first = convolve(
        widen_grad(grad_act_second), conv_second, col_count, row_count, True
    )
    grad_normed_first = grad_hidden_first * elu_slope(normed_first)
    grad_act_first = norm_back(grad_normed_first, normed_first, inverse_first, cell_count).astype(
        jnp.bfloat16
    )
    first_term = weight_terms(grad_act_first, wide_in, col_count, row_count)
    input_grad = (
        convolve(widen_grad(grad_act_first), conv_first, col_count, row_count, True) + grad_summed
    ).astype(jnp.bfloat16)
    reduced = lax.psum((first_term, second_term, head_term, bias_term), ("row", "col"))
    inverse_len = 1.0 / length
    return (
        logits,
        input_grad,
        reduced[0] * inverse_len,
        reduced[1] * inverse_len,
        reduced[2] * inverse_len,
        reduced[3] * inverse_len,
    )


def solution(mesh):
    placed = (P(None, "col", "row"), P(), P(), P(), P(), P(None, "col", "row"))
    return jax.shard_map(
        on_device,
        mesh=mesh,
        in_specs=placed,
        out_specs=(P(None, "col", "row"), P(None, "col", "row"), P(), P(), P(), P()),
        check_vma=False,
    )
```

profile of v0, /device:TPU:1, one launch (start us, length us, event | category | flops | bytes accessed | tf_op | source)
XLA Modules:
  0.0 945.5 jit_solution(8504347659862040630)
XLA Ops:
  12.6 5.3 collective-permute-start
  21.0 7.8 all-to-all-start.3
  45.4 7.2 collective-permute-done.3
  63.5 67.2 %psum.84 = f32[64]{0:T(128)S(1)} all-reduce(f32[64]{0:T(128)S(1)} %get-tuple-element.108), channel_id=1, replica_groups=mesh['row'=8,'col'=16] {'row','col'}, use_global_device_ids=true, to_apply=%region_1.0 | all-reduce | flops 64 | bytes 512 | tf_op jit(solution)/shard_map/psum | solution.py:86
  131.1 63.5 %psum.85 = f32[64]{0:T(128)S(1)} all-reduce(f32[64]{0:T(128)S(1)} %multiply_reduce_fusion.2), channel_id=1, replica_groups=mesh['row'=8,'col'=16] {'row','col'}, use_global_device_ids=true, to_apply=%region_3.0 | all-reduce | flops 64 | bytes 512 | tf_op jit(solution)/shard_map/psum | solution.py:89
  209.8 4.3 collective-permute-done.5
  233.1 11.2 %all-to-all-start.4 = ((bf16[128,2,1184]{2,1,0:T(2,128)(2,1)}), bf16[128,2,1184]{2,1,0:T(2,128)(2,1)}, u32[]{:S(2)}, u32[]{:S(2)}) async-start(bf16[128,2,1184]{2,1,0:T(2,128)(2,1)} %reshape.289), calls=%async_computation.4 | async-start | bytes 1310720 | tf_op jit(solution)/shard_map/all_to_all | solution.py:138
  247.3 4.2 pad_maximum_fusion.1
  260.6 67.2 %psum.86 = f32[64]{0:T(128)S(1)} all-reduce(f32[64]{0:T(128)S(1)} %get-tuple-element.110), channel_id=1, replica_groups=mesh['row'=8,'col'=16] {'row','col'}, use_global_device_ids=true, to_apply=%region_5.6 | all-reduce | flops 64 | bytes 512 | tf_op jit(solution)/shard_map/psum | solution.py:86
  327.7 6.2 reshape.290
  336.5 4.3 all-to-all-start.5
  342.8 65.3 %psum.87 = f32[64]{0:T(128)S(1)} all-reduce(f32[64]{0:T(128)S(1)} %fusion.19), channel_id=1, replica_groups=mesh['row'=8,'col'=16] {'row','col'}, use_global_device_ids=true, to_apply=%region_7.8 | all-reduce | flops 64 | bytes 512 | tf_op jit(solution)/shard_map/psum | solution.py:89
  409.4 12.2 %reshape.288 = f32[128,8,37,8]{3,2,1,0:T(8,128)} reshape(f32[16,8,1,8,296]{4,3,1,0,2:T(8,128)} %convert_bitcast_fusion) | data formatting | bytes 2424832 | tf_op jit(solution)/shard_map/convert_element_type | solution.py:213
  421.5 11.1 %copy.273 = f32[37,8,8,128]{3,2,1,0:T(8,128)S(1)} copy(f32[37,8,8,128]{2,0,1,3:T(8,128)} %bitcast.528) | data formatting | bytes 2424832 | tf_op jit(solution)/shard_map/convert_element_type | solution.py:213
  439.4 62.9 %all-reduce.1 = (f32[64]{0:T(128)S(1)}, f32[64]{0:T(128)S(1)}) all-reduce(f32[64]{0:T(128)S(1)} %get-tuple-element.39, f32[64]{0:T(128)S(1)} %get-tuple-element.38), channel_id=1, replica_groups=mesh['row'=8,'col'=16] {'row','col'}, use_global_device_ids=true, to_apply=%region_11.12 | all-reduce | flops 128 | bytes 1024 | tf_op jit(solution)/shard_map/psum | solution.py:95
  524.1 4.7 collective-permute-start.8
  538.7 5.1 copy.259
  546.9 5.3 all-to-all-start
  568.5 8.1 collective-permute-done.11
  576.5 7.2 collective-permute-done.10
  595.0 67.2 %all-reduce = (f32[64]{0:T(128)S(1)}, f32[64]{0:T(128)S(1)}, f32[37,64]{1,0:T(8,128)S(1)}, f32[37]{0:T(128)S(1)}) all-reduce(f32[64]{0:T(128)S(1)} %get-tuple-element.37, f32[64]{0:T(128)S(1)} %get-tuple-element.36, f32[37,64]{1,0:T(8,128)S(1)} %convolution_bitcast_fusion.23, ...), channel_id=1, replica_groups=mesh['row'=8,'col'=16] {'row','col'}, use_global_device_ids=true, to_apply=%region_15.16 | all-reduce | flops 2533 | bytes 20264 | tf_op jit(solution)/shard_map/psum | solution.py:95
  680.8 5.1 collective-permute-start.12
  699.2 4.6 collective-permute-start.15
  708.2 125.5 %all-reduce.5.cloned.1.call-done = (f32[9,64,64]{2,1,0:T(8,128)}, f32[9,64,64]{2,1,0:T(8,128)}) async-done(((f32[9,64,64]{2,1,0:T(8,128)}, f32[9,64,64]{2,1,0:T(8,128)}), (f32[9,64,64]{2,1,0:T(8,128)}, f32[9,64,64]{2,1,0:T(8,128)})) %all-reduce.5.cloned.1.call-update) | async-done | bytes 294928 | tf_op jit(solution)/shard_map/psum | solution.py:240
  837.1 4.8 maximum_maximum_fusion.3
  848.5 4.2 copy.261
  852.7 7.4 all-to-all-start.1
  866.1 17.9 %all-to-all-done.1 = f32[1024,1,296]{2,1,0:T(1,128)} async-done(((f32[1024,1,296]{2,1,0:T(1,128)}), f32[1024,1,296]{2,1,0:T(1,128)}, u32[]{:S(2)}, u32[]{:S(2)}) %all-to-all-start.1) | async-done | bytes 1212448 | tf_op jit(solution)/shard_map/all_to_all | solution.py:171
  887.0 5.5 all-to-all-start.2
  898.6 15.5 %all-to-all-done.2 = f32[8,16,8,296]{3,2,0,1:T(8,128)} async-done(((f32[8,16,8,296]{3,2,0,1:T(8,128)}), f32[8,16,8,296]{3,2,0,1:T(8,128)}, u32[]{:S(2)}, u32[]{:S(2)}) %all-to-all-start.2) | async-done | bytes 1212448 | tf_op jit(solution)/shard_map/all_to_all | solution.py:178
  914.1 12.2 %reshape.287 = f32[128,8,37,8]{3,2,1,0:T(8,128)} reshape(f32[16,8,1,8,296]{4,3,1,0,2:T(8,128)} %bitcast.32) | data formatting | bytes 2424832 | tf_op jit(solution)/shard_map/reshape | solution.py:123
  926.2 11.2 %copy.265 = f32[37,8,8,128]{3,2,1,0:T(8,128)S(1)} copy(f32[37,8,8,128]{2,0,1,3:T(8,128)} %bitcast.529) | data formatting | bytes 2424832 | tf_op jit(solution)/shard_map/transpose | solution.py:123
  (261 shorter events, 219.1 us)
Async XLA Ops:
  7.2 427.7 %copy-start = (bf16[37,64]{1,0:T(8,128)(2,1)S(1)}, bf16[37,64]{1,0:T(8,128)(2,1)}, u32[]{:S(2)}) copy-start(bf16[37,64]{1,0:T(8,128)(2,1)} %param.9) | copy-start | bytes 14212
  10.3 22.0 %collective-permute-start.1 = (bf16[64,64,16]{1,2,0:T(8,128)(2,1)}, bf16[64,64,16]{1,2,0:T(8,128)(2,1)}, u32[]{:S(2)}, u32[]{:S(2)}) collective-permute-start(bf16[64,64,16]{1,2,0:T(8,128)(2,1)} %copy.320), channel_id=1, source_target_pairs={{16,0},{32,16},{48,32},{64,48},{80,64},{96,80},{112,96},{17,1},{33... | collective-permute-start | bytes 393224 | tf_op jit(solution)/shard_map/ppermute | solution.py:20
  12.6 16.9 %collective-permute-start = (bf16[64,64,16]{1,2,0:T(8,128)(2,1)}, bf16[64,64,16]{1,2,0:T(8,128)(2,1)}, u32[]{:S(2)}, u32[]{:S(2)}) collective-permute-start(bf16[64,64,16]{1,2,0:T(8,128)(2,1)} %copy.319), channel_id=1, source_target_pairs={{0,16},{16,32},{32,48},{48,64},{64,80},{80,96},{96,112},{1,17},{17... | collective-permute-start | bytes 393224 | tf_op jit(solution)/shard_map/ppermute | solution.py:17
  21.0 205.0 %all-to-all-start.3 = ((bf16[16,64,296]{2,1,0:T(8,128)(2,1)}), bf16[16,64,296]{2,1,0:T(8,128)(2,1)}, u32[]{:S(2)}, u32[]{:S(2)}) async-start(bf16[16,64,296]{2,1,0:T(8,128)(2,1)} %copy.268), calls=%async_computation.3 | async-start | bytes 1572864 | tf_op jit(solution)/shard_map/all_to_all | solution.py:131
  29.6 23.1 %copy-start.4 = (bf16[64,64,128]{2,0,1:T(8,128)(2,1)}, bf16[64,64,128]{2,0,1:T(8,128)(2,1)S(1)}, u32[]{:S(2)}) copy-start(bf16[64,64,128]{2,0,1:T(8,128)(2,1)S(1)} %copy.226) | copy-start | bytes 3145732
  32.3 20.3 %copy-start.9 = (bf16[64,64,16]{2,0,1:T(8,128)(2,1)}, bf16[64,64,16]{2,0,1:T(8,128)(2,1)S(1)}, u32[]{:S(2)}) copy-start(bf16[64,64,16]{2,0,1:T(8,128)(2,1)S(1)} %copy.225) | copy-start | bytes 393220
  35.1 17.6 %copy-start.7 = (bf16[64,64,16]{2,0,1:T(8,128)(2,1)}, bf16[64,64,16]{2,0,1:T(8,128)(2,1)S(1)}, u32[]{:S(2)}) copy-start(bf16[64,64,16]{2,0,1:T(8,128)(2,1)S(1)} %copy.227) | copy-start | bytes 393220
  35.7 9.7 %collective-permute-start.2 = (bf16[64,16,160]{2,0,1:T(8,128)(2,1)S(1)}, bf16[64,16,160]{2,0,1:T(8,128)(2,1)S(1)}, u32[]{:S(2)}, u32[]{:S(2)}) collective-permute-start(bf16[64,16,160]{2,0,1:T(8,128)(2,1)S(1)} %get-tuple-element.66), channel_id=1, source_target_pairs={{0,1},{1,2},{2,3},{3,4},{4,5},{5,6},{6,7},{7,8},{8,9},{9,10},{10,1... | collective-permute-start | bytes 983048 | tf_op jit(solution)/shard_map/ppermute | solution.py:17
  39.3 13.3 %collective-permute-start.3 = (bf16[64,16,160]{2,0,1:T(8,128)(2,1)S(1)}, bf16[64,16,160]{2,0,1:T(8,128)(2,1)S(1)}, u32[]{:S(2)}, u32[]{:S(2)}) collective-permute-start(bf16[64,16,160]{2,0,1:T(8,128)(2,1)S(1)} %get-tuple-element.67), channel_id=1, source_target_pairs={{1,0},{2,1},{3,2},{4,3},{5,4},{6,5},{7,6},{8,7},{9,8},{10,9},{11,1... | collective-permute-start | bytes 983048 | tf_op jit(solution)/shard_map/ppermute | solution.py:20
  195.2 52.0 %copy-start.2 = (bf16[64,64,128]{2,0,1:T(8,128)(2,1)}, bf16[64,64,128]{2,0,1:T(8,128)(2,1)S(1)}, u32[]{:S(2)}) copy-start(bf16[64,64,128]{2,0,1:T(8,128)(2,1)S(1)} %fusion.5) | copy-start | bytes 3145732
  199.3 7.2 collective-permute-start.4
  205.2 8.9 collective-permute-start.5
  220.2 27.0 %collective-permute-start.7 = (bf16[64,16,160]{2,0,1:T(8,128)(2,1)}, bf16[64,16,160]{2,0,1:T(8,128)(2,1)}, u32[]{:S(2)}, u32[]{:S(2)}) collective-permute-start(bf16[64,16,160]{2,0,1:T(8,128)(2,1)} %get-tuple-element.62), channel_id=1, source_target_pairs={{1,0},{2,1},{3,2},{4,3},{5,4},{6,5},{7,6},{8,7},{9,8},{10,9},{11,1... | collective-permute-start | bytes 983048 | tf_op jit(solution)/shard_map/ppermute | solution.py:20
  224.1 23.1 %collective-permute-start.6 = (bf16[64,16,160]{2,0,1:T(8,128)(2,1)}, bf16[64,16,160]{2,0,1:T(8,128)(2,1)}, u32[]{:S(2)}, u32[]{:S(2)}) collective-permute-start(bf16[64,16,160]{2,0,1:T(8,128)(2,1)} %get-tuple-element.63), channel_id=1, source_target_pairs={{0,1},{1,2},{2,3},{3,4},{4,5},{5,6},{6,7},{7,8},{8,9},{9,10},{10,1... | collective-permute-start | bytes 983048 | tf_op jit(solution)/shard_map/ppermute | solution.py:17
  233.1 94.7 %all-to-all-start.4 = ((bf16[128,2,1184]{2,1,0:T(2,128)(2,1)}), bf16[128,2,1184]{2,1,0:T(2,128)(2,1)}, u32[]{:S(2)}, u32[]{:S(2)}) async-start(bf16[128,2,1184]{2,1,0:T(2,128)(2,1)} %reshape.289), calls=%async_computation.4 | async-start | bytes 1310720 | tf_op jit(solution)/shard_map/all_to_all | solution.py:138
  336.5 71.6 %all-to-all-start.5 = ((bf16[8,16,8,296]{3,2,0,1:T(8,128)(2,1)}), bf16[8,16,8,296]{3,2,0,1:T(8,128)(2,1)S(1)}, u32[]{:S(2)}, u32[]{:S(2)}) async-start(bf16[8,16,8,296]{3,2,0,1:T(8,128)(2,1)} %copy.271), calls=%async_computation.5 | async-start | bytes 1572864 | tf_op jit(solution)/shard_map/all_to_all | solution.py:145
  517.0 11.8 %copy-start.48 = (f32[37]{0:T(128)S(1)}, f32[37]{0:T(128)}, u32[]{:S(2)}) copy-start(f32[37]{0:T(128)} %param.10) | copy-start | bytes 448
  522.8 33.1 %collective-permute-start.9 = (bf16[64,64,16]{1,2,0:T(8,128)(2,1)}, bf16[64,64,16]{1,2,0:T(8,128)(2,1)}, u32[]{:S(2)}, u32[]{:S(2)}) collective-permute-start(bf16[64,64,16]{1,2,0:T(8,128)(2,1)} %copy.276), channel_id=1, source_target_pairs={{16,0},{32,16},{48,32},{64,48},{80,64},{96,80},{112,96},{17,1},{33... | collective-permute-start | bytes 393224 | tf_op jit(solution)/shard_map/ppermute | solution.py:20
  524.1 28.4 %collective-permute-start.8 = (bf16[64,64,16]{1,2,0:T(8,128)(2,1)}, bf16[64,64,16]{1,2,0:T(8,128)(2,1)}, u32[]{:S(2)}, u32[]{:S(2)}) collective-permute-start(bf16[64,64,16]{1,2,0:T(8,128)(2,1)} %copy.275), channel_id=1, source_target_pairs={{0,16},{16,32},{32,48},{48,64},{64,80},{80,96},{96,112},{1,17},{17... | collective-permute-start | bytes 393224 | tf_op jit(solution)/shard_map/ppermute | solution.py:17
  546.9 301.6 %all-to-all-start = ((f32[16,64,296]{2,1,0:T(8,128)}), f32[16,64,296]{2,1,0:T(8,128)}, u32[]{:S(2)}, u32[]{:S(2)}) async-start(f32[16,64,296]{2,1,0:T(8,128)} %copy.260), calls=%async_computation | async-start | bytes 3145728 | tf_op jit(solution)/shard_map/all_to_all | solution.py:164
  552.3 281.4 %all-reduce.5.cloned.1.call-start = ((), (), s32[]{:S(2)}) async-start(), calls=%async_computation.6 | async-start | bytes 1179648 | tf_op jit(solution)/shard_map/psum | solution.py:240
  561.2 15.3 %collective-permute-start.11 = (bf16[64,16,160]{2,0,1:T(8,128)(2,1)S(1)}, bf16[64,16,160]{2,0,1:T(8,128)(2,1)S(1)}, u32[]{:S(2)}, u32[]{:S(2)}) collective-permute-start(bf16[64,16,160]{2,0,1:T(8,128)(2,1)S(1)} %get-tuple-element.58), channel_id=1, source_target_pairs={{0,1},{1,2},{2,3},{3,4},{4,5},{5,6},{6,7},{7,8},{8,9},{9,10},{10,1... | collective-permute-start | bytes 983048 | tf_op jit(solution)/shard_map/ppermute | solution.py:17
  564.8 18.9 %collective-permute-start.10 = (bf16[64,16,160]{2,0,1:T(8,128)(2,1)S(1)}, bf16[64,16,160]{2,0,1:T(8,128)(2,1)S(1)}, u32[]{:S(2)}, u32[]{:S(2)}) collective-permute-start(bf16[64,16,160]{2,0,1:T(8,128)(2,1)S(1)} %get-tuple-element.59), channel_id=1, source_target_pairs={{1,0},{2,1},{3,2},{4,3},{5,4},{6,5},{7,6},{8,7},{9,8},{10,9},{11,1... | collective-permute-start | bytes 983048 | tf_op jit(solution)/shard_map/ppermute | solution.py:20
  673.5 12.3 %copy-start.47 = (f32[9,64,64]{2,1,0:T(8,128)}, f32[9,64,64]{2,1,0:T(8,128)S(1)}, u32[]{:S(2)}) copy-start(f32[9,64,64]{2,1,0:T(8,128)S(1)} %fusion.34) | copy-start | bytes 442372
  679.5 13.4 %collective-permute-start.13 = (bf16[64,64,16]{1,2,0:T(8,128)(2,1)}, bf16[64,64,16]{1,2,0:T(8,128)(2,1)}, u32[]{:S(2)}, u32[]{:S(2)}) collective-permute-start(bf16[64,64,16]{1,2,0:T(8,128)(2,1)} %copy.292), channel_id=1, source_target_pairs={{16,0},{32,16},{48,32},{64,48},{80,64},{96,80},{112,96},{17,1},{33... | collective-permute-start | bytes 393224 | tf_op jit(solution)/shard_map/ppermute | solution.py:20
  680.8 8.8 collective-permute-start.12
  699.2 137.9 %collective-permute-start.15 = (bf16[64,16,160]{2,0,1:T(8,128)(2,1)}, bf16[64,16,160]{2,0,1:T(8,128)(2,1)}, u32[]{:S(2)}, u32[]{:S(2)}) collective-permute-start(bf16[64,16,160]{2,0,1:T(8,128)(2,1)} %get-tuple-element.54), channel_id=1, source_target_pairs={{0,1},{1,2},{2,3},{3,4},{4,5},{5,6},{6,7},{7,8},{8,9},{9,10},{10,1... | collective-permute-start | bytes 983048 | tf_op jit(solution)/shard_map/ppermute | solution.py:17
  703.8 133.3 %collective-permute-start.14 = (bf16[64,16,160]{2,0,1:T(8,128)(2,1)}, bf16[64,16,160]{2,0,1:T(8,128)(2,1)}, u32[]{:S(2)}, u32[]{:S(2)}) collective-permute-start(bf16[64,16,160]{2,0,1:T(8,128)(2,1)} %get-tuple-element.55), channel_id=1, source_target_pairs={{1,0},{2,1},{3,2},{4,3},{5,4},{6,5},{7,6},{8,7},{9,8},{10,9},{11,1... | collective-permute-start | bytes 983048 | tf_op jit(solution)/shard_map/ppermute | solution.py:20
  852.7 31.3 %all-to-all-start.1 = ((f32[1024,1,296]{2,1,0:T(1,128)}), f32[1024,1,296]{2,1,0:T(1,128)}, u32[]{:S(2)}, u32[]{:S(2)}) async-start(f32[1024,1,296]{2,1,0:T(1,128)} %copy.261), calls=%async_computation.1 | async-start | bytes 3145728 | tf_op jit(solution)/shard_map/all_to_all | solution.py:171
  887.0 27.1 %all-to-all-start.2 = ((f32[8,16,8,296]{3,2,0,1:T(8,128)}), f32[8,16,8,296]{3,2,0,1:T(8,128)}, u32[]{:S(2)}, u32[]{:S(2)}) async-start(f32[8,16,8,296]{3,2,0,1:T(8,128)} %copy.263), calls=%async_computation.2 | async-start | bytes 3145728 | tf_op jit(solution)/shard_map/all_to_all | solution.py:178
  926.2 11.2 %copy-start.37 = (f32[5,8,64,128]{3,2,1,0:T(8,128)S(1)}, f32[5,8,64,128]{3,2,1,0:T(8,128)}, u32[]{:S(2)}) copy-start(f32[5,8,64,128]{3,2,1,0:T(8,128)} %copy.361) | copy-start | bytes 3932164
  926.2 12.2 %copy-start.1 = (bf16[37,64]{1,0:T(8,128)(2,1)S(1)}, bf16[37,64]{1,0:T(8,128)(2,1)}, u32[]{:S(2)}) copy-start(bf16[37,64]{1,0:T(8,128)(2,1)} %param.9) | copy-start | bytes 14212
  (40 other events, 132.6 us)
Sparse Core Ops, SparseCore 0:
  686.0 147.6 all-reduce.4
where the time goes:
time: 954 us; the launch traced here: 946 us
  blocking collectives  393 us (41%)
  waiting for transfers between devices  191 us (20%)
  local copies, waits for them, and re-layouts  156 us (16%)
  starting transfers between devices  88.6 us (9%)
  other arithmetic  55 us (6%)
  matrix products  46.3 us (5%)
  between operations  15.3 us (2%)
    psum x2, blocking collectives, normalize(): totals = lax.psum(jnp.sum(activation, axis=(1, 2)), ('row', 'col'))  134 us
    psum x2, blocking collectives, norm_back(): lax.psum((jnp.sum(gradient, axis=(1, 2)), jnp.sum(gradient * normed, axis...  130 us
    psum x2, blocking collectives, normalize(): lax.psum(jnp.sum(centered * centered, axis=(1, 2)), ('row', 'col'))  129 us
    psum x1, waiting for transfers between devices, on_device(): lax.psum((first_term, second_term, head_term, bias_term), ('row', 'col'))  125 us
    unnamed x117, local copies, waits for them, and re-layouts  38.8 us
    ppermute x8, starting transfers between devices, with_halo(): lax.ppermute(lax.slice_in_dim(block, block.shape[dim] - width, None, axis...  31.6 us
    dot_general x36, matrix products, convolve(): jnp.dot(matrix, window, preferred_element_type=jnp.float32)  25.6 us
    convert_element_type x2, local copies, waits for them, and re-layouts, on_device(): cot_mirror.astype(jnp.float32)  23.2 us
  transfers between devices with their start and end apart: 23, of which 9 were waited for; matrix products, arithmetic and copies ran while one was open for 16% of the time, Pallas kernels for 0%

commit v1 on v0

--- a/solution.py
+++ b/solution.py
@@ -20,14 +20,6 @@
         high = lax.ppermute(lax.slice_in_dim(block, 0, width, axis=dim), axis, backward)
         block = jnp.concatenate([low, block, high], axis=dim)
     return block
-
-
-def as_sent(shard):
-
-    def short(part):
-        return part.astype(jnp.bfloat16) if part.dtype == jnp.float32 else part
-
-    return jax.tree.map(short, shard)
 
 
 def elu_apply(value_entries):
@@ -82,119 +74,81 @@
     return jnp.stack(collected, 0)
 
 
+def share(vector):
+    count = lax.axis_size("row") * lax.axis_size("col")
+    spread_out = jnp.broadcast_to(vector[None], (count,) + vector.shape)
+    return lax.all_to_all(spread_out, ("row", "col"), split_axis=0, concat_axis=0, tiled=True)
+
+
+def total(flat, chunk):
+    count = lax.axis_size("row") * lax.axis_size("col")
+    padded = jnp.pad(flat, (0, count * chunk - flat.shape[0])).reshape(count, chunk)
+    parts = lax.all_to_all(padded, ("row", "col"), split_axis=0, concat_axis=0, tiled=True)
+    return share(jnp.sum(parts, axis=0)).reshape(-1)
+
+
 def normalize(activation, cell_count):
-    totals = lax.psum(jnp.sum(activation, axis=(1, 2)), ("row", "col"))
-    average = totals / cell_count
-    centered = activation - average[:, None, None]
-    spread = lax.psum(jnp.sum(centered * centered, axis=(1, 2)), ("row", "col")) / cell_count
+    channels = activation.shape[0]
+    own_count = activation.shape[1] * activation.shape[2]
+    own_sum = jnp.sum(activation, axis=(1, 2))
+    own_mean = own_sum / own_count
+    off = activation - own_mean[:, None, None]
+    own_square = jnp.sum(off * off, axis=(1, 2))
+    table = share(jnp.concatenate([own_sum, own_square]))
+    sums = table[:, :channels]
+    average = jnp.sum(sums, axis=0) / cell_count
+    shift = sums / own_count - average[None]
+    spread = (
+        jnp.sum(table[:, channels:], axis=0) + own_count * jnp.sum(shift * shift, axis=0)
+    ) / cell_count
     inverse_std = lax.rsqrt(spread + epsilon)
-    return (centered * inverse_std[:, None, None], inverse_std)
+    return ((activation - average[:, None, None]) * inverse_std[:, None, None], inverse_std)
 
 
 def norm_back(gradient, normed, inverse_std, cell_count):
-    first_sum, second_sum = lax.psum(
-        (jnp.sum(gradient, axis=(1, 2)), jnp.sum(gradient * normed, axis=(1, 2))), ("row", "col")
-    )
-    first_mean = first_sum / cell_count
-    second_mean = second_sum / cell_count
+    channels = gradient.shape[0]
+    sums = jnp.sum(
+        share(
+            jnp.concatenate(
+                [jnp.sum(gradient, axis=(1, 2)), jnp.sum(gradient * normed, axis=(1, 2))]
+            )
+        ),
+        axis=0,
+    )
+    first_mean = sums[:channels] / cell_count
+    second_mean = sums[channels:] / cell_count
     return inverse_std[:, None, None] * (
         gradient - first_mean[:, None, None] - normed * second_mean[:, None, None]
     )
 
 
-def mirror_prepare(tensor, col_devices):
-    planes, col_count, row_count = tensor.shape
-    slab_rows = row_count // col_devices
-    shaped = tensor.reshape(planes, col_count, col_devices, slab_rows).transpose(2, 1, 0, 3)
-    return shaped.reshape(col_devices, col_count, planes * slab_rows)
-
-
-def mirror_middle(received):
-    return received.reshape(received.shape[1], 1, received.shape[2])
-
-
-def mirror_tail(received, col_devices, row_devices):
-    return received.reshape(received.shape[0], col_devices, row_devices, received.shape[2])
-
-
-def mirror_finish(received, planes, row_devices):
-    row_count = received.shape[0]
-    slab_rows = received.shape[3] // planes
-    shaped = received.reshape(row_count, row_devices, planes, slab_rows).transpose(2, 1, 3, 0)
-    return shaped.reshape(planes, row_devices * slab_rows, row_count)
-
-
-def mirror_half(tensors):
-    col_devices = lax.axis_size("col")
-    row_devices = lax.axis_size("row")
-    planes = tuple((member.shape[0] for member in tensors))
-    first = lax.all_to_all(
-        as_sent(tuple((mirror_prepare(member, col_devices) for member in tensors))),
-        "col",
-        split_axis=0,
-        concat_axis=1,
-        tiled=True,
-    )
-    second = lax.all_to_all(
-        as_sent(tuple((mirror_middle(member) for member in first))),
-        ("row", "col"),
-        split_axis=0,
-        concat_axis=1,
-        tiled=True,
-    )
-    third = lax.all_to_all(
-        as_sent(tuple((mirror_tail(member, col_devices, row_devices) for member in second))),
-        "col",
-        split_axis=1,
-        concat_axis=0,
-        tiled=True,
-    )
-    return tuple(
-        (
-            mirror_finish(member, count_planes, row_devices)
-            for member, count_planes in zip(third, planes)
-        )
-    )
-
-
-def mirror_full(tensors):
-    col_devices = lax.axis_size("col")
-    row_devices = lax.axis_size("row")
-    planes = tuple((member.shape[0] for member in tensors))
-    first = lax.all_to_all(
-        tuple((mirror_prepare(member, col_devices) for member in tensors)),
-        "col",
-        split_axis=0,
-        concat_axis=1,
-        tiled=True,
-    )
-    second = lax.all_to_all(
-        tuple((mirror_middle(member) for member in first)),
-        ("row", "col"),
-        split_axis=0,
-        concat_axis=1,
-        tiled=True,
-    )
-    third = lax.all_to_all(
-        tuple((mirror_tail(member, col_devices, row_devices) for member in second)),
-        "col",
-        split_axis=1,
-        concat_axis=0,
-        tiled=True,
-    )
-    return tuple(
-        (
-            mirror_finish(member, count_planes, row_devices)
-            for member, count_planes in zip(third, planes)
-        )
-    )
+def mirror(tensor):
+    rows = lax.axis_size("row")
+    cols = lax.axis_size("col")
+    ratio = cols // rows
+    turned = jnp.swapaxes(tensor, 1, 2)
+    planes, length, width = turned.shape
+    halves = turned.reshape(planes, ratio, length // ratio, width)
+    parity = lax.axis_index("col") % ratio
+    got = []
+    for step in range(ratio):
+        half = lax.dynamic_index_in_dim(halves, (parity + step) % ratio, 1, keepdims=False)
+        pairs = []
+        for row in range(rows):
+            for col in range(cols):
+                target = (col // ratio) * cols + ratio * row + (col + step) % ratio
+                pairs.append((row * cols + col, target))
+        got.append(lax.ppermute(half, ("row", "col"), pairs))
+    low = jnp.where(parity == 0, got[0], got[1])
+    high = jnp.where(parity == 0, got[1], got[0])
+    return jnp.concatenate([low, high], axis=2)
 
 
 def on_device(features, conv_first, conv_second, head_weight, head_bias, cotangent):
     channels, col_count, row_count = features.shape
     length = col_count * lax.axis_size("col")
     cell_count = float(length * length)
-    cot_mirror = mirror_half((cotangent,))[0]
+    cot_mirror = mirror(cotangent)
     wide_in = widen(features)
     act_first = convolve(wide_in, conv_first, col_count, row_count, False)
     normed_first, inverse_first = normalize(act_first, cell_count)
@@ -208,7 +162,7 @@
     raw_logits = (
         jnp.dot(head_weight, flat_hidden, preferred_element_type=jnp.float32) + head_bias[:, None]
     ).reshape(-1, col_count, row_count)
-    logit_mirror = mirror_full((raw_logits,))[0]
+    logit_mirror = mirror(raw_logits.astype(jnp.bfloat16)).astype(jnp.float32)
     logits = (0.5 * (raw_logits + logit_mirror)).astype(jnp.bfloat16)
     grad_sym = (0.5 * (cotangent.astype(jnp.float32) + cot_mirror.astype(jnp.float32))).astype(
         jnp.bfloat16
@@ -237,15 +191,18 @@
     input_grad = (
         convolve(widen_grad(grad_act_first), conv_first, col_count, row_count, True) + grad_summed
     ).astype(jnp.bfloat16)
-    reduced = lax.psum((first_term, second_term, head_term, bias_term), ("row", "col"))
     inverse_len = 1.0 / length
+    early = total(jnp.concatenate([second_term.reshape(-1), head_term.reshape(-1), bias_term]), 384)
+    late = total(first_term.reshape(-1), 384)
+    first_size = first_term.size
+    head_end = first_size + head_term.size
     return (
         logits,
         input_grad,
-        reduced[0] * inverse_len,
-        reduced[1] * inverse_len,
-        reduced[2] * inverse_len,
-        reduced[3] * inverse_len,
+        (late[:first_size] * inverse_len).reshape(first_term.shape),
+        (early[:first_size] * inverse_len).reshape(first_term.shape),
+        (early[first_size:head_end] * inverse_len).reshape(head_term.shape),
+        early[head_end : head_end + bias_term.size] * inverse_len,
     )
 
 

time: 954 us -> 468 us (0.49)
  blocking collectives: 393 us -> 0 us
  waiting for transfers between devices: 191 us -> 77.9 us
  starting transfers between devices: 88.6 us -> 164 us
  local copies, waits for them, and re-layouts: 156 us -> 110 us
  between operations: 15.3 us -> 2.26 us
    psum x6 -> x0, blocking collectives: 393 us -> none  [the longest x2 134 us: normalize(): totals = lax.psum(jnp.sum(activation, axis=(1, 2)), ('row', 'col'))]
    psum x1 -> x0, waiting for transfers between devices: 125 us -> none  [on_device(): lax.psum((first_term, second_term, head_term, bias_term), ('row', 'col'))]
    all_to_all x6 -> x8, starting transfers between devices: 41.6 us -> 104 us  [the longest x6 86.6 us: share(): lax.all_to_all(spread_out, ('row', 'col'), split_axis=0, concat_axis=0, t...]
    convert_element_type x2 -> x0, local copies, waits for them, and re-layouts: 23.2 us -> none  [on_device(): cot_mirror.astype(jnp.float32)]
    reshape x8 -> x5, local copies, waits for them, and re-layouts: 24 us -> 6.38 us  [the longest x2 4.19 us: mirror(): halves = turned.reshape(planes, ratio, length // ratio, width)]
    transpose x2 -> x1, local copies, waits for them, and re-layouts: 16.3 us -> 0.92 us  [mirror(): turned = jnp.swapaxes(tensor, 1, 2)]
    ppermute x0 -> x4, starting transfers between devices: none -> 15.1 us  [mirror(): got.append(lax.ppermute(half, ('row', 'col'), pairs))]
    dynamic_slice x0 -> x4, local copies, waits for them, and re-layouts: none -> 14.4 us  [mirror(): lax.dynamic_index_in_dim(halves, (parity + step) % ratio, 1, keepdims=False)]
  transfers between devices with their start and end apart: 23 -> 28, of which waited for: 9 -> 13; matrix products, arithmetic and copies ran while one was open for 16% -> 26% of each run, Pallas kernels for 0% -> 0%
where the time goes in v1:
time: 468 us; the launch traced here: 460 us
  starting transfers between devices  164 us (35%)
  local copies, waits for them, and re-layouts  110 us (24%)
  waiting for transfers between devices  77.9 us (17%)
  other arithmetic  57.1 us (12%)
  matrix products  49.3 us (11%)
    all_to_all x6, starting transfers between devices, share(): lax.all_to_all(spread_out, ('row', 'col'), split_axis=0, concat_axis=0, t...  86.6 us
    unnamed x126, local copies, waits for them, and re-layouts  30.1 us
    ppermute x8, starting transfers between devices, with_halo(): lax.ppermute(lax.slice_in_dim(block, block.shape[dim] - width, None, axis...  29.6 us
    ppermute x8, waiting for transfers between devices, with_halo(): lax.ppermute(lax.slice_in_dim(block, 0, width, axis=dim), axis, backward)  27.8 us
    all_to_all x6, waiting for transfers between devices, share(): lax.all_to_all(spread_out, ('row', 'col'), split_axis=0, concat_axis=0, t...  26 us
    concatenate x7, other arithmetic, with_halo(): block = jnp.concatenate([low, block, high], axis=dim)  23.8 us
    dot_general x18, matrix products, weight_terms(): lax.dot_general(flattened, window, (((1,), (1,)), ((), ())), preferred_el...  23.2 us
    dot_general x36, matrix products, convolve(): jnp.dot(matrix, window, preferred_element_type=jnp.float32)  20.9 us
  transfers between devices with their start and end apart: 28, of which 13 were waited for; matrix products, arithmetic and copies ran while one was open for 26% of the time, Pallas kernels for 0%

profile of v1, /device:TPU:1, one launch (start us, length us, event | category | flops | bytes accessed | tf_op | source)
XLA Modules:
  0.0 460.3 jit_solution(7951999483261087411)
XLA Ops:
  3.1 4.1 collective-permute-start
  13.8 3.5 collective-permute-done.1
  20.5 4.9 %collective-permute-start.2 = (bf16[64,16,160]{2,0,1:T(8,128)(2,1)S(1)}, bf16[64,16,160]{2,0,1:T(8,128)(2,1)S(1)}, u32[]{:S(2)}, u32[]{:S(2)}) collective-permute-start(bf16[64,16,160]{2,0,1:T(8,128)(2,1)S(1)} %get-tuple-element.68), channel_id=1, source_target_pairs={{0,1},{1,2},{2,3},{3,4},{4,5},{5,6},{6,7},{7,8},{8,9},{9,10},{10,1... | collective-permute-start | bytes 983048 | tf_op jit(solution)/shard_map/ppermute | solution.py:17
  31.5 7.6 %collective-permute-done.3 = bf16[64,16,160]{2,0,1:T(8,128)(2,1)S(1)} collective-permute-done((bf16[64,16,160]{2,0,1:T(8,128)(2,1)S(1)}, bf16[64,16,160]{2,0,1:T(8,128)(2,1)S(1)}, u32[]{:S(2)}, u32[]{:S(2)}) %collective-permute-start.3) | collective-permute-done | bytes 327712 | tf_op jit(solution)/shard_map/ppermute | solution.py:20
  51.1 12.6 %all-to-all-start = ((f32[128,1,128]{2,1,0:T(1,128)}), f32[128,1,128]{2,1,0:T(1,128)S(1)}, u32[]{:S(2)}, u32[]{:S(2)}) async-start(f32[128,1,128]{2,1,0:T(1,128)} %broadcast_in_dim.14), calls=%async_computation | async-start | bytes 131072 | tf_op jit(solution)/shard_map/all_to_all | solution.py:80
  63.8 4.2 constant_dynamic-slice_fusion.1
  68.0 3.6 copy.386
  71.6 6.4 %collective-permute-start.10 = (bf16[37,64,64]{2,1,0:T(8,128)(2,1)}, bf16[37,64,64]{2,1,0:T(8,128)(2,1)}, u32[]{:S(2)}, u32[]{:S(2)}) collective-permute-start(bf16[37,64,64]{2,1,0:T(8,128)(2,1)} %bitcast.509), channel_id=1, source_target_pairs={{0,0},{1,1},{2,16},{3,17},{4,32},{5,33},{6,48},{7,49},{8,64},{9,65... | collective-permute-start | bytes 909320 | tf_op jit(solution)/shard_map/ppermute | solution.py:141
  98.1 12.7 %collective-permute-done.5 = bf16[64,64,16]{1,2,0:T(8,128)(2,1)} collective-permute-done((bf16[64,64,16]{1,2,0:T(8,128)(2,1)}, bf16[64,64,16]{1,2,0:T(8,128)(2,1)}, u32[]{:S(2)}, u32[]{:S(2)}) %collective-permute-start.5) | collective-permute-done | bytes 131104 | tf_op jit(solution)/shard_map/ppermute | solution.py:20
  116.1 6.6 %collective-permute-start.6 = (bf16[64,16,160]{2,0,1:T(8,128)(2,1)S(1)}, bf16[64,16,160]{2,0,1:T(8,128)(2,1)S(1)}, u32[]{:S(2)}, u32[]{:S(2)}) collective-permute-start(bf16[64,16,160]{2,0,1:T(8,128)(2,1)S(1)} %get-tuple-element.65), channel_id=1, source_target_pairs={{0,1},{1,2},{2,3},{3,4},{4,5},{5,6},{6,7},{7,8},{8,9},{9,10},{10,1... | collective-permute-start | bytes 983048 | tf_op jit(solution)/shard_map/ppermute | solution.py:17
  129.1 13.7 %collective-permute-done.6 = bf16[64,16,160]{2,0,1:T(8,128)(2,1)S(1)} collective-permute-done((bf16[64,16,160]{2,0,1:T(8,128)(2,1)S(1)}, bf16[64,16,160]{2,0,1:T(8,128)(2,1)S(1)}, u32[]{:S(2)}, u32[]{:S(2)}) %collective-permute-start.6) | collective-permute-done | bytes 327712 | tf_op jit(solution)/shard_map/ppermute | solution.py:17
  156.2 32.4 %all-to-all-start.1 = ((f32[128,1,128]{2,1,0:T(1,128)}), f32[128,1,128]{2,1,0:T(1,128)S(1)}, u32[]{:S(2)}, u32[]{:S(2)}) async-start(f32[128,1,128]{2,1,0:T(1,128)} %broadcast_in_dim.15), calls=%async_computation.1 | async-start | bytes 131072 | tf_op jit(solution)/shard_map/all_to_all | solution.py:80
  191.5 6.7 %all-to-all-done.1 = f32[128,1,128]{2,1,0:T(1,128)S(1)} async-done(((f32[128,1,128]{2,1,0:T(1,128)}), f32[128,1,128]{2,1,0:T(1,128)S(1)}, u32[]{:S(2)}, u32[]{:S(2)}) %all-to-all-start.1) | async-done | bytes 65568 | tf_op jit(solution)/shard_map/all_to_all | solution.py:80
  198.3 5.5 %fusion.227 = (f32[64]{0:T(128)S(1)}, f32[64]{0:T(128)S(1)}, f32[64,64,128]{2,0,1:T(8,128)}, bf16[64,64,128]{2,0,1:T(8,128)(2,1)}) fusion(f32[64]{0:T(128)S(1)} %add_rsqrt_fusion, f32[64]{0:T(128)S(1)} %broadcast_multiply_fusion, bf16[64,64,128]{2,1,0:T(8,128)(2,1)S(1)} %copy-done.17, f32[8,64,8,128]{3,2,1,0:T(8,128)} %convolution_bitcast_fusion.4, ...), kind=kLoop, calls=%fused_computation.386 | loop fusion | flops 7339904 | bytes 8389632 | tf_op jit(solution)/shard_map/reduce_sum | solution.py:113
  204.5 4.4 all-to-all-start.2
  216.1 4.2 constant_dynamic-slice_fusion.3
  220.4 3.6 copy.339
  224.0 6.4 %collective-permute-start.8 = (bf16[37,64,64]{2,1,0:T(8,128)(2,1)}, bf16[37,64,64]{2,1,0:T(8,128)(2,1)}, u32[]{:S(2)}, u32[]{:S(2)}) collective-permute-start(bf16[37,64,64]{2,1,0:T(8,128)(2,1)} %bitcast.507), channel_id=1, source_target_pairs={{0,0},{1,1},{2,16},{3,17},{4,32},{5,33},{6,48},{7,49},{8,64},{9,65... | collective-permute-start | bytes 909320 | tf_op jit(solution)/shard_map/ppermute | solution.py:141
  262.7 12.6 %all-to-all-start.6 = ((f32[128,1,384]{2,1,0:T(1,128)}), f32[128,1,384]{2,1,0:T(1,128)S(1)}, u32[]{:S(2)}, u32[]{:S(2)}) async-start(f32[128,1,384]{2,1,0:T(1,128)} %bitcast.76), calls=%async_computation.6 | async-start | bytes 393216 | tf_op jit(solution)/shard_map/all_to_all | solution.py:86
  293.2 7.8 %all-to-all-done.6 = f32[128,1,384]{2,1,0:T(1,128)S(1)} async-done(((f32[128,1,384]{2,1,0:T(1,128)}), f32[128,1,384]{2,1,0:T(1,128)S(1)}, u32[]{:S(2)}, u32[]{:S(2)}) %all-to-all-start.6) | async-done | bytes 196640 | tf_op jit(solution)/shard_map/all_to_all | solution.py:86
  301.9 20.8 %all-to-all-start.7 = ((f32[128,1,384]{2,1,0:T(1,128)}), f32[128,1,384]{2,1,0:T(1,128)S(1)}, u32[]{:S(2)}, u32[]{:S(2)}) async-start(f32[128,1,384]{2,1,0:T(1,128)} %broadcast_in_dim.20), calls=%async_computation.7 | async-start | bytes 393216 | tf_op jit(solution)/shard_map/all_to_all | solution.py:80
  325.6 7.6 %all-to-all-done.7 = f32[128,1,384]{2,1,0:T(1,128)S(1)} async-done(((f32[128,1,384]{2,1,0:T(1,128)}), f32[128,1,384]{2,1,0:T(1,128)S(1)}, u32[]{:S(2)}, u32[]{:S(2)}) %all-to-all-start.7) | async-done | bytes 196640 | tf_op jit(solution)/shard_map/all_to_all | solution.py:80
  334.6 4.9 %maximum_maximum_fusion.2 = (bf16[64,80,160]{2,0,1:T(8,128)(2,1)S(1)}, bf16[64,80,160]{2,0,1:T(8,128)(2,1)S(1)}) fusion(bf16[64,64,16]{2,0,1:T(8,128)(2,1)} %copy.348, bf16[64,64,128]{2,0,1:T(8,128)(2,1)S(1)} %multiply_convert_fusion.1, bf16[64,64,16]{2,0,1:T(8,128)(2,1)} %copy.347, bf16[64,16,160]{2,0,1:T(8,128)(2,1)} %collective-permute-done.15, ...), kind=kLoop, calls=%fused_computation.49 | loop fusion | flops 13107200 | bytes 5242880 | tf_op jit(solution)/shard_map/concatenate | solution.py:21
  349.7 4.5 all-to-all-start.3
  355.6 8.2 %all-to-all-done.3 = f32[128,1,128]{2,1,0:T(1,128)S(1)} async-done(((f32[128,1,128]{2,1,0:T(1,128)}), f32[128,1,128]{2,1,0:T(1,128)S(1)}, u32[]{:S(2)}, u32[]{:S(2)}) %all-to-all-start.3) | async-done | bytes 65568 | tf_op jit(solution)/shard_map/all_to_all | solution.py:80
  381.6 4.4 all-to-all-start.4
  389.0 4.0 collective-permute-start.16
  401.2 4.0 collective-permute-done.17
  419.0 11.9 %all-to-all-start.5 = ((f32[128,1,384]{2,1,0:T(1,128)}), f32[128,1,384]{2,1,0:T(1,128)S(1)}, u32[]{:S(2)}, u32[]{:S(2)}) async-start(f32[128,1,384]{2,1,0:T(1,128)} %broadcast_in_dim.19), calls=%async_computation.5 | async-start | bytes 393216 | tf_op jit(solution)/shard_map/all_to_all | solution.py:80
  433.7 4.0 fusion.114
  437.7 3.6 all-to-all-done.5
  442.6 4.8 %maximum_maximum_fusion.3 = (bf16[64,80,160]{2,0,1:T(8,128)(2,1)S(1)}, bf16[64,80,160]{2,0,1:T(8,128)(2,1)S(1)}) fusion(bf16[64,64,16]{2,0,1:T(8,128)(2,1)} %copy.365, bf16[64,64,128]{2,0,1:T(8,128)(2,1)S(1)} %fusion.10, bf16[64,64,16]{2,0,1:T(8,128)(2,1)} %copy.364, bf16[64,16,160]{2,0,1:T(8,128)(2,1)} %collective-permute-done.19, ...), kind=kLoop, calls=%fused_computation.51 | loop fusion | flops 13107200 | bytes 5242880 | tf_op jit(solution)/shard_map/concatenate | solution.py:21
  (295 shorter events, 211.9 us)
Async XLA Ops:
  0.6 188.0 %copy-start = (bf16[37,64]{1,0:T(8,128)(2,1)S(1)}, bf16[37,64]{1,0:T(8,128)(2,1)}, u32[]{:S(2)}) copy-start(bf16[37,64]{1,0:T(8,128)(2,1)} %param.9) | copy-start | bytes 14212
  3.1 9.0 %collective-permute-start = (bf16[64,64,16]{1,2,0:T(8,128)(2,1)S(1)}, bf16[64,64,16]{1,2,0:T(8,128)(2,1)S(1)}, u32[]{:S(2)}, u32[]{:S(2)}) collective-permute-start(bf16[64,64,16]{1,2,0:T(8,128)(2,1)S(1)} %copy.384), channel_id=1, source_target_pairs={{0,16},{16,32},{32,48},{48,64},{64,80},{80,96},{96,112},{1,17},{17... | collective-permute-start | bytes 393224 | tf_op jit(solution)/shard_map/ppermute | solution.py:17
  8.2 9.1 %collective-permute-start.1 = (bf16[64,64,16]{1,2,0:T(8,128)(2,1)}, bf16[64,64,16]{1,2,0:T(8,128)(2,1)}, u32[]{:S(2)}, u32[]{:S(2)}) collective-permute-start(bf16[64,64,16]{1,2,0:T(8,128)(2,1)} %copy.385), channel_id=1, source_target_pairs={{16,0},{32,16},{48,32},{64,48},{80,64},{96,80},{112,96},{17,1},{33... | collective-permute-start | bytes 393224 | tf_op jit(solution)/shard_map/ppermute | solution.py:20
  20.5 11.0 %collective-permute-start.2 = (bf16[64,16,160]{2,0,1:T(8,128)(2,1)S(1)}, bf16[64,16,160]{2,0,1:T(8,128)(2,1)S(1)}, u32[]{:S(2)}, u32[]{:S(2)}) collective-permute-start(bf16[64,16,160]{2,0,1:T(8,128)(2,1)S(1)} %get-tuple-element.68), channel_id=1, source_target_pairs={{0,1},{1,2},{2,3},{3,4},{4,5},{5,6},{6,7},{7,8},{8,9},{9,10},{10,1... | collective-permute-start | bytes 983048 | tf_op jit(solution)/shard_map/ppermute | solution.py:17
  25.5 13.7 %collective-permute-start.3 = (bf16[64,16,160]{2,0,1:T(8,128)(2,1)S(1)}, bf16[64,16,160]{2,0,1:T(8,128)(2,1)S(1)}, u32[]{:S(2)}, u32[]{:S(2)}) collective-permute-start(bf16[64,16,160]{2,0,1:T(8,128)(2,1)S(1)} %get-tuple-element.69), channel_id=1, source_target_pairs={{1,0},{2,1},{3,2},{4,3},{5,4},{6,5},{7,6},{8,7},{9,8},{10,9},{11,1... | collective-permute-start | bytes 983048 | tf_op jit(solution)/shard_map/ppermute | solution.py:20
  51.1 30.1 %all-to-all-start = ((f32[128,1,128]{2,1,0:T(1,128)}), f32[128,1,128]{2,1,0:T(1,128)S(1)}, u32[]{:S(2)}, u32[]{:S(2)}) async-start(f32[128,1,128]{2,1,0:T(1,128)} %broadcast_in_dim.14), calls=%async_computation | async-start | bytes 131072 | tf_op jit(solution)/shard_map/all_to_all | solution.py:80
  71.6 20.7 %collective-permute-start.10 = (bf16[37,64,64]{2,1,0:T(8,128)(2,1)}, bf16[37,64,64]{2,1,0:T(8,128)(2,1)}, u32[]{:S(2)}, u32[]{:S(2)}) collective-permute-start(bf16[37,64,64]{2,1,0:T(8,128)(2,1)} %bitcast.509), channel_id=1, source_target_pairs={{0,0},{1,1},{2,16},{3,17},{4,32},{5,33},{6,48},{7,49},{8,64},{9,65... | collective-permute-start | bytes 909320 | tf_op jit(solution)/shard_map/ppermute | solution.py:141
  80.3 12.1 %collective-permute-start.11 = (bf16[37,64,64]{2,1,0:T(8,128)(2,1)}, bf16[37,64,64]{2,1,0:T(8,128)(2,1)}, u32[]{:S(2)}, u32[]{:S(2)}) collective-permute-start(bf16[37,64,64]{2,1,0:T(8,128)(2,1)} %bitcast.510), channel_id=1, source_target_pairs={{0,1},{1,0},{2,17},{3,16},{4,33},{5,32},{6,49},{7,48},{8,65},{9,64... | collective-permute-start | bytes 909320 | tf_op jit(solution)/shard_map/ppermute | solution.py:141
  81.4 69.4 %copy-start.50 = (f32[64]{0:T(128)}, f32[64]{0:T(128)S(1)}, u32[]{:S(2)}) copy-start(f32[64]{0:T(128)S(1)} %add_rsqrt_fusion.1) | copy-start | bytes 772
  82.1 60.6 %copy-start.2 = (bf16[64,64,128]{2,0,1:T(8,128)(2,1)}, bf16[64,64,128]{2,0,1:T(8,128)(2,1)S(1)}, u32[]{:S(2)}) copy-start(bf16[64,64,128]{2,0,1:T(8,128)(2,1)S(1)} %fusion.5) | copy-start | bytes 3145732
  86.1 8.6 %collective-permute-start.4 = (bf16[64,64,16]{1,2,0:T(8,128)(2,1)S(1)}, bf16[64,64,16]{1,2,0:T(8,128)(2,1)}, u32[]{:S(2)}, u32[]{:S(2)}) collective-permute-start(bf16[64,64,16]{1,2,0:T(8,128)(2,1)S(1)} %copy.322), channel_id=1, source_target_pairs={{0,16},{16,32},{32,48},{48,64},{64,80},{80,96},{96,112},{1,17},{17... | collective-permute-start | bytes 393224 | tf_op jit(solution)/shard_map/ppermute | solution.py:17
  91.1 19.8 %collective-permute-start.5 = (bf16[64,64,16]{1,2,0:T(8,128)(2,1)}, bf16[64,64,16]{1,2,0:T(8,128)(2,1)}, u32[]{:S(2)}, u32[]{:S(2)}) collective-permute-start(bf16[64,64,16]{1,2,0:T(8,128)(2,1)} %copy.323), channel_id=1, source_target_pairs={{16,0},{32,16},{48,32},{64,48},{80,64},{96,80},{112,96},{17,1},{33... | collective-permute-start | bytes 393224 | tf_op jit(solution)/shard_map/ppermute | solution.py:20
  116.1 26.6 %collective-permute-start.6 = (bf16[64,16,160]{2,0,1:T(8,128)(2,1)S(1)}, bf16[64,16,160]{2,0,1:T(8,128)(2,1)S(1)}, u32[]{:S(2)}, u32[]{:S(2)}) collective-permute-start(bf16[64,16,160]{2,0,1:T(8,128)(2,1)S(1)} %get-tuple-element.65), channel_id=1, source_target_pairs={{0,1},{1,2},{2,3},{3,4},{4,5},{5,6},{6,7},{7,8},{8,9},{9,10},{10,1... | collective-permute-start | bytes 983048 | tf_op jit(solution)/shard_map/ppermute | solution.py:17
  122.8 19.9 %collective-permute-start.7 = (bf16[64,16,160]{2,0,1:T(8,128)(2,1)S(1)}, bf16[64,16,160]{2,0,1:T(8,128)(2,1)S(1)}, u32[]{:S(2)}, u32[]{:S(2)}) collective-permute-start(bf16[64,16,160]{2,0,1:T(8,128)(2,1)S(1)} %get-tuple-element.64), channel_id=1, source_target_pairs={{1,0},{2,1},{3,2},{4,3},{5,4},{6,5},{7,6},{8,7},{9,8},{10,9},{11,1... | collective-permute-start | bytes 983048 | tf_op jit(solution)/shard_map/ppermute | solution.py:20
  155.4 42.9 %copy-start.17 = (bf16[64,64,128]{2,1,0:T(8,128)(2,1)S(1)}, bf16[64,64,128]{2,1,0:T(8,128)(2,1)}, u32[]{:S(2)}) copy-start(bf16[64,64,128]{2,1,0:T(8,128)(2,1)} %param.6) | copy-start | bytes 3145732
  156.2 42.0 %all-to-all-start.1 = ((f32[128,1,128]{2,1,0:T(1,128)}), f32[128,1,128]{2,1,0:T(1,128)S(1)}, u32[]{:S(2)}, u32[]{:S(2)}) async-start(f32[128,1,128]{2,1,0:T(1,128)} %broadcast_in_dim.15), calls=%async_computation.1 | async-start | bytes 131072 | tf_op jit(solution)/shard_map/all_to_all | solution.py:80
  204.5 29.6 %all-to-all-start.2 = ((f32[128,1,128]{2,1,0:T(1,128)}), f32[128,1,128]{2,1,0:T(1,128)S(1)}, u32[]{:S(2)}, u32[]{:S(2)}) async-start(f32[128,1,128]{2,1,0:T(1,128)} %broadcast_in_dim.16), calls=%async_computation.2 | async-start | bytes 131072 | tf_op jit(solution)/shard_map/all_to_all | solution.py:80
  224.0 98.7 %collective-permute-start.8 = (bf16[37,64,64]{2,1,0:T(8,128)(2,1)}, bf16[37,64,64]{2,1,0:T(8,128)(2,1)}, u32[]{:S(2)}, u32[]{:S(2)}) collective-permute-start(bf16[37,64,64]{2,1,0:T(8,128)(2,1)} %bitcast.507), channel_id=1, source_target_pairs={{0,0},{1,1},{2,16},{3,17},{4,32},{5,33},{6,48},{7,49},{8,64},{9,65... | collective-permute-start | bytes 909320 | tf_op jit(solution)/shard_map/ppermute | solution.py:141
  232.7 90.0 %collective-permute-start.9 = (bf16[37,64,64]{2,1,0:T(8,128)(2,1)}, bf16[37,64,64]{2,1,0:T(8,128)(2,1)}, u32[]{:S(2)}, u32[]{:S(2)}) collective-permute-start(bf16[37,64,64]{2,1,0:T(8,128)(2,1)} %bitcast.508), channel_id=1, source_target_pairs={{0,1},{1,0},{2,17},{3,16},{4,33},{5,32},{6,49},{7,48},{8,65},{9,64... | collective-permute-start | bytes 909320 | tf_op jit(solution)/shard_map/ppermute | solution.py:141
  251.9 23.4 %collective-permute-start.12 = (bf16[64,64,16]{1,2,0:T(8,128)(2,1)}, bf16[64,64,16]{1,2,0:T(8,128)(2,1)}, u32[]{:S(2)}, u32[]{:S(2)}) collective-permute-start(bf16[64,64,16]{1,2,0:T(8,128)(2,1)} %copy.345), channel_id=1, source_target_pairs={{0,16},{16,32},{32,48},{48,64},{64,80},{80,96},{96,112},{1,17},{17... | collective-permute-start | bytes 393224 | tf_op jit(solution)/shard_map/ppermute | solution.py:17
  256.8 21.8 %collective-permute-start.13 = (bf16[64,64,16]{1,2,0:T(8,128)(2,1)}, bf16[64,64,16]{1,2,0:T(8,128)(2,1)}, u32[]{:S(2)}, u32[]{:S(2)}) collective-permute-start(bf16[64,64,16]{1,2,0:T(8,128)(2,1)} %copy.346), channel_id=1, source_target_pairs={{16,0},{32,16},{48,32},{64,48},{80,64},{96,80},{112,96},{17,1},{33... | collective-permute-start | bytes 393224 | tf_op jit(solution)/shard_map/ppermute | solution.py:20
  262.7 38.2 %all-to-all-start.6 = ((f32[128,1,384]{2,1,0:T(1,128)}), f32[128,1,384]{2,1,0:T(1,128)S(1)}, u32[]{:S(2)}, u32[]{:S(2)}) async-start(f32[128,1,384]{2,1,0:T(1,128)} %bitcast.76), calls=%async_computation.6 | async-start | bytes 393216 | tf_op jit(solution)/shard_map/all_to_all | solution.py:86
  284.9 49.6 %collective-permute-start.14 = (bf16[64,16,160]{2,0,1:T(8,128)(2,1)}, bf16[64,16,160]{2,0,1:T(8,128)(2,1)}, u32[]{:S(2)}, u32[]{:S(2)}) collective-permute-start(bf16[64,16,160]{2,0,1:T(8,128)(2,1)} %get-tuple-element.61), channel_id=1, source_target_pairs={{1,0},{2,1},{3,2},{4,3},{5,4},{6,5},{7,6},{8,7},{9,8},{10,9},{11,1... | collective-permute-start | bytes 983048 | tf_op jit(solution)/shard_map/ppermute | solution.py:20
  287.9 46.6 %collective-permute-start.15 = (bf16[64,16,160]{2,0,1:T(8,128)(2,1)}, bf16[64,16,160]{2,0,1:T(8,128)(2,1)}, u32[]{:S(2)}, u32[]{:S(2)}) collective-permute-start(bf16[64,16,160]{2,0,1:T(8,128)(2,1)} %get-tuple-element.60), channel_id=1, source_target_pairs={{0,1},{1,2},{2,3},{3,4},{4,5},{5,6},{6,7},{7,8},{8,9},{9,10},{10,1... | collective-permute-start | bytes 983048 | tf_op jit(solution)/shard_map/ppermute | solution.py:17
  301.9 31.3 %all-to-all-start.7 = ((f32[128,1,384]{2,1,0:T(1,128)}), f32[128,1,384]{2,1,0:T(1,128)S(1)}, u32[]{:S(2)}, u32[]{:S(2)}) async-start(f32[128,1,384]{2,1,0:T(1,128)} %broadcast_in_dim.20), calls=%async_computation.7 | async-start | bytes 393216 | tf_op jit(solution)/shard_map/all_to_all | solution.py:80
  349.7 14.1 %all-to-all-start.3 = ((f32[128,1,128]{2,1,0:T(1,128)}), f32[128,1,128]{2,1,0:T(1,128)S(1)}, u32[]{:S(2)}, u32[]{:S(2)}) async-start(f32[128,1,128]{2,1,0:T(1,128)} %broadcast_in_dim.17), calls=%async_computation.3 | async-start | bytes 131072 | tf_op jit(solution)/shard_map/all_to_all | solution.py:80
  381.6 36.4 %all-to-all-start.4 = ((f32[128,1,384]{2,1,0:T(1,128)}), f32[128,1,384]{2,1,0:T(1,128)S(1)}, u32[]{:S(2)}, u32[]{:S(2)}) async-start(f32[128,1,384]{2,1,0:T(1,128)} %bitcast.506), calls=%async_computation.4 | async-start | bytes 393216 | tf_op jit(solution)/shard_map/all_to_all | solution.py:86
  389.0 8.8 %collective-permute-start.16 = (bf16[64,64,16]{1,2,0:T(8,128)(2,1)}, bf16[64,64,16]{1,2,0:T(8,128)(2,1)}, u32[]{:S(2)}, u32[]{:S(2)}) collective-permute-start(bf16[64,64,16]{1,2,0:T(8,128)(2,1)} %copy.362), channel_id=1, source_target_pairs={{0,16},{16,32},{32,48},{48,64},{64,80},{80,96},{96,112},{1,17},{17... | collective-permute-start | bytes 393224 | tf_op jit(solution)/shard_map/ppermute | solution.py:17
  395.8 9.4 %collective-permute-start.17 = (bf16[64,64,16]{1,2,0:T(8,128)(2,1)}, bf16[64,64,16]{1,2,0:T(8,128)(2,1)}, u32[]{:S(2)}, u32[]{:S(2)}) collective-permute-start(bf16[64,64,16]{1,2,0:T(8,128)(2,1)} %copy.363), channel_id=1, source_target_pairs={{16,0},{32,16},{48,32},{64,48},{80,64},{96,80},{112,96},{17,1},{33... | collective-permute-start | bytes 393224 | tf_op jit(solution)/shard_map/ppermute | solution.py:20
  411.4 31.3 %collective-permute-start.18 = (bf16[64,16,160]{2,0,1:T(8,128)(2,1)}, bf16[64,16,160]{2,0,1:T(8,128)(2,1)}, u32[]{:S(2)}, u32[]{:S(2)}) collective-permute-start(bf16[64,16,160]{2,0,1:T(8,128)(2,1)} %get-tuple-element.57), channel_id=1, source_target_pairs={{1,0},{2,1},{3,2},{4,3},{5,4},{6,5},{7,6},{8,7},{9,8},{10,9},{11,1... | collective-permute-start | bytes 983048 | tf_op jit(solution)/shard_map/ppermute | solution.py:20
  414.8 27.8 %collective-permute-start.19 = (bf16[64,16,160]{2,0,1:T(8,128)(2,1)}, bf16[64,16,160]{2,0,1:T(8,128)(2,1)}, u32[]{:S(2)}, u32[]{:S(2)}) collective-permute-start(bf16[64,16,160]{2,0,1:T(8,128)(2,1)} %get-tuple-element.56), channel_id=1, source_target_pairs={{0,1},{1,2},{2,3},{3,4},{4,5},{5,6},{6,7},{7,8},{8,9},{9,10},{10,1... | collective-permute-start | bytes 983048 | tf_op jit(solution)/shard_map/ppermute | solution.py:17
  419.0 22.4 %all-to-all-start.5 = ((f32[128,1,384]{2,1,0:T(1,128)}), f32[128,1,384]{2,1,0:T(1,128)S(1)}, u32[]{:S(2)}, u32[]{:S(2)}) async-start(f32[128,1,384]{2,1,0:T(1,128)} %broadcast_in_dim.19), calls=%async_computation.5 | async-start | bytes 393216 | tf_op jit(solution)/shard_map/all_to_all | solution.py:80
  (51 other events, 255.1 us)

commit v2 on v1

v2 whole, which is shorter than its diff:
```python
import jax
import jax.numpy as jnp
from jax import lax
from jax.experimental import pallas as pl
from jax.experimental.pallas import tpu as pltpu
from jax.sharding import PartitionSpec as P


STEP = 16
GRID = 64
epsilon = 1e-05
F32 = jnp.float32
BF16 = jnp.bfloat16
ROWS = 8
COLS = 16
DEVICES = 128
CH = 64
BINS = 37
CELLS = float(1024 * 1024)
OWN = float(64 * 128)
WIDE = 24


def class_table():
    place = {}
    count = 0
    for a in range(STEP):
        for b in range(a + 1, STEP):
            place[(a, b)] = (count, 0)
            place[(b, a)] = (count, 1)
            count += 1
    for a in range(STEP // 2):
        place[(a, a)] = (count, 0)
        place[(a + 8, a + 8)] = (count, 1)
        count += 1
    return place, STEP * (STEP - 1) // 2


PLACE, FIRST_DIAGONAL = class_table()


def dot(lhs, rhs):
    return jnp.dot(lhs, rhs, preferred_element_type=F32)


def dot_nt(lhs, rhs):
    return lax.dot_general(lhs, rhs, (((1,), (1,)), ((), ())), preferred_element_type=F32)


def iota(shape, dim):
    return lax.broadcasted_iota(jnp.int32, shape, dim)


def eye(n):
    return jnp.where(iota((n, n), 0) == iota((n, n), 1), 1.0, 0.0).astype(BF16)


def class_order():
    row = iota((128, 128), 0)
    lane = iota((128, 128), 1)
    return jnp.where(lane == STEP * (row % 8) + row // 8, 1.0, 0.0).astype(BF16)


def elu(z):
    return jnp.where(z > 0, z, jnp.exp(jnp.minimum(z, 0.0)) - 1.0)


def slope(z):
    return jnp.where(z > 0, 1.0, jnp.exp(jnp.minimum(z, 0.0)))


def pack_kernel(x_ref, o_ref):
    order = class_order()
    for a in range(STEP):
        parts = []
        for h in range(2):
            x = x_ref[:, :, :] if False else jnp.concatenate(
                [x_ref[32 * h + a], x_ref[32 * h + 16 + a]], axis=0
            )
            parts.append(dot_nt(order, x))
        for b in range(STEP):
            dest, slot = PLACE[(a, b)]
            tile = jnp.concatenate([p[8 * b : 8 * b + 8] for p in parts], axis=0)
            o_ref[dest, 16 * slot : 16 * slot + 16, :] = tile.astype(BF16)


def unpack_kernel(r_ref, o_ref):
    back = class_order()
    for a in range(STEP):
        rows = [[], []]
        for b in range(STEP):
            src, slot = PLACE[(a, b)]
            tile = r_ref[src, 16 * slot : 16 * slot + 16, :].astype(F32)
            rows[0].append(tile[:8])
            rows[1].append(tile[8:])
        for h in range(2):
            z = jnp.concatenate(rows[h], axis=0)
            x = dot(z.T.astype(BF16), back).astype(BF16)
            o_ref[32 * h + a] = x[:64]
            o_ref[32 * h + 16 + a] = x[64:]


def collect(r_ref, first, put):
    unit = eye(128)

    def step(col, carry):
        rows = [[], []]
        for slot in range(2):
            for r in range(ROWS):
                tile = r_ref[r * COLS + col, first + 16 * slot : first + 16 * slot + 16, :].astype(F32)
                rows[0].append(tile[:8])
                rows[1].append(tile[8:])
        for h in range(2):
            z = jnp.concatenate(rows[h], axis=0).astype(BF16)
            t = dot_nt(unit, z)
            put(4 * col + 2 * h, t[:64])
            put(4 * col + 2 * h + 1, t[64:])
        return carry

    lax.fori_loop(0, COLS, step, 0)


def spread(o_ref, first, get):
    unit = eye(128)

    def step(col, carry):
        parts = []
        for h in range(2):
            y = jnp.concatenate([get(4 * col + 2 * h), get(4 * col + 2 * h + 1)], axis=0)
            parts.append(dot_nt(unit, y))
        for slot in range(2):
            for r in range(ROWS):
                at = 64 * slot + 8 * r
                tile = jnp.concatenate([p[at : at + 8] for p in parts], axis=0)
                o_ref[r * COLS + col, first + 16 * slot : first + 16 * slot + 16, :] = tile.astype(BF16)
        return carry

    lax.fori_loop(0, COLS, step, 0)


def put_taps(dst_ref, at, v):
    lane = iota((CH, 128), 1) % GRID
    dst_ref[at, 0:64, :] = jnp.where(lane == 0, 0.0, pltpu.roll(v, 1, 1)).astype(BF16)
    dst_ref[at, 64:128, :] = v.astype(BF16)
    dst_ref[at, 128:192, :] = jnp.where(lane == GRID - 1, 0.0, pltpu.roll(v, 127, 1)).astype(BF16)


def stack_weights(w_ref, dst_ref, adjoint):
    for kb in range(3):
        row = []
        for ka in range(3):
            if adjoint:
                row.append(w_ref[3 * (2 - ka) + (2 - kb)].astype(F32).T.astype(BF16))
            else:
                row.append(w_ref[3 * ka + kb])
        dst_ref[64 * kb : 64 * kb + 64, :] = jnp.concatenate(row, axis=1)


def convolve(w_ref, taps_ref, emit, state):
    w = w_ref[...]

    def step(t, carry):
        one, two, state = carry
        rhs = jnp.concatenate([taps_ref[2 * t], taps_ref[2 * t + 1]], axis=1)
        p = dot(w, rhs)
        a0, a1, a2 = p[0:64, :128], p[64:128, :128], p[128:192, :128]
        b0, b1, b2 = p[0:64, 128:], p[64:128, 128:], p[128:192, 128:]
        state = emit(2 * t - 1, one + a2, state)
        state = emit(2 * t, two + a1 + b2, state)
        return a0 + b1, b0, state

    zero = jnp.zeros((CH, 128), F32)
    one, two, state = lax.fori_loop(0, GRID // 2, step, (zero, zero, state))
    return emit(GRID - 1, one, state)


def weight_terms(u_ref, taps_ref, acc_ref):
    acc_ref[...] = jnp.zeros((192, 192), F32)

    def step(t, carry):
        lhs = []
        rhs = []
        for k in range(4):
            at = 4 * t + k
            lhs.append(jnp.concatenate([u_ref[at + 2], u_ref[at + 1], u_ref[at]], axis=0))
            rhs.append(taps_ref[at])
        acc_ref[...] += dot_nt(jnp.concatenate(lhs, axis=1), jnp.concatenate(rhs, axis=1))
        return carry

    lax.fori_loop(0, GRID // 4, step, 0)


def own_row(first, second):
    one = jnp.broadcast_to(jnp.sum(first, axis=1, keepdims=True), (CH, 128)).T
    two = jnp.broadcast_to(jnp.sum(second, axis=1, keepdims=True), (CH, 128)).T
    return jnp.concatenate([one[:, :64], two[:, :64]], axis=1)


def turned(row):
    return jnp.broadcast_to(row, (128, 128)).T


def moments(table_ref):
    table = table_ref[...]
    sums = jnp.sum(table, axis=0, keepdims=True)
    mean_row = sums / CELLS
    off = table / OWN - mean_row
    between = turned(OWN * jnp.sum(off * off, axis=0, keepdims=True))
    total = turned(sums)
    mean = total[:64] / CELLS
    spread_ = (total[64:] + between[:64]) / CELLS
    return mean, lax.rsqrt(spread_ + epsilon)


def means(table_ref):
    total = turned(jnp.sum(table_ref[...], axis=0, keepdims=True))
    return total[:64] / CELLS, total[64:] / CELLS


def own_moments(act_ref, total):
    mean = jnp.broadcast_to(jnp.sum(total, axis=1, keepdims=True) / OWN, (CH, 128))

    def step(j, acc):
        off = act_ref[j] - mean
        return acc + off * off

    square = lax.fori_loop(0, GRID, step, jnp.zeros((CH, 128), F32), unroll=4)
    return own_row(total, square)


def symmetric(x_ref, k_ref, flag, put):
    bins = x_ref.shape[1]
    k_ref[...] = jnp.swapaxes(x_ref[...], 0, 1)

    def step(k, carry):
        x = k_ref[k]
        t = x.T
        low, high = t[:64], t[64:]
        m = jnp.where(
            flag > 0,
            jnp.concatenate([low, high], axis=1),
            jnp.concatenate([high, low], axis=1),
        )
        k_ref[k] = 0.5 * (x + m)
        return carry

    lax.fori_loop(0, bins, step, 0, unroll=2)
    x_ref[...] = jnp.swapaxes(k_ref[...], 0, 1)


def first_kernel(flag_ref, r_ref, w_ref, act_ref, stat_ref, taps_ref, sym_ref, x_ref, k_ref, w_s):
    stack_weights(w_ref, w_s, False)

    def put(j, v):
        put_taps(taps_ref, j, v)

    collect(r_ref, 0, put)

    def emit(j, v, total):
        act_ref[jnp.maximum(j, 0)] = v
        return total + jnp.where(j >= 0, v, 0.0)

    total = convolve(w_s, taps_ref, emit, jnp.zeros((CH, 128), F32))
    stat_ref[...] = own_moments(act_ref, total)

    def put_cot(j, v):
        x_ref[j] = v[:40]

    collect(r_ref, 32, put_cot)
    symmetric(x_ref, k_ref, flag_ref[0], None)
    sym_ref[...] = x_ref[...].astype(BF16)


def second_kernel(act_ref, table_ref, w_ref, out_ref, stat_ref, taps_ref, w_s):
    stack_weights(w_ref, w_s, False)
    mean, inverse = moments(table_ref)

    def step(j, carry):
        put_taps(taps_ref, j, elu((act_ref[j] - mean) * inverse))
        return carry

    lax.fori_loop(0, GRID, step, 0, unroll=2)

    def emit(j, v, total):
        out_ref[jnp.maximum(j, 0)] = v
        return total + jnp.where(j >= 0, v, 0.0)

    total = convolve(w_s, taps_ref, emit, jnp.zeros((CH, 128), F32))
    stat_ref[...] = own_moments(out_ref, total)


def third_kernel(act_ref, table_ref, taps_ref, sym_ref, head_ref, bias_ref, grad_ref, stat_ref, raw_ref, term_ref):
    mean, inverse = moments(table_ref)
    head = head_ref[...]
    head_t = head.astype(F32).T.astype(BF16)
    bias = bias_ref[...]

    def step(j, carry):
        first, second, count, term = carry
        normed = (act_ref[j] - mean) * inverse
        summed = normed + taps_ref[j, 64:128, :].astype(F32)
        hidden = elu(summed).astype(BF16)
        sym = sym_ref[j]
        raw_ref[j] = dot(head, hidden) + bias
        grad = dot(head_t, sym) * slope(summed)
        grad_ref[j] = grad
        term = term + dot_nt(sym, hidden)
        return first + grad, second + grad * normed, count + sym.astype(F32), term

    zero = jnp.zeros((CH, 128), F32)
    first, second, count, term = lax.fori_loop(
        0, GRID, step, (zero, zero, jnp.zeros((40, 128), F32), jnp.zeros((40, 64), F32)), unroll=2
    )
    stat_ref[...] = own_row(first, second)
    count = jnp.broadcast_to(jnp.sum(count, axis=1, keepdims=True), (40, 64))
    term_ref[...] = jnp.concatenate([term, count], axis=1)


def store_terms(acc_ref, out_ref):
    acc = acc_ref[...]
    left = acc[:, :128]
    right = jnp.concatenate([acc[:96, 128:], acc[96:, 128:]], axis=1)
    out_ref[0:24] = left.reshape(24, 8, 128)
    out_ref[24:36] = right.reshape(12, 8, 128)


def fourth_kernel(
    flag_ref, act_ref, table_ref, grad_ref, table3_ref, taps_ref, act1_ref, table1_ref, w_ref, term_ref, raw_ref,
    out_ref, stat_ref, part_ref, logit_ref,
    u_ref, utaps_ref, acc_ref, w_s, k_ref, x_ref
):
    stack_weights(w_ref, w_s, True)
    mean, inverse = moments(table_ref)
    first_mean, second_mean = means(table3_ref)
    u_ref[0] = jnp.zeros((CH, 128), BF16)
    u_ref[GRID + 1] = jnp.zeros((CH, 128), BF16)

    def step(j, carry):
        normed = (act_ref[j] - mean) * inverse
        u = inverse * (grad_ref[j] - first_mean - normed * second_mean)
        u_ref[j + 1] = u.astype(BF16)
        put_taps(utaps_ref, j, u)
        return carry

    lax.fori_loop(0, GRID, step, 0, unroll=2)
    mean1, inverse1 = moments(table1_ref)

    def emit(j, v, carry):
        first, second = carry
        at = jnp.maximum(j, 0)
        normed = (act1_ref[at] - mean1) * inverse1
        grad = jnp.where(j >= 0, v * slope(normed), 0.0)
        out_ref[at] = grad
        return first + grad, second + grad * normed

    zero = jnp.zeros((CH, 128), F32)
    first, second = convolve(w_s, utaps_ref, emit, (zero, zero))
    stat_ref[...] = own_row(first, second)
    weight_terms(u_ref, taps_ref, acc_ref)
    store_terms(acc_ref, part_ref)
    part_ref[36:41] = term_ref[...].reshape(5, 8, 128)
    x_ref[...] = raw_ref[...]
    symmetric(x_ref, k_ref, flag_ref[0], None)
    logit_ref[...] = x_ref[...].astype(BF16)


def fifth_kernel(
    grad_ref, table4_ref, act1_ref, table1_ref, taps_ref, part_ref, utaps_ref, u_ref, acc_ref
):
    mean1, inverse1 = moments(table1_ref)
    first_mean, second_mean = means(table4_ref)
    u_ref[0] = jnp.zeros((CH, 128), BF16)
    u_ref[GRID + 1] = jnp.zeros((CH, 128), BF16)

    def step(j, carry):
        normed = (act1_ref[j] - mean1) * inverse1
        u = inverse1 * (grad_ref[j] - first_mean - normed * second_mean)
        u_ref[j + 1] = u.astype(BF16)
        put_taps(utaps_ref, j, u)
        return carry

    lax.fori_loop(0, GRID, step, 0, unroll=2)
    weight_terms(u_ref, taps_ref, acc_ref)
    store_terms(acc_ref, part_ref)


def sixth_kernel(utaps_ref, w_ref, grad_ref, logit_ref, out_ref, x_ref, w_s):
    stack_weights(w_ref, w_s, True)

    def emit(j, v, carry):
        at = jnp.maximum(j, 0)
        x_ref[at] = (v + grad_ref[at]).astype(BF16)
        return carry

    convolve(w_s, utaps_ref, emit, 0)
    spread(out_ref, 0, lambda j: x_ref[j])
    pad = jnp.zeros((WIDE, 128), BF16)
    spread(out_ref, 32, lambda j: jnp.concatenate([logit_ref[j], pad], axis=0))


def sum_kernel(r_ref, o_ref):
    def step(k, acc):
        return acc + r_ref[k]

    total = lax.fori_loop(1, DEVICES, step, r_ref[0], unroll=8)
    o_ref[...] = jnp.broadcast_to(total[None], o_ref.shape)


def call(kernel, outs, scratch=(), smem=0, n=0):
    specs = [pl.BlockSpec(memory_space=pltpu.SMEM)] * smem + [
        pl.BlockSpec(memory_space=pltpu.VMEM)
    ] * n
    return pl.pallas_call(
        kernel,
        out_shape=tuple(jax.ShapeDtypeStruct(s, d) for s, d in outs),
        in_specs=specs,
        out_specs=tuple(pl.BlockSpec(memory_space=pltpu.VMEM) for _ in outs),
        scratch_shapes=[pltpu.VMEM(s, d) for s, d in scratch],
    )


def exchange(x):
    return lax.all_to_all(x, ("row", "col"), split_axis=0, concat_axis=0, tiled=True)


FIELD = ((GRID, CH, 128), F32)
HALF = ((GRID, CH, 128), BF16)
TAPS = ((GRID, 192, 128), BF16)
PADDED = ((GRID + 2, CH, 128), BF16)
STAT = ((128, 128), F32)
STACK = ((192, 192), BF16)
ACC = ((192, 192), F32)
PART = ((DEVICES, 8, 128), F32)
BINF = ((GRID, 40, 128), F32)
BINH = ((GRID, 40, 128), BF16)
BINK = ((40, GRID, 128), F32)


def terms_of(part):
    left = part[0:24].reshape(192, 128)
    right = part[24:36].reshape(96, 128)
    right = jnp.concatenate([right[:, :64], right[:, 64:]], axis=0)
    acc = jnp.concatenate([left, right], axis=1)
    return acc.reshape(3, CH, 3, CH).transpose(2, 0, 1, 3).reshape(9, CH, CH)


def on_device(features, conv_first, conv_second, head_weight, head_bias, cotangent):
    spot = lax.axis_index("row") * COLS + lax.axis_index("col")
    flag = (spot >= FIRST_DIAGONAL).astype(jnp.int32).reshape(1)
    head = jnp.pad(head_weight, ((0, 3), (0, 0)))
    bias = jnp.broadcast_to(jnp.pad(head_bias, (0, 3))[:, None], (40, 128))
    cot = jnp.pad(cotangent, ((0, CH - BINS), (0, 0), (0, 0)))

    packed = call(pack_kernel, [((DEVICES, 32, 128), BF16)], n=1)
    sent = jnp.concatenate(
        [packed(features.transpose(1, 0, 2))[0], packed(cot.transpose(1, 0, 2))[0]], axis=1
    )
    cells = exchange(sent)

    act1, stat, taps, sym = call(
        first_kernel, [FIELD, STAT, TAPS, BINH], [BINF, BINK, STACK], smem=1, n=2
    )(flag, cells, conv_first)
    table1 = exchange(stat)
    act2, stat, taps2 = call(second_kernel, [FIELD, STAT, TAPS], [STACK], n=3)(
        act1, table1, conv_second
    )
    table2 = exchange(stat)
    grad, stat, raw, term = call(third_kernel, [FIELD, STAT, BINF, ((40, 128), F32)], n=6)(
        act2, table2, taps, sym, head, bias
    )
    table3 = exchange(stat)
    grad1, stat, part2, logit = call(
        fourth_kernel, [FIELD, STAT, PART, BINH], [PADDED, TAPS, ACC, STACK, BINK, BINF], smem=1, n=10
    )(flag, act2, table2, grad, table3, taps2, act1, table1, conv_second, term, raw)
    table4 = exchange(stat)
    got2 = exchange(part2)
    part1, utaps = call(fifth_kernel, [PART, TAPS], [PADDED, ACC], n=5)(
        grad1, table4, act1, table1, taps
    )
    got1 = exchange(part1)
    result = exchange(
        call(sixth_kernel, [((DEVICES, 64, 128), BF16)], [HALF, STACK], n=4)(
            utaps, conv_first, grad, logit
        )[0]
    )
    summed = call(sum_kernel, [PART], n=1)
    all2 = exchange(summed(got2)[0])
    all1 = exchange(summed(got1)[0])
    unpacked = call(unpack_kernel, [HALF], n=1)
    input_grad = unpacked(result[:, :32])[0].transpose(1, 0, 2)
    logits = unpacked(result[:, 32:])[0].transpose(1, 0, 2)[:BINS]
    scale = 1.0 / 1024
    tail = all2[36:41].reshape(40, 128) * scale
    return (
        logits,
        input_grad,
        terms_of(all1) * scale,
        terms_of(all2) * scale,
        tail[:BINS, :CH],
        tail[:BINS, CH],
    )


def solution(mesh):
    placed = (P(None, "col", "row"), P(), P(), P(), P(), P(None, "col", "row"))
    return jax.shard_map(
        on_device,
        mesh=mesh,
        in_specs=placed,
        out_specs=(P(None, "col", "row"), P(None, "col", "row"), P(), P(), P(), P()),
        check_vma=False,
    )
```

time: 468 us -> 318 us (0.68); the launches traced: 460 us -> 317 us
  starting transfers between devices: 164 us -> 47.7 us
  Pallas kernels: 0 us -> 112 us
  local copies, waits for them, and re-layouts: 110 us -> 17.9 us
  other arithmetic: 57.1 us -> 3.61 us
  matrix products: 49.3 us -> 0 us
  blocking collectives: 0 us -> 45.8 us
  waiting for transfers between devices: 77.9 us -> 88.7 us
    pallas_call x0 -> x12, Pallas kernels: none -> 112 us  [the longest x1 23.2 us: on_device(): call(fourth_kernel, [FIELD, STAT, PART, BINH], [PADDED, TAPS, ACC, STACK,...]
    ppermute x20 -> x0, starting transfers between devices: 60.6 us -> none  [the longest x8 29.6 us: with_halo(): lax.ppermute(lax.slice_in_dim(block, block.shape[dim] - width, None, axis...]
    all_to_all x8 -> x7, starting transfers between devices: 104 us -> 47.7 us  [exchange(): lax.all_to_all(x, ('row', 'col'), split_axis=0, concat_axis=0, tiled=True)]
    all_to_all x8 -> x7, waiting for transfers between devices: 33.8 us -> 88.7 us  [exchange(): lax.all_to_all(x, ('row', 'col'), split_axis=0, concat_axis=0, tiled=True)]
    dot_general x57 -> x0, matrix products: 49.3 us -> none  [the longest x18 23.2 us: weight_terms(): lax.dot_general(flattened, window, (((1,), (1,)), ((), ())), preferred_el...]
    all_to_all x0 -> x3, blocking collectives: none -> 45.8 us  [exchange(): lax.all_to_all(x, ('row', 'col'), split_axis=0, concat_axis=0, tiled=True)]
    ppermute x20 -> x0, waiting for transfers between devices: 44.1 us -> none  [the longest x8 27.8 us: with_halo(): lax.ppermute(lax.slice_in_dim(block, 0, width, axis=dim), axis, backward)]
    ppermute x8 -> x0, local copies, waits for them, and re-layouts: 24.5 us -> none  [the longest x4 12.6 us: with_halo(): lax.ppermute(lax.slice_in_dim(block, 0, width, axis=dim), axis, backward)]
  transfers between devices with their start and end apart: 28 -> 7, of which waited for: 13 -> 6; matrix products, arithmetic and copies ran while one was open for 26% -> 2% of each run, Pallas kernels for 0% -> 10%
where the time goes in v2:
time: 318 us; the launch traced here: 317 us
  Pallas kernels  112 us (35%)
  waiting for transfers between devices  88.7 us (28%)
  starting transfers between devices  47.7 us (15%)
  blocking collectives  45.8 us (14%)
  local copies, waits for them, and re-layouts  17.9 us (6%)
  other arithmetic  3.61 us (1%)
    all_to_all x7, waiting for transfers between devices, exchange(): lax.all_to_all(x, ('row', 'col'), split_axis=0, concat_axis=0, tiled=True)  88.7 us
    all_to_all x7, starting transfers between devices, exchange(): lax.all_to_all(x, ('row', 'col'), split_axis=0, concat_axis=0, tiled=True)  47.7 us
    all_to_all x3, blocking collectives, exchange(): lax.all_to_all(x, ('row', 'col'), split_axis=0, concat_axis=0, tiled=True)  45.8 us
    pallas_call x1, Pallas kernels, on_device(): call(fourth_kernel, [FIELD, STAT, PART, BINH], [PADDED, TAPS, ACC, STACK,...  23.2 us
    pallas_call x1, Pallas kernels, on_device(): call(first_kernel, [FIELD, STAT, TAPS, BINH], [BINF, BINK, STACK], smem=1...  21.2 us
    pallas_call x1, Pallas kernels, on_device(): call(sixth_kernel, [((DEVICES, 64, 128), BF16)], [HALF, STACK], n=4)  15.5 us
    pallas_call x1, Pallas kernels, on_device(): call(second_kernel, [FIELD, STAT, TAPS], [STACK], n=3)  13.4 us
    pallas_call x1, Pallas kernels, on_device(): call(fifth_kernel, [PART, TAPS], [PADDED, ACC], n=5)  11.9 us
  transfers between devices with their start and end apart: 7, of which 6 were waited for; matrix products, arithmetic and copies ran while one was open for 2% of the time, Pallas kernels for 10%

profile of v2, /device:TPU:1, one launch (start us, length us, event | category | flops | bytes accessed | tf_op | source)
XLA Modules:
  0.0 316.6 jit_solution(1206173327921478824)
XLA Ops:
  3.3 3.1 shard_map.110
  6.4 1.6 copy.39
  8.0 3.1 shard_map.109
  11.1 2.9 pad_maximum_fusion
  14.0 11.5 %all-to-all-start = ((bf16[128,64,128]{2,1,0:T(8,128)(2,1)}), bf16[128,64,128]{2,1,0:T(8,128)(2,1)S(1)}, u32[]{:S(2)}, u32[]{:S(2)}) async-start(bf16[128,64,128]{2,1,0:T(8,128)(2,1)} %pad_maximum_fusion), calls=%async_computation | async-start | bytes 4194304 | tf_op jit(solution)/shard_map/all_to_all | solution.py:423
  25.5 30.1 %all-to-all-done.r_ref = bf16[128,64,128]{2,1,0:T(8,128)(2,1)S(1)} async-done(((bf16[128,64,128]{2,1,0:T(8,128)(2,1)}), bf16[128,64,128]{2,1,0:T(8,128)(2,1)S(1)}, u32[]{:S(2)}, u32[]{:S(2)}) %all-to-all-start) | async-done | bytes 2097184 | tf_op jit(solution)/shard_map/all_to_all | solution.py:423
  56.9 21.2 %shard_map.111 = (f32[64,64,128]{2,1,0:T(8,128)}, f32[128,128]{1,0:T(8,128)}, bf16[64,192,128]{2,1,0:T(8,128)(2,1)}, bf16[64,40,128]{2,1,0:T(8,128)(2,1)}) custom-call(s32[1]{0:T(128)} %bitcast.flag_ref, bf16[128,64,128]{2,1,0:T(8,128)(2,1)} %copy-done, bf16[9,64,64]{2,1,0:T(8,128)(2,1)} %w_ref.7), custom_call_target="tpu_custom_call" | custom-call | tf_op jit(solution)/shard_map/pallas_call | solution.py:460
  78.2 16.0 %all_to_all.74 = f32[128,1,128]{2,1,0:T(1,128)} all-to-all(f32[128,1,128]{2,1,0:T(1,128)} %bitcast.57), channel_id=1, replica_groups=mesh['row'=8,'col'=16] {'row','col'}, dimensions={0} | all-to-all | bytes 131072 | tf_op jit(solution)/shard_map/all_to_all | solution.py:423
  94.2 13.4 %shard_map.112 = (f32[64,64,128]{2,1,0:T(8,128)}, f32[128,128]{1,0:T(8,128)}, bf16[64,192,128]{2,1,0:T(8,128)(2,1)}) custom-call(f32[64,64,128]{2,1,0:T(8,128)} %get-tuple-element.23.act_ref.act1_ref, f32[128,128]{1,0:T(8,128)} %bitcast.44, bf16[9,64,64]{2,1,0:T(8,128)(2,1)} %w_ref.6), custom_call_target="tpu_custom_call" | custom-call | tf_op jit(solution)/shard_map/pallas_call | solution.py:464
  107.6 4.6 %all-to-all-start.2 = ((f32[128,1,128]{2,1,0:T(1,128)}), f32[128,1,128]{2,1,0:T(1,128)S(1)}, u32[]{:S(2)}, u32[]{:S(2)}) async-start(f32[128,1,128]{2,1,0:T(1,128)} %bitcast.54), calls=%async_computation.2 | async-start | bytes 131072 | tf_op jit(solution)/shard_map/all_to_all | solution.py:423
  112.8 8.9 %all-to-all-done.2 = f32[128,1,128]{2,1,0:T(1,128)S(1)} async-done(((f32[128,1,128]{2,1,0:T(1,128)}), f32[128,1,128]{2,1,0:T(1,128)S(1)}, u32[]{:S(2)}, u32[]{:S(2)}) %all-to-all-start.2) | async-done | bytes 65568 | tf_op jit(solution)/shard_map/all_to_all | solution.py:423
  122.4 11.1 %shard_map.113 = (f32[64,64,128]{2,1,0:T(8,128)}, f32[128,128]{1,0:T(8,128)}, f32[64,40,128]{2,1,0:T(8,128)}, f32[40,128]{1,0:T(8,128)}) custom-call(f32[64,64,128]{2,1,0:T(8,128)} %get-tuple-element.25.act_ref, f32[128,128]{1,0:T(8,128)} %bitcast.47, bf16[64,192,128]{2,1,0:T(8,128)(2,1)} %get-tuple-element.27.taps_ref, ...), custom_call_target="tpu_custom_call" | custom-call | tf_op jit(solution)/shard_map/pallas_call | solution.py:468
  133.5 14.9 %all_to_all.75 = f32[128,1,128]{2,1,0:T(1,128)} all-to-all(f32[128,1,128]{2,1,0:T(1,128)} %bitcast.56), channel_id=1, replica_groups=mesh['row'=8,'col'=16] {'row','col'}, dimensions={0} | all-to-all | bytes 131072 | tf_op jit(solution)/shard_map/all_to_all | solution.py:423
  148.5 23.2 %shard_map.114 = (f32[64,64,128]{2,1,0:T(8,128)}, f32[128,128]{1,0:T(8,128)}, f32[128,8,128]{2,1,0:T(8,128)}, bf16[64,40,128]{2,1,0:T(8,128)(2,1)}) custom-call(s32[1]{0:T(128)} %bitcast.flag_ref, f32[64,64,128]{2,1,0:T(8,128)} %get-tuple-element.25.act_ref, f32[128,128]{1,0:T(8,128)} %bitcast.48, f32[64,64,128]{2,1,0:T(8,128)} %get-tuple-element.29.grad_ref, ...), custom_call_target="tpu_custom_call" | custom-call | tf_op jit(solution)/shard_map/pallas_call | solution.py:472
  171.7 14.8 %all_to_all.76 = f32[128,1,128]{2,1,0:T(1,128)} all-to-all(f32[128,1,128]{2,1,0:T(1,128)} %bitcast.55), channel_id=1, replica_groups=mesh['row'=8,'col'=16] {'row','col'}, dimensions={0} | all-to-all | bytes 131072 | tf_op jit(solution)/shard_map/all_to_all | solution.py:423
  186.5 4.7 %all-to-all-start.8 = ((f32[128,8,128]{2,1,0:T(8,128)}), f32[128,8,128]{2,1,0:T(8,128)S(1)}, u32[]{:S(2)}, u32[]{:S(2)}) async-start(f32[128,8,128]{2,1,0:T(8,128)} %get-tuple-element.39), calls=%async_computation.8 | async-start | bytes 1048576 | tf_op jit(solution)/shard_map/all_to_all | solution.py:423
  191.2 11.9 %shard_map.115 = (f32[128,8,128]{2,1,0:T(8,128)}, bf16[64,192,128]{2,1,0:T(8,128)(2,1)}) custom-call(f32[64,64,128]{2,1,0:T(8,128)} %get-tuple-element.34.grad_ref, f32[128,128]{1,0:T(8,128)} %bitcast.51, f32[64,64,128]{2,1,0:T(8,128)} %get-tuple-element.23.act_ref.act1_ref, f32[128,128]{1,0:T(8,128)} %bitcast.46, ...), custom_call_target="tpu_custom_call" | custom-call | tf_op jit(solution)/shard_map/pallas_call | solution.py:477
  203.1 1.6 all-to-all-done.8.r_ref
  204.8 8.1 %all-to-all-start.6 = ((f32[128,8,128]{2,1,0:T(8,128)}), f32[128,8,128]{2,1,0:T(8,128)S(1)}, u32[]{:S(2)}, u32[]{:S(2)}) async-start(f32[128,8,128]{2,1,0:T(8,128)} %get-tuple-element.38), calls=%async_computation.6 | async-start | bytes 1048576 | tf_op jit(solution)/shard_map/all_to_all | solution.py:423
  212.9 2.1 shard_map.120
  214.9 11.5 %all-to-all-done.6.r_ref = f32[128,8,128]{2,1,0:T(8,128)S(1)} async-done(((f32[128,8,128]{2,1,0:T(8,128)}), f32[128,8,128]{2,1,0:T(8,128)S(1)}, u32[]{:S(2)}, u32[]{:S(2)}) %all-to-all-start.6) | async-done | bytes 524320 | tf_op jit(solution)/shard_map/all_to_all | solution.py:423
  226.4 4.6 %all-to-all-start.9 = ((f32[128,8,128]{2,1,0:T(8,128)}), f32[128,8,128]{2,1,0:T(8,128)S(1)}, u32[]{:S(2)}, u32[]{:S(2)}) async-start(f32[128,8,128]{2,1,0:T(8,128)} %shard_map.120), calls=%async_computation.9 | async-start | bytes 1048576 | tf_op jit(solution)/shard_map/all_to_all | solution.py:423
  231.0 2.1 shard_map.119
  233.1 11.5 %all-to-all-done.9 = f32[128,8,128]{2,1,0:T(8,128)S(1)} async-done(((f32[128,8,128]{2,1,0:T(8,128)}), f32[128,8,128]{2,1,0:T(8,128)S(1)}, u32[]{:S(2)}, u32[]{:S(2)}) %all-to-all-start.9) | async-done | bytes 524320 | tf_op jit(solution)/shard_map/all_to_all | solution.py:423
  244.6 4.6 %all-to-all-start.7 = ((f32[128,8,128]{2,1,0:T(8,128)}), f32[128,8,128]{2,1,0:T(8,128)S(1)}, u32[]{:S(2)}, u32[]{:S(2)}) async-start(f32[128,8,128]{2,1,0:T(8,128)} %shard_map.119), calls=%async_computation.7 | async-start | bytes 1048576 | tf_op jit(solution)/shard_map/all_to_all | solution.py:423
  249.1 15.5 %shard_map.116 = bf16[128,64,128]{2,1,0:T(8,128)(2,1)} custom-call(bf16[64,192,128]{2,1,0:T(8,128)(2,1)} %get-tuple-element.36.utaps_ref, bf16[9,64,64]{2,1,0:T(8,128)(2,1)} %w_ref.7, f32[64,64,128]{2,1,0:T(8,128)} %get-tuple-element.29.grad_ref, bf16[64,40,128]{2,1,0:T(8,128)(2,1)} %get-tuple-element.37.logit_ref), custom_call_target="tpu_custom_call" | custom-call | tf_op jit(solution)/shard_map/pallas_call | solution.py:482
  264.6 9.8 %all-to-all-start.5 = ((bf16[128,64,128]{2,1,0:T(8,128)(2,1)}), bf16[128,64,128]{2,1,0:T(8,128)(2,1)S(1)}, u32[]{:S(2)}, u32[]{:S(2)}) async-start(bf16[128,64,128]{2,1,0:T(8,128)(2,1)} %shard_map.116), calls=%async_computation.5 | async-start | bytes 4194304 | tf_op jit(solution)/shard_map/all_to_all | solution.py:423
  279.3 25.1 %all-to-all-done.5 = bf16[128,64,128]{2,1,0:T(8,128)(2,1)S(1)} async-done(((bf16[128,64,128]{2,1,0:T(8,128)(2,1)}), bf16[128,64,128]{2,1,0:T(8,128)(2,1)S(1)}, u32[]{:S(2)}, u32[]{:S(2)}) %all-to-all-start.5) | async-done | bytes 2097184 | tf_op jit(solution)/shard_map/all_to_all | solution.py:423
  304.5 1.7 fusion.1
  306.2 2.7 shard_map.118
  308.9 2.9 copy.37
  311.8 2.7 shard_map.117
  (40 shorter events, 12.4 us)
Async XLA Ops:
  2.1 4.3 %copy-start.4 = (bf16[64,64,128]{2,1,0:T(8,128)(2,1)S(1)}, bf16[64,64,128]{2,1,0:T(8,128)(2,1)}, u32[]{:S(2)}) copy-start(bf16[64,64,128]{2,1,0:T(8,128)(2,1)} %param.6) | copy-start | bytes 3145732
  6.4 4.7 %copy-start.1 = (bf16[128,32,128]{2,1,0:T(8,128)(2,1)S(1)}, bf16[128,32,128]{2,1,0:T(8,128)(2,1)}, u32[]{:S(2)}) copy-start(bf16[128,32,128]{2,1,0:T(8,128)(2,1)} %shard_map.110) | copy-start | bytes 3145732
  14.0 41.6 %all-to-all-start = ((bf16[128,64,128]{2,1,0:T(8,128)(2,1)}), bf16[128,64,128]{2,1,0:T(8,128)(2,1)S(1)}, u32[]{:S(2)}, u32[]{:S(2)}) async-start(bf16[128,64,128]{2,1,0:T(8,128)(2,1)} %pad_maximum_fusion), calls=%async_computation | async-start | bytes 4194304 | tf_op jit(solution)/shard_map/all_to_all | solution.py:423
  55.6 1.4 copy-start
  56.9 55.3 %copy-start.8 = (f32[37]{0:T(128)S(1)}, f32[37]{0:T(128)}, u32[]{:S(2)}) copy-start(f32[37]{0:T(128)} %param.10) | copy-start | bytes 448
  56.9 55.3 %copy-start.7 = (bf16[37,64]{1,0:T(8,128)(2,1)S(1)}, bf16[37,64]{1,0:T(8,128)(2,1)}, u32[]{:S(2)}) copy-start(bf16[37,64]{1,0:T(8,128)(2,1)} %param.9) | copy-start | bytes 14212
  107.6 14.1 %all-to-all-start.2 = ((f32[128,1,128]{2,1,0:T(1,128)}), f32[128,1,128]{2,1,0:T(1,128)S(1)}, u32[]{:S(2)}, u32[]{:S(2)}) async-start(f32[128,1,128]{2,1,0:T(1,128)} %bitcast.54), calls=%async_computation.2 | async-start | bytes 131072 | tf_op jit(solution)/shard_map/all_to_all | solution.py:423
  121.7 0.7 copy-start.5
  186.5 18.3 %all-to-all-start.8 = ((f32[128,8,128]{2,1,0:T(8,128)}), f32[128,8,128]{2,1,0:T(8,128)S(1)}, u32[]{:S(2)}, u32[]{:S(2)}) async-start(f32[128,8,128]{2,1,0:T(8,128)} %get-tuple-element.39), calls=%async_computation.8 | async-start | bytes 1048576 | tf_op jit(solution)/shard_map/all_to_all | solution.py:423
  204.8 8.1 %copy-start.2 = (f32[128,8,128]{2,1,0:T(8,128)}, f32[128,8,128]{2,1,0:T(8,128)S(1)}, u32[]{:S(2)}) copy-start(f32[128,8,128]{2,1,0:T(8,128)S(1)} %all-to-all-done.8.r_ref) | copy-start | bytes 1572868
  204.8 21.7 %all-to-all-start.6 = ((f32[128,8,128]{2,1,0:T(8,128)}), f32[128,8,128]{2,1,0:T(8,128)S(1)}, u32[]{:S(2)}, u32[]{:S(2)}) async-start(f32[128,8,128]{2,1,0:T(8,128)} %get-tuple-element.38), calls=%async_computation.6 | async-start | bytes 1048576 | tf_op jit(solution)/shard_map/all_to_all | solution.py:423
  226.4 4.6 %copy-start.3 = (f32[128,8,128]{2,1,0:T(8,128)}, f32[128,8,128]{2,1,0:T(8,128)S(1)}, u32[]{:S(2)}) copy-start(f32[128,8,128]{2,1,0:T(8,128)S(1)} %all-to-all-done.6.r_ref) | copy-start | bytes 1572868
  226.4 18.1 %all-to-all-start.9 = ((f32[128,8,128]{2,1,0:T(8,128)}), f32[128,8,128]{2,1,0:T(8,128)S(1)}, u32[]{:S(2)}, u32[]{:S(2)}) async-start(f32[128,8,128]{2,1,0:T(8,128)} %shard_map.120), calls=%async_computation.9 | async-start | bytes 1048576 | tf_op jit(solution)/shard_map/all_to_all | solution.py:423
  244.6 20.1 %all-to-all-start.7 = ((f32[128,8,128]{2,1,0:T(8,128)}), f32[128,8,128]{2,1,0:T(8,128)S(1)}, u32[]{:S(2)}, u32[]{:S(2)}) async-start(f32[128,8,128]{2,1,0:T(8,128)} %shard_map.119), calls=%async_computation.7 | async-start | bytes 1048576 | tf_op jit(solution)/shard_map/all_to_all | solution.py:423
  264.6 39.9 %all-to-all-start.5 = ((bf16[128,64,128]{2,1,0:T(8,128)(2,1)}), bf16[128,64,128]{2,1,0:T(8,128)(2,1)S(1)}, u32[]{:S(2)}, u32[]{:S(2)}) async-start(bf16[128,64,128]{2,1,0:T(8,128)(2,1)} %shard_map.116), calls=%async_computation.5 | async-start | bytes 4194304 | tf_op jit(solution)/shard_map/all_to_all | solution.py:423
  277.0 0.6 copy-start.6

commit v3 on v2

v3 whole, which is shorter than its diff:
```python
import jax
import jax.numpy as jnp
from jax import lax
from jax.experimental import pallas as pl
from jax.experimental.pallas import tpu as pltpu
from jax.sharding import PartitionSpec as P


STEP = 16
GRID = 64
epsilon = 1e-05
F32 = jnp.float32
BF16 = jnp.bfloat16
ROWS = 8
COLS = 16
DEVICES = 128
CH = 64
BINS = 37
CELLS = float(1024 * 1024)
OWN = float(64 * 128)
WIDE = 24
PARTS = 4


def class_table():
    place = {}
    count = 0
    for a in range(STEP):
        for b in range(a + 1, STEP):
            place[(a, b)] = (count, 0)
            place[(b, a)] = (count, 1)
            count += 1
    for a in range(STEP // 2):
        place[(a, a)] = (count, 0)
        place[(a + 8, a + 8)] = (count, 1)
        count += 1
    return place, STEP * (STEP - 1) // 2


PLACE, FIRST_DIAGONAL = class_table()


def dot(lhs, rhs):
    return jnp.dot(lhs, rhs, preferred_element_type=F32)


def dot_nt(lhs, rhs):
    return lax.dot_general(lhs, rhs, (((1,), (1,)), ((), ())), preferred_element_type=F32)


def iota(shape, dim):
    return lax.broadcasted_iota(jnp.int32, shape, dim)


def eye(n):
    return jnp.where(iota((n, n), 0) == iota((n, n), 1), 1.0, 0.0).astype(BF16)


def class_order():
    row = iota((128, 128), 0)
    lane = iota((128, 128), 1)
    return jnp.where(lane == STEP * (row % 8) + row // 8, 1.0, 0.0).astype(BF16)


def elu(z):
    return jnp.where(z > 0, z, jnp.exp(jnp.minimum(z, 0.0)) - 1.0)


def slope(z):
    return jnp.where(z > 0, 1.0, jnp.exp(jnp.minimum(z, 0.0)))


def pack_kernel(f_ref, c_ref, o_ref, f_s, c_s):
    order = class_order()
    f_s[...] = f_ref[...].astype(F32)
    c_s[0:BINS] = c_ref[...].astype(F32)
    c_s[BINS:40] = jnp.zeros((40 - BINS, GRID, 128), F32)
    pad = jnp.zeros((WIDE, 128), F32)

    def feature(j):
        return f_s[:, j, :]

    def bins(j):
        return jnp.concatenate([c_s[:, j, :], pad], axis=0)

    for first, get in ((0, feature), (32, bins)):
        for a in range(STEP):
            parts = []
            for h in range(2):
                x = jnp.concatenate([get(32 * h + a), get(32 * h + 16 + a)], axis=0)
                parts.append(dot_nt(order, x.astype(BF16)))
            for b in range(STEP):
                dest, slot = PLACE[(a, b)]
                tile = jnp.concatenate([p[8 * b : 8 * b + 8] for p in parts], axis=0)
                at = first + 16 * slot
                o_ref[dest, at : at + 16, :] = tile.astype(BF16)


def last_kernel(r_ref, f_ref, l_ref, first_ref, second_ref, head_ref, bias_ref, f_s, c_s):
    back = class_order()

    def feature(j, x):
        f_s[:, j, :] = x

    def bins(j, x):
        c_s[:, j, :] = x[:40]

    for first, put in ((0, feature), (32, bins)):
        for a in range(STEP):
            rows = [[], []]
            for b in range(STEP):
                src, slot = PLACE[(a, b)]
                at = first + 16 * slot
                tile = r_ref[src, at : at + 16, :].astype(F32)
                rows[0].append(tile[:8])
                rows[1].append(tile[8:])
            for h in range(2):
                z = jnp.concatenate(rows[h], axis=0)
                x = dot(z.T.astype(BF16), back)
                put(32 * h + a, x[:64])
                put(32 * h + 16 + a, x[64:])
    f_ref[...] = f_s[...].astype(BF16)
    l_ref[...] = c_s[0:BINS].astype(BF16)
    tail = r_ref[:, 64:72, :].astype(F32) * (1.0 / 1024)

    def fill(at, out_ref):
        low, mid, high = tail[:, at], tail[:, at + 1], tail[:, at + 2]
        left = jnp.concatenate([low, mid[:64]], axis=0)
        right = jnp.concatenate([mid[64:], high[:32]], axis=0)
        right = jnp.concatenate([right[:, :64], right[:, 64:]], axis=0)
        for kb in range(3):
            span = slice(64 * kb, 64 * kb + 64)
            out_ref[kb] = left[span, :64]
            out_ref[3 + kb] = left[span, 64:]
            out_ref[6 + kb] = right[span]
        return high

    fill(0, first_ref)
    high = fill(3, second_ref)
    head_ref[...] = high[32 : 32 + BINS, :64]
    bias_ref[...] = jnp.broadcast_to(high[:, 64:65], (128, 128)).T[0:1, 32 : 32 + BINS]


def collect(r_ref, first, put):
    unit = eye(128)

    def step(col, carry):
        rows = [[], []]
        for slot in range(2):
            for r in range(ROWS):
                tile = r_ref[r * COLS + col, first + 16 * slot : first + 16 * slot + 16, :].astype(F32)
                rows[0].append(tile[:8])
                rows[1].append(tile[8:])
        for h in range(2):
            z = jnp.concatenate(rows[h], axis=0).astype(BF16)
            t = dot_nt(unit, z)
            put(4 * col + 2 * h, t[:64])
            put(4 * col + 2 * h + 1, t[64:])
        return carry

    lax.fori_loop(0, COLS, step, 0)


def spread(o_ref, first, get):
    unit = eye(128)

    def step(col, carry):
        parts = []
        for h in range(2):
            y = jnp.concatenate([get(4 * col + 2 * h), get(4 * col + 2 * h + 1)], axis=0)
            parts.append(dot_nt(unit, y))
        for slot in range(2):
            for r in range(ROWS):
                at = 64 * slot + 8 * r
                tile = jnp.concatenate([p[at : at + 8] for p in parts], axis=0)
                o_ref[r * COLS + col, first + 16 * slot : first + 16 * slot + 16, :] = tile.astype(BF16)
        return carry

    lax.fori_loop(0, COLS, step, 0)


def put_taps(dst_ref, at, v):
    lane = iota((CH, 128), 1) % GRID
    dst_ref[at, 0:64, :] = jnp.where(lane == 0, 0.0, pltpu.roll(v, 1, 1)).astype(BF16)
    dst_ref[at, 64:128, :] = v.astype(BF16)
    dst_ref[at, 128:192, :] = jnp.where(lane == GRID - 1, 0.0, pltpu.roll(v, 127, 1)).astype(BF16)


def stack_weights(w_ref, dst_ref, adjoint):
    for kb in range(3):
        row = []
        for ka in range(3):
            if adjoint:
                row.append(w_ref[3 * (2 - ka) + (2 - kb)].astype(F32).T.astype(BF16))
            else:
                row.append(w_ref[3 * ka + kb])
        dst_ref[64 * kb : 64 * kb + 64, :] = jnp.concatenate(row, axis=1)


def convolve(w_ref, taps_ref, emit, state, before=None, after=None):
    w = w_ref[...]

    def step(t, carry):
        one, two, state = carry
        rhs = jnp.concatenate([taps_ref[2 * t], taps_ref[2 * t + 1]], axis=1)
        p = dot(w, rhs)
        a0, a1, a2 = p[0:64, :128], p[64:128, :128], p[128:192, :128]
        b0, b1, b2 = p[0:64, 128:], p[64:128, 128:], p[128:192, 128:]
        state = emit(2 * t - 1, one + a2, state)
        state = emit(2 * t, two + a1 + b2, state)
        return a0 + b1, b0, state

    zero = jnp.zeros((CH, 128), F32)
    carry = (zero, zero, state)
    for part in range(PARTS):
        if before is not None:
            before(part)
        carry = lax.fori_loop(8 * part, 8 * part + 8, step, carry)
        if part == PARTS - 1:
            one, two, state = carry
            state = emit(GRID - 1, one, state)
        if after is not None:
            after(part)
    return state


def whole(part):
    return slice(16 * part, 16 * part + 16)


def ready(part):
    first = 16 * part - 1 if part else 0
    last = 16 * part + 15 if part < PARTS - 1 else GRID
    return slice(first, last)


def copies(src, dst, sems, span=whole):
    return [
        pltpu.make_async_copy(src.at[span(part)], dst.at[span(part)], sems.at[part])
        for part in range(PARTS)
    ]


def start(*groups):
    for group in groups:
        for copy in group:
            copy.start()


def wait(*groups):
    for group in groups:
        for copy in group:
            copy.wait()


def weight_terms(u_ref, taps_ref, acc_ref):
    acc_ref[...] = jnp.zeros((192, 192), F32)

    def step(t, carry):
        lhs = []
        rhs = []
        for k in range(4):
            at = 4 * t + k
            lhs.append(jnp.concatenate([u_ref[at + 2], u_ref[at + 1], u_ref[at]], axis=0))
            rhs.append(taps_ref[at])
        acc_ref[...] += dot_nt(jnp.concatenate(lhs, axis=1), jnp.concatenate(rhs, axis=1))
        return carry

    lax.fori_loop(0, GRID // 4, step, 0)


def own_row(first, second):
    one = jnp.broadcast_to(jnp.sum(first, axis=1, keepdims=True), (CH, 128)).T
    two = jnp.broadcast_to(jnp.sum(second, axis=1, keepdims=True), (CH, 128)).T
    return jnp.concatenate([one[:, :64], two[:, :64]], axis=1)


def turned(row):
    return jnp.broadcast_to(row, (128, 128)).T


def moments(table_ref):
    table = table_ref[...]
    sums = jnp.sum(table, axis=0, keepdims=True)
    mean_row = sums / CELLS
    off = table / OWN - mean_row
    between = turned(OWN * jnp.sum(off * off, axis=0, keepdims=True))
    total = turned(sums)
    mean = total[:64] / CELLS
    spread_ = (total[64:] + between[:64]) / CELLS
    return mean, lax.rsqrt(spread_ + epsilon)


def means(table_ref):
    total = turned(jnp.sum(table_ref[...], axis=0, keepdims=True))
    return total[:64] / CELLS, total[64:] / CELLS


def own_moments(act_ref, total):
    mean = jnp.broadcast_to(jnp.sum(total, axis=1, keepdims=True) / OWN, (CH, 128))

    def step(j, acc):
        off = act_ref[j] - mean
        return acc + off * off

    square = lax.fori_loop(0, GRID, step, jnp.zeros((CH, 128), F32), unroll=4)
    return own_row(total, square)


def symmetric(x_ref, k_ref, flag):
    bins = x_ref.shape[1]
    k_ref[...] = jnp.swapaxes(x_ref[...], 0, 1)

    def step(k, carry):
        x = k_ref[k]
        t = x.T
        low, high = t[:64], t[64:]
        m = jnp.where(
            flag > 0,
            jnp.concatenate([low, high], axis=1),
            jnp.concatenate([high, low], axis=1),
        )
        k_ref[k] = 0.5 * (x + m)
        return carry

    lax.fori_loop(0, bins, step, 0, unroll=2)
    x_ref[...] = jnp.swapaxes(k_ref[...], 0, 1)


def first_kernel(r_hbm, w_ref, act_ref, stat_ref, taps_out, r_ref, taps_ref, w_s, sem, sem_out):
    cells = pltpu.make_async_copy(r_hbm.at[:, 0:32, :], r_ref, sem)
    cells.start()
    stack_weights(w_ref, w_s, False)
    cells.wait()

    def put(j, v):
        put_taps(taps_ref, j, v)

    collect(r_ref, 0, put)
    out = pltpu.make_async_copy(taps_ref, taps_out, sem_out)
    out.start()

    def emit(j, v, total):
        act_ref[jnp.maximum(j, 0)] = v
        return total + jnp.where(j >= 0, v, 0.0)

    total = convolve(w_s, taps_ref, emit, jnp.zeros((CH, 128), F32))
    stat_ref[...] = own_moments(act_ref, total)
    out.wait()


def sym_kernel(flag_ref, r_hbm, sym_ref, r_ref, x_ref, k_ref, sem):
    cells = pltpu.make_async_copy(r_hbm.at[:, 32:64, :], r_ref, sem)
    cells.start()
    cells.wait()

    def put(j, v):
        x_ref[j] = v[:40]

    collect(r_ref, 0, put)
    symmetric(x_ref, k_ref, flag_ref[0])
    sym_ref[...] = x_ref[...].astype(BF16)


def logit_kernel(flag_ref, raw_hbm, big_ref, x_ref, k_ref, o_ref, sem, sem_out):
    cells = pltpu.make_async_copy(raw_hbm, x_ref, sem)
    cells.start()
    cells.wait()
    symmetric(x_ref, k_ref, flag_ref[0])
    pad = jnp.zeros((WIDE, 128), F32)
    spread(o_ref, 0, lambda j: jnp.concatenate([x_ref[j], pad], axis=0).astype(BF16))
    out = pltpu.make_async_copy(o_ref, big_ref.at[:, 32:64, :], sem_out)
    out.start()
    out.wait()


def second_kernel(act_ref, table_ref, w_ref, out_hbm, stat_ref, taps_hbm, out_ref, taps_ref, w_s, sem_taps, sem_out):
    stack_weights(w_ref, w_s, False)
    mean, inverse = moments(table_ref)

    def step(j, carry):
        put_taps(taps_ref, j, elu((act_ref[j] - mean) * inverse))
        return carry

    lax.fori_loop(0, GRID, step, 0, unroll=2)
    taps_copy = pltpu.make_async_copy(taps_ref, taps_hbm, sem_taps)
    taps_copy.start()
    outs = copies(out_ref, out_hbm, sem_out, ready)

    def emit(j, v, total):
        out_ref[jnp.maximum(j, 0)] = v
        return total + jnp.where(j >= 0, v, 0.0)

    total = convolve(
        w_s, taps_ref, emit, jnp.zeros((CH, 128), F32), after=lambda part: outs[part].start()
    )
    stat_ref[...] = own_moments(out_ref, total)
    taps_copy.wait()
    wait(outs)


def third_kernel(
    act_hbm, table_ref, taps_hbm, sym_ref, head_ref, bias_ref,
    grad_hbm, stat_ref, raw_hbm, term_ref,
    act_ref, mid_ref, grad_ref, raw_ref, sem_act, sem_mid, sem_grad, sem_raw
):
    acts = copies(act_hbm, act_ref, sem_act)
    mids = [
        pltpu.make_async_copy(
            taps_hbm.at[whole(part), 64:128, :], mid_ref.at[whole(part)], sem_mid.at[part]
        )
        for part in range(PARTS)
    ]
    for part in range(PARTS):
        acts[part].start()
        mids[part].start()
    grads = copies(grad_ref, grad_hbm, sem_grad)
    raws = copies(raw_ref, raw_hbm, sem_raw)
    mean, inverse = moments(table_ref)
    head = head_ref[...]
    head_t = head.astype(F32).T.astype(BF16)
    bias = bias_ref[...]

    def step(j, carry):
        first, second, count, term = carry
        normed = (act_ref[j] - mean) * inverse
        summed = normed + mid_ref[j].astype(F32)
        hidden = elu(summed).astype(BF16)
        sym = sym_ref[j]
        raw_ref[j] = dot(head, hidden) + bias
        grad = dot(head_t, sym) * slope(summed)
        grad_ref[j] = grad
        term = term + dot_nt(sym, hidden)
        return first + grad, second + grad * normed, count + sym.astype(F32), term

    zero = jnp.zeros((CH, 128), F32)
    carry = (zero, zero, jnp.zeros((40, 128), F32), jnp.zeros((40, 64), F32))
    for part in range(PARTS):
        acts[part].wait()
        mids[part].wait()
        carry = lax.fori_loop(16 * part, 16 * part + 16, step, carry, unroll=2)
        grads[part].start()
        raws[part].start()
    first, second, count, term = carry
    stat_ref[...] = own_row(first, second)
    count = jnp.broadcast_to(jnp.sum(count, axis=1, keepdims=True), (40, 64))
    term_ref[...] = jnp.concatenate([term, count], axis=1)
    wait(grads, raws)


def store_terms(acc_ref, out_ref):
    acc = acc_ref[...]
    out_ref[0:192] = acc[:, :128]
    out_ref[192:288] = jnp.concatenate([acc[:96, 128:], acc[96:, 128:]], axis=1)


def norm_back(act_ref, moments_, grad_ref, means_, u_ref, utaps_ref, before):
    mean, inverse = moments_
    first_mean, second_mean = means_
    u_ref[0] = jnp.zeros((CH, 128), BF16)
    u_ref[GRID + 1] = jnp.zeros((CH, 128), BF16)

    def step(j, carry):
        normed = (act_ref[j] - mean) * inverse
        u = inverse * (grad_ref[j] - first_mean - normed * second_mean)
        u_ref[j + 1] = u.astype(BF16)
        put_taps(utaps_ref, j, u)
        return carry

    for part in range(PARTS):
        before(part)
        lax.fori_loop(16 * part, 16 * part + 16, step, 0, unroll=2)


def fourth_kernel(
    act_hbm, table_ref, grad_hbm, table3_ref, act1_ref, table1_ref, w_ref,
    out_hbm, stat_ref, u_hbm,
    act_ref, grad_ref, out_ref, u_ref, utaps_ref, w_s, sem_act, sem_grad, sem_out, sem_u
):
    acts = copies(act_hbm, act_ref, sem_act)
    grads = copies(grad_hbm, grad_ref, sem_grad)
    for part in range(PARTS):
        acts[part].start()
        grads[part].start()
    stack_weights(w_ref, w_s, True)

    def before(part):
        acts[part].wait()
        grads[part].wait()

    norm_back(act_ref, moments(table_ref), grad_ref, means(table3_ref), u_ref, utaps_ref, before)
    u_copy = pltpu.make_async_copy(u_ref, u_hbm, sem_u)
    u_copy.start()
    mean1, inverse1 = moments(table1_ref)
    outs = copies(out_ref, out_hbm, sem_out, ready)

    def emit(j, v, carry):
        first, second = carry
        at = jnp.maximum(j, 0)
        normed = (act1_ref[at] - mean1) * inverse1
        grad = jnp.where(j >= 0, v * slope(normed), 0.0)
        out_ref[at] = grad
        return first + grad, second + grad * normed

    zero = jnp.zeros((CH, 128), F32)
    first, second = convolve(
        w_s, utaps_ref, emit, (zero, zero), after=lambda part: outs[part].start()
    )
    stat_ref[...] = own_row(first, second)
    u_copy.wait()
    wait(outs)


def terms_kernel(u_hbm, taps_hbm, term_ref, out_ref, u_ref, taps_ref, acc_ref, sem_u, sem_taps):
    u_copy = pltpu.make_async_copy(u_hbm, u_ref, sem_u)
    u_copy.start()
    taps_copy = pltpu.make_async_copy(taps_hbm, taps_ref, sem_taps)
    taps_copy.start()
    u_copy.wait()
    taps_copy.wait()
    weight_terms(u_ref, taps_ref, acc_ref)
    store_terms(acc_ref, out_ref)
    out_ref[288:328] = term_ref[...]
    out_ref[328:384] = jnp.zeros((56, 128), F32)


def fifth_kernel(
    grad_hbm, table4_ref, act1_ref, table1_ref, taps_hbm, terms_ref,
    part_ref, utaps_hbm,
    grad_ref, taps_ref, utaps_ref, u_ref, acc_ref, buf_ref, sem_grad, sem_taps, sem_out
):
    grads = copies(grad_hbm, grad_ref, sem_grad)
    start(grads)
    taps_copy = pltpu.make_async_copy(taps_hbm, taps_ref, sem_taps)
    taps_copy.start()
    norm_back(
        act1_ref, moments(table1_ref), grad_ref, means(table4_ref), u_ref, utaps_ref,
        lambda part: grads[part].wait(),
    )
    out = pltpu.make_async_copy(utaps_ref, utaps_hbm, sem_out)
    out.start()
    taps_copy.wait()
    weight_terms(u_ref, taps_ref, acc_ref)
    store_terms(acc_ref, buf_ref)
    buf_ref[288:384] = jnp.zeros((96, 128), F32)
    for p in range(3):
        part_ref[:, p, :] = buf_ref[128 * p : 128 * p + 128]
        part_ref[:, 3 + p, :] = terms_ref[128 * p : 128 * p + 128]
    for p in range(6, 8):
        part_ref[:, p, :] = jnp.zeros((128, 128), F32)
    out.wait()


def sixth_kernel(
    utaps_hbm, w_ref, grad_hbm, big_in, big_ref,
    utaps_ref, grad_ref, x_ref, w_s, o_ref, sem_taps, sem_grad, sem_out
):
    taps = copies(utaps_hbm, utaps_ref, sem_taps)
    grads = copies(grad_hbm, grad_ref, sem_grad)
    for part in range(PARTS):
        taps[part].start()
        grads[part].start()
    stack_weights(w_ref, w_s, True)

    def before(part):
        taps[part].wait()
        grads[part].wait()

    def emit(j, v, carry):
        at = jnp.maximum(j, 0)
        x_ref[at] = (v + grad_ref[at]).astype(BF16)
        return carry

    convolve(w_s, utaps_ref, emit, 0, before=before)
    spread(o_ref, 0, lambda j: x_ref[j])
    out = pltpu.make_async_copy(o_ref, big_ref.at[:, 0:32, :], sem_out)
    out.start()
    out.wait()


def share_kernel(r_ref, big_in, big_ref, o_ref, sem):
    def step(k, acc):
        return acc + r_ref[k]

    total = lax.fori_loop(1, DEVICES, step, r_ref[0], unroll=8)
    o_ref[...] = jnp.broadcast_to(total.astype(BF16)[None], o_ref.shape)
    copy = pltpu.make_async_copy(o_ref, big_ref.at[:, 64:72, :], sem)
    copy.start()
    copy.wait()


def call(kernel, outs, ins, scratch=(), sems=(), alias=None, limit=28):
    spaces = {"v": pltpu.VMEM, "s": pltpu.SMEM, "h": pltpu.HBM}
    run = pl.pallas_call(
        kernel,
        out_shape=tuple(
            pltpu.HBM(o[0], o[1]) if len(o) > 2 else jax.ShapeDtypeStruct(o[0], o[1]) for o in outs
        ),
        in_specs=[pl.BlockSpec(memory_space=spaces[k]) for k in ins],
        out_specs=tuple(
            pl.BlockSpec(memory_space=pltpu.HBM if len(o) > 2 else pltpu.VMEM) for o in outs
        ),
        scratch_shapes=[pltpu.VMEM(o[0], o[1]) for o in scratch]
        + [pltpu.SemaphoreType.DMA((n,)) if n else pltpu.SemaphoreType.DMA for n in sems],
        input_output_aliases=alias or {},
        compiler_params=pltpu.CompilerParams(vmem_limit_bytes=limit << 20),
    )

    def placed(*args):
        return run(
            *(
                pltpu.with_memory_space_constraint(x, pltpu.HBM) if k == "h" else x
                for k, x in zip(ins, args)
            )
        )

    return placed


def hbm(form):
    return form + (True,)


def exchange(x):
    return lax.all_to_all(x, ("row", "col"), split_axis=0, concat_axis=0, tiled=True)


FIELD = ((GRID, CH, 128), F32)
HALF = ((GRID, CH, 128), BF16)
TAPS = ((GRID, 192, 128), BF16)
PADDED = ((GRID + 2, CH, 128), BF16)
STAT = ((128, 128), F32)
STACK = ((192, 192), BF16)
ACC = ((192, 192), F32)
PART = ((DEVICES, 8, 128), F32)
TERMS = ((384, 128), F32)
BIG = ((DEVICES, 72, 128), BF16)
PACKED = ((DEVICES, 32, 128), BF16)
PLANES = ((CH, GRID, 128), F32)
BINF = ((GRID, 40, 128), F32)
BINH = ((GRID, 40, 128), BF16)
BINK = ((40, GRID, 128), F32)


def on_device(features, conv_first, conv_second, head_weight, head_bias, cotangent):
    spot = lax.axis_index("row") * COLS + lax.axis_index("col")
    flag = (spot >= FIRST_DIAGONAL).astype(jnp.int32).reshape(1)
    head = jnp.pad(head_weight, ((0, 3), (0, 0)))
    bias = jnp.broadcast_to(jnp.pad(head_bias, (0, 3))[:, None], (40, 128))

    sent = call(pack_kernel, [((DEVICES, 64, 128), BF16)], "vv", [PLANES, BINK])(
        features, cotangent
    )[0]
    cells = exchange(sent)
    act1, stat, taps = call(
        first_kernel, [FIELD, STAT, hbm(TAPS)], "hv", [PACKED, TAPS, STACK], (0, 0)
    )(cells, conv_first)
    table1 = exchange(stat)
    sym = call(sym_kernel, [BINH], "sh", [PACKED, BINF, BINK], (0,))(flag, cells)[0]
    act2, stat, taps2 = call(
        second_kernel, [hbm(FIELD), STAT, hbm(TAPS)], "vvv", [FIELD, TAPS, STACK], (0, PARTS)
    )(act1, table1, conv_second)
    table2 = exchange(stat)
    table2, sym = lax.optimization_barrier((table2, sym))
    grad, stat, raw, term = call(
        third_kernel,
        [hbm(FIELD), STAT, hbm(BINF), ((40, 128), F32)],
        "hvhvvv",
        [FIELD, HALF, FIELD, BINF],
        (PARTS,) * 4,
    )(act2, table2, taps, sym, head, bias)
    table3 = exchange(stat)
    big = call(logit_kernel, [hbm(BIG)], "sh", [BINF, BINK, PACKED], (0, 0))(flag, raw)[0]
    table3, big = lax.optimization_barrier((table3, big))
    grad1, stat, u2 = call(
        fourth_kernel,
        [hbm(FIELD), STAT, hbm(PADDED)],
        "hvhvvvv",
        [FIELD, FIELD, FIELD, PADDED, TAPS, STACK],
        (PARTS, PARTS, PARTS, 0),
    )(act2, table2, grad, table3, act1, table1, conv_second)
    table4 = exchange(stat)
    terms2 = call(terms_kernel, [TERMS], "hhv", [PADDED, TAPS, ACC], (0, 0))(u2, taps2, term)[0]
    table4, terms2 = lax.optimization_barrier((table4, terms2))
    part, utaps = call(
        fifth_kernel,
        [PART, hbm(TAPS)],
        "hvvvhv",
        [FIELD, TAPS, TAPS, PADDED, ACC, TERMS],
        (PARTS, 0, 0),
    )(grad1, table4, act1, table1, taps, terms2)
    got = exchange(part)
    big = call(
        sixth_kernel,
        [hbm(BIG)],
        "hvhh",
        [TAPS, FIELD, HALF, STACK, PACKED],
        (PARTS, PARTS, 0),
        {3: 0},
    )(utaps, conv_first, grad, big)[0]
    big = call(share_kernel, [hbm(BIG)], "vh", [((DEVICES, 8, 128), BF16)], (0,), {1: 0})(got, big)[0]
    result = exchange(big)
    input_grad, logits, first, second, head_grad, bias_grad = call(
        last_kernel,
        [
            ((CH, GRID, 128), BF16),
            ((BINS, GRID, 128), BF16),
            ((9, CH, CH), F32),
            ((9, CH, CH), F32),
            ((BINS, CH), F32),
            ((1, BINS), F32),
        ],
        "v",
        [PLANES, BINK],
    )(result)
    return logits, input_grad, first, second, head_grad, bias_grad.reshape(BINS)


def solution(mesh):
    placed = (P(None, "col", "row"), P(), P(), P(), P(), P(None, "col", "row"))
    return jax.shard_map(
        on_device,
        mesh=mesh,
        in_specs=placed,
        out_specs=(P(None, "col", "row"), P(None, "col", "row"), P(), P(), P(), P()),
        check_vma=False,
    )
```

time: 318 us -> 236 us (0.74)
  waiting for transfers between devices: 88.7 us -> 7.12 us
  blocking collectives: 45.8 us -> 97.5 us
  starting transfers between devices: 47.7 us -> 28.9 us
  local copies, waits for them, and re-layouts: 17.9 us -> 2.39 us
  Pallas kernels: 112 us -> 99 us
  other arithmetic: 3.61 us -> 0 us
    all_to_all x7 -> x4, waiting for transfers between devices: 88.7 us -> 7.12 us  [exchange(): lax.all_to_all(x, ('row', 'col'), split_axis=0, concat_axis=0, tiled=True)]
    all_to_all x3, blocking collectives: 45.8 us -> 97.5 us  [exchange(): lax.all_to_all(x, ('row', 'col'), split_axis=0, concat_axis=0, tiled=True)]
    all_to_all x7 -> x4, starting transfers between devices: 47.7 us -> 28.9 us  [exchange(): lax.all_to_all(x, ('row', 'col'), split_axis=0, concat_axis=0, tiled=True)]
    pallas_call x12, Pallas kernels: 112 us -> 99 us  [placed(): run(*(pltpu.with_memory_space_constraint(x, pltpu.HBM) if k == 'h' else x...]
    unnamed x22 -> x12, local copies, waits for them, and re-layouts: 8.96 us -> 2.3 us
    slice x5 -> x0, local copies, waits for them, and re-layouts: 3.73 us -> none  [the longest x1 1.74 us: on_device(): input_grad = unpacked(result[:, :32])[0].transpose(1, 0, 2)]
  transfers between devices with their start and end apart: 7 -> 4, of which waited for: 6 -> 4; matrix products, arithmetic and copies ran while one was open for 2% -> 0% of each run, Pallas kernels for 10% -> 15%
where the time goes in v3:
time: 236 us
  Pallas kernels  99 us (42%)
  blocking collectives  97.5 us (41%)
  starting transfers between devices  28.9 us (12%)
  waiting for transfers between devices  7.12 us (3%)
  local copies, waits for them, and re-layouts  2.39 us (1%)
    pallas_call x12, Pallas kernels, placed(): run(*(pltpu.with_memory_space_constraint(x, pltpu.HBM) if k == 'h' else x...  99 us
    all_to_all x3, blocking collectives, exchange(): lax.all_to_all(x, ('row', 'col'), split_axis=0, concat_axis=0, tiled=True)  97.5 us
    all_to_all x4, starting transfers between devices, exchange(): lax.all_to_all(x, ('row', 'col'), split_axis=0, concat_axis=0, tiled=True)  28.9 us
    all_to_all x4, waiting for transfers between devices, exchange(): lax.all_to_all(x, ('row', 'col'), split_axis=0, concat_axis=0, tiled=True)  7.12 us
  transfers between devices with their start and end apart: 4, of which 4 were waited for; matrix products, arithmetic and copies ran while one was open for 0% of the time, Pallas kernels for 15%

profile of v3, /device:TPU:1, one launch (start us, length us, event | category | flops | bytes accessed | tf_op | source)
XLA Modules:
  0.0 235.7 jit_solution(362165904562102985)
XLA Ops:
  0.6 0.0 copy-start
  0.6 1.2 copy-done
  1.9 1.1 copy-done.1
  2.9 3.8 %shard_map.109 = bf16[128,64,128]{2,1,0:T(8,128)(2,1)S(1)} custom-call(bf16[64,64,128]{2,1,0:T(8,128)(2,1)S(1)} %copy-done, bf16[37,64,128]{2,1,0:T(8,128)(2,1)S(1)} %copy-done.1), custom_call_target="tpu_custom_call" | custom-call | tf_op jit(solution)/shard_map/pallas_call | solution.py:610
  6.8 0.0 copy-start.3
  6.8 41.5 %all_to_all.62.r_hbm = bf16[128,64,128]{2,1,0:T(8,128)(2,1)} all-to-all(bf16[128,64,128]{2,1,0:T(8,128)(2,1)S(1)} %shard_map.109), channel_id=1, replica_groups=mesh['row'=8,'col'=16] {'row','col'}, dimensions={0} | all-to-all | bytes 4194304 | tf_op jit(solution)/shard_map/all_to_all | solution.py:625
  48.3 0.0 copy-done.3
  48.3 11.7 %shard_map.110 = (f32[64,64,128]{2,1,0:T(8,128)S(1)}, f32[128,128]{1,0:T(8,128)S(1)}, bf16[64,192,128]{2,1,0:T(8,128)(2,1)}) custom-call(bf16[128,64,128]{2,1,0:T(8,128)(2,1)} %all_to_all.62.r_hbm, bf16[9,64,64]{2,1,0:T(8,128)(2,1)S(1)} %copy-done.3), custom_call_target="tpu_custom_call" | custom-call | tf_op jit(solution)/shard_map/pallas_call | solution.py:610
  60.0 15.5 %all_to_all.63 = f32[128,1,128]{2,1,0:T(1,128)S(1)} all-to-all(f32[128,1,128]{2,1,0:T(1,128)S(1)} %bitcast.25), channel_id=1, replica_groups=mesh['row'=8,'col'=16] {'row','col'}, dimensions={0} | all-to-all | bytes 131072 | tf_op jit(solution)/shard_map/all_to_all | solution.py:625
  75.6 0.0 copy-done.2
  75.6 10.6 %shard_map.111 = (f32[64,64,128]{2,1,0:T(8,128)}, f32[128,128]{1,0:T(8,128)}, bf16[64,192,128]{2,1,0:T(8,128)(2,1)}) custom-call(f32[64,64,128]{2,1,0:T(8,128)S(1)} %get-tuple-element.33.act_ref.act1_ref, f32[128,128]{1,0:T(8,128)S(1)} %bitcast.18, bf16[9,64,64]{2,1,0:T(8,128)(2,1)S(1)} %copy-done.2), custom_call_target="tpu_custom_call" | custom-call | tf_op jit(solution)/shard_map/pallas_call | solution.py:610
  86.1 4.4 %all-to-all-start.2 = ((f32[128,1,128]{2,1,0:T(1,128)}), f32[128,1,128]{2,1,0:T(1,128)S(1)}, u32[]{:S(2)}, u32[]{:S(2)}) async-start(f32[128,1,128]{2,1,0:T(1,128)} %bitcast.4), calls=%async_computation.2 | async-start | bytes 131072 | tf_op jit(solution)/shard_map/all_to_all | solution.py:625
  90.6 0.0 copy-done.5
  90.6 0.0 copy-done.4
  90.6 8.2 %shard_map.112.sym_ref = bf16[64,40,128]{2,1,0:T(8,128)(2,1)S(1)} custom-call(s32[1]{0:T(128)} %bitcast.6.flag_ref, bf16[128,64,128]{2,1,0:T(8,128)(2,1)} %all_to_all.62.r_hbm), custom_call_target="tpu_custom_call" | custom-call | tf_op jit(solution)/shard_map/pallas_call | solution.py:610
  98.8 1.2 all-to-all-done.2
  100.1 0.1 broadcast_in_dim.2.bias_ref
  100.1 9.3 %shard_map.113 = (f32[64,64,128]{2,1,0:T(8,128)}, f32[128,128]{1,0:T(8,128)}, f32[64,40,128]{2,1,0:T(8,128)}, f32[40,128]{1,0:T(8,128)S(1)}) custom-call(f32[64,64,128]{2,1,0:T(8,128)} %get-tuple-element.35.act_hbm, f32[128,128]{1,0:T(8,128)S(1)} %bitcast.21, bf16[64,192,128]{2,1,0:T(8,128)(2,1)} %get-tuple-element.38.taps_hbm, ...), custom_call_target="tpu_custom_call" | custom-call | tf_op jit(solution)/shard_map/pallas_call | solution.py:610
  109.4 8.5 %all-to-all-start.3 = ((f32[128,1,128]{2,1,0:T(1,128)}), f32[128,1,128]{2,1,0:T(1,128)S(1)}, u32[]{:S(2)}, u32[]{:S(2)}) async-start(f32[128,1,128]{2,1,0:T(1,128)} %bitcast.8), calls=%async_computation.3 | async-start | bytes 131072 | tf_op jit(solution)/shard_map/all_to_all | solution.py:625
  118.0 9.4 %shard_map.114.big_in = bf16[128,72,128]{2,1,0:T(8,128)(2,1)} custom-call(s32[1]{0:T(128)} %bitcast.6.flag_ref, f32[64,40,128]{2,1,0:T(8,128)} %get-tuple-element.42.raw_hbm), custom_call_target="tpu_custom_call" | custom-call | tf_op jit(solution)/shard_map/pallas_call | solution.py:610
  127.4 0.1 all-to-all-done.3
  127.5 12.4 %shard_map.115 = (f32[64,64,128]{2,1,0:T(8,128)}, f32[128,128]{1,0:T(8,128)}, bf16[66,64,128]{2,1,0:T(8,128)(2,1)}) custom-call(f32[64,64,128]{2,1,0:T(8,128)} %get-tuple-element.35.act_hbm, f32[128,128]{1,0:T(8,128)S(1)} %bitcast.22, f32[64,64,128]{2,1,0:T(8,128)} %get-tuple-element.40.grad_hbm, f32[128,128]{1,0:T(8,128)S(1)} %bitcast.24, ...), custom_call_target="tpu_custom_call" | custom-call | tf_op jit(solution)/shard_map/pallas_call | solution.py:610
  140.0 9.7 %all-to-all-start.4 = ((f32[128,1,128]{2,1,0:T(1,128)}), f32[128,1,128]{2,1,0:T(1,128)S(1)}, u32[]{:S(2)}, u32[]{:S(2)}) async-start(f32[128,1,128]{2,1,0:T(1,128)} %bitcast.11), calls=%async_computation.4 | async-start | bytes 131072 | tf_op jit(solution)/shard_map/all_to_all | solution.py:625
  149.6 6.0 %shard_map.116.terms_ref = f32[384,128]{1,0:T(8,128)S(1)} custom-call(bf16[66,64,128]{2,1,0:T(8,128)(2,1)} %get-tuple-element.46.u_hbm, bf16[64,192,128]{2,1,0:T(8,128)(2,1)} %get-tuple-element.47.taps_hbm, f32[40,128]{1,0:T(8,128)S(1)} %get-tuple-element.48.term_ref), custom_call_target="tpu_custom_call" | custom-call | tf_op jit(solution)/shard_map/pallas_call | solution.py:610
  155.7 3.5 %all-to-all-done.4 = f32[128,1,128]{2,1,0:T(1,128)S(1)} async-done(((f32[128,1,128]{2,1,0:T(1,128)}), f32[128,1,128]{2,1,0:T(1,128)S(1)}, u32[]{:S(2)}, u32[]{:S(2)}) %all-to-all-start.4) | async-done | bytes 65568 | tf_op jit(solution)/shard_map/all_to_all | solution.py:625
  159.2 9.9 %shard_map.117 = (f32[128,8,128]{2,1,0:T(8,128)}, bf16[64,192,128]{2,1,0:T(8,128)(2,1)}) custom-call(f32[64,64,128]{2,1,0:T(8,128)} %get-tuple-element.44.grad_hbm, f32[128,128]{1,0:T(8,128)S(1)} %bitcast.23, f32[64,64,128]{2,1,0:T(8,128)S(1)} %get-tuple-element.33.act_ref.act1_ref, f32[128,128]{1,0:T(8,128)S(1)} %bitcast.20, ...), custom_call_target="tpu_custom_call" | custom-call | tf_op jit(solution)/shard_map/pallas_call | solution.py:610
  169.1 6.3 %all-to-all-start.5 = ((f32[128,8,128]{2,1,0:T(8,128)}), f32[128,8,128]{2,1,0:T(8,128)S(1)}, u32[]{:S(2)}, u32[]{:S(2)}) async-start(f32[128,8,128]{2,1,0:T(8,128)} %get-tuple-element.51), calls=%async_computation.5 | async-start | bytes 1048576 | tf_op jit(solution)/shard_map/all_to_all | solution.py:625
  175.4 11.3 %shard_map.118.big_in = bf16[128,72,128]{2,1,0:T(8,128)(2,1)} custom-call(bf16[64,192,128]{2,1,0:T(8,128)(2,1)} %get-tuple-element.52.utaps_hbm, bf16[9,64,64]{2,1,0:T(8,128)(2,1)S(1)} %copy-done.3, f32[64,64,128]{2,1,0:T(8,128)} %get-tuple-element.40.grad_hbm, bf16[128,72,128]{2,1,0:T(8,128)(2,1)} %shard_map.114.big_in), custom_call_target="tpu_custom_call", output_to_operand_aliasing={{}: (3, {})} | custom-call | tf_op jit(solution)/shard_map/pallas_call | solution.py:610
  186.7 2.3 all-to-all-done.5.r_ref
  189.0 0.9 shard_map.119
  189.9 40.4 %all_to_all.64.r_ref = bf16[128,72,128]{2,1,0:T(8,128)(2,1)S(1)} all-to-all(bf16[128,72,128]{2,1,0:T(8,128)(2,1)} %shard_map.119), channel_id=1, replica_groups=mesh['row'=8,'col'=16] {'row','col'}, dimensions={0} | all-to-all | bytes 4718592 | tf_op jit(solution)/shard_map/all_to_all | solution.py:625
  230.3 5.4 %shard_map.120 = (bf16[64,64,128]{2,1,0:T(8,128)(2,1)}, bf16[37,64,128]{2,1,0:T(8,128)(2,1)}, f32[9,64,64]{2,1,0:T(8,128)}, f32[9,64,64]{2,1,0:T(8,128)}, f32[37,64]{1,0:T(8,128)}, /*index=5*/f32[1,37]{1,0:T(1,128)}) custom-call(bf16[128,72,128]{2,1,0:T(8,128)(2,1)S(1)} %all_to_all.64.r_ref), custom_call_target="tpu_custom_call" | custom-call | tf_op jit(solution)/shard_map/pallas_call | solution.py:610
  (6 shorter events, 0.0 us)
Async XLA Ops:
  0.6 1.2 copy-start
  1.9 1.1 copy-start.1
  6.8 41.5 %copy-start.3 = (bf16[9,64,64]{2,1,0:T(8,128)(2,1)S(1)}, bf16[9,64,64]{2,1,0:T(8,128)(2,1)}, u32[]{:S(2)}) copy-start(bf16[9,64,64]{2,1,0:T(8,128)(2,1)} %w_ref.7) | copy-start | bytes 221188
  48.3 27.3 %copy-start.2 = (bf16[9,64,64]{2,1,0:T(8,128)(2,1)S(1)}, bf16[9,64,64]{2,1,0:T(8,128)(2,1)}, u32[]{:S(2)}) copy-start(bf16[9,64,64]{2,1,0:T(8,128)(2,1)} %w_ref.6) | copy-start | bytes 221188
  48.3 42.3 %copy-start.5 = (f32[37]{0:T(128)S(1)}, f32[37]{0:T(128)}, u32[]{:S(2)}) copy-start(f32[37]{0:T(128)} %param.10) | copy-start | bytes 448
  48.3 42.3 %copy-start.4 = (bf16[37,64]{1,0:T(8,128)(2,1)S(1)}, bf16[37,64]{1,0:T(8,128)(2,1)}, u32[]{:S(2)}) copy-start(bf16[37,64]{1,0:T(8,128)(2,1)} %param.9) | copy-start | bytes 14212
  86.1 13.9 %all-to-all-start.2 = ((f32[128,1,128]{2,1,0:T(1,128)}), f32[128,1,128]{2,1,0:T(1,128)S(1)}, u32[]{:S(2)}, u32[]{:S(2)}) async-start(f32[128,1,128]{2,1,0:T(1,128)} %bitcast.4), calls=%async_computation.2 | async-start | bytes 131072 | tf_op jit(solution)/shard_map/all_to_all | solution.py:625
  109.4 18.1 %all-to-all-start.3 = ((f32[128,1,128]{2,1,0:T(1,128)}), f32[128,1,128]{2,1,0:T(1,128)S(1)}, u32[]{:S(2)}, u32[]{:S(2)}) async-start(f32[128,1,128]{2,1,0:T(1,128)} %bitcast.8), calls=%async_computation.3 | async-start | bytes 131072 | tf_op jit(solution)/shard_map/all_to_all | solution.py:625
  140.0 19.2 %all-to-all-start.4 = ((f32[128,1,128]{2,1,0:T(1,128)}), f32[128,1,128]{2,1,0:T(1,128)S(1)}, u32[]{:S(2)}, u32[]{:S(2)}) async-start(f32[128,1,128]{2,1,0:T(1,128)} %bitcast.11), calls=%async_computation.4 | async-start | bytes 131072 | tf_op jit(solution)/shard_map/all_to_all | solution.py:625
  169.1 19.8 %all-to-all-start.5 = ((f32[128,8,128]{2,1,0:T(8,128)}), f32[128,8,128]{2,1,0:T(8,128)S(1)}, u32[]{:S(2)}, u32[]{:S(2)}) async-start(f32[128,8,128]{2,1,0:T(8,128)} %get-tuple-element.51), calls=%async_computation.5 | async-start | bytes 1048576 | tf_op jit(solution)/shard_map/all_to_all | solution.py:625

commit v4 on v3

--- a/solution.py
+++ b/solution.py
@@ -158,7 +158,7 @@
             put(4 * col + 2 * h + 1, t[64:])
         return carry
 
-    lax.fori_loop(0, COLS, step, 0)
+    lax.fori_loop(0, COLS, step, 0, unroll=8)
 
 
 def spread(o_ref, first, get):
@@ -176,7 +176,7 @@
                 o_ref[r * COLS + col, first + 16 * slot : first + 16 * slot + 16, :] = tile.astype(BF16)
         return carry
 
-    lax.fori_loop(0, COLS, step, 0)
+    lax.fori_loop(0, COLS, step, 0, unroll=8)
 
 
 def put_taps(dst_ref, at, v):
@@ -215,7 +215,7 @@
     for part in range(PARTS):
         if before is not None:
             before(part)
-        carry = lax.fori_loop(8 * part, 8 * part + 8, step, carry)
+        carry = lax.fori_loop(8 * part, 8 * part + 8, step, carry, unroll=8)
         if part == PARTS - 1:
             one, two, state = carry
             state = emit(GRID - 1, one, state)
@@ -266,7 +266,7 @@
         acc_ref[...] += dot_nt(jnp.concatenate(lhs, axis=1), jnp.concatenate(rhs, axis=1))
         return carry
 
-    lax.fori_loop(0, GRID // 4, step, 0)
+    lax.fori_loop(0, GRID // 4, step, 0, unroll=8)
 
 
 def own_row(first, second):
@@ -303,7 +303,7 @@
         off = act_ref[j] - mean
         return acc + off * off
 
-    square = lax.fori_loop(0, GRID, step, jnp.zeros((CH, 128), F32), unroll=4)
+    square = lax.fori_loop(0, GRID, step, jnp.zeros((CH, 128), F32), unroll=8)
     return own_row(total, square)
 
 
@@ -323,7 +323,7 @@
         k_ref[k] = 0.5 * (x + m)
         return carry
 
-    lax.fori_loop(0, bins, step, 0, unroll=2)
+    lax.fori_loop(0, bins, step, 0, unroll=8)
     x_ref[...] = jnp.swapaxes(k_ref[...], 0, 1)
 
 
@@ -382,7 +382,7 @@
         put_taps(taps_ref, j, elu((act_ref[j] - mean) * inverse))
         return carry
 
-    lax.fori_loop(0, GRID, step, 0, unroll=2)
+    lax.fori_loop(0, GRID, step, 0, unroll=8)
     taps_copy = pltpu.make_async_copy(taps_ref, taps_hbm, sem_taps)
     taps_copy.start()
     outs = copies(out_ref, out_hbm, sem_out, ready)
@@ -421,24 +421,33 @@
     head_t = head.astype(F32).T.astype(BF16)
     bias = bias_ref[...]
 
-    def step(j, carry):
+    wide = jnp.concatenate([bias, bias], axis=1)
+
+    def step(t, carry):
         first, second, count, term = carry
-        normed = (act_ref[j] - mean) * inverse
-        summed = normed + mid_ref[j].astype(F32)
-        hidden = elu(summed).astype(BF16)
-        sym = sym_ref[j]
-        raw_ref[j] = dot(head, hidden) + bias
-        grad = dot(head_t, sym) * slope(summed)
-        grad_ref[j] = grad
+        pair = (2 * t, 2 * t + 1)
+        normed = [(act_ref[j] - mean) * inverse for j in pair]
+        summed = [n + mid_ref[j].astype(F32) for n, j in zip(normed, pair)]
+        hidden = jnp.concatenate([elu(x).astype(BF16) for x in summed], axis=1)
+        sym = jnp.concatenate([sym_ref[j] for j in pair], axis=1)
+        raw = dot(head, hidden) + wide
+        back = dot(head_t, sym)
         term = term + dot_nt(sym, hidden)
-        return first + grad, second + grad * normed, count + sym.astype(F32), term
+        for k, j in enumerate(pair):
+            raw_ref[j] = raw[:, 128 * k : 128 * k + 128]
+            grad = back[:, 128 * k : 128 * k + 128] * slope(summed[k])
+            grad_ref[j] = grad
+            first = first + grad
+            second = second + grad * normed[k]
+            count = count + sym_ref[j].astype(F32)
+        return first, second, count, term
 
     zero = jnp.zeros((CH, 128), F32)
     carry = (zero, zero, jnp.zeros((40, 128), F32), jnp.zeros((40, 64), F32))
     for part in range(PARTS):
         acts[part].wait()
         mids[part].wait()
-        carry = lax.fori_loop(16 * part, 16 * part + 16, step, carry, unroll=2)
+        carry = lax.fori_loop(8 * part, 8 * part + 8, step, carry, unroll=8)
         grads[part].start()
         raws[part].start()
     first, second, count, term = carry
@@ -469,7 +478,7 @@
 
     for part in range(PARTS):
         before(part)
-        lax.fori_loop(16 * part, 16 * part + 16, step, 0, unroll=2)
+        lax.fori_loop(16 * part, 16 * part + 16, step, 0, unroll=8)
 
 
 def fourth_kernel(

time: 236 us -> 195 us (0.83)
  Pallas kernels: 99 us -> 53.9 us
  waiting for transfers between devices: 7.12 us -> 23 us
  starting transfers between devices: 28.9 us -> 19.6 us
  blocking collectives: 97.5 us -> 94.6 us
    pallas_call x12, Pallas kernels: 99 us -> 53.9 us  [placed(): run(*(pltpu.with_memory_space_constraint(x, pltpu.HBM) if k == 'h' else x...]
    all_to_all x4, waiting for transfers between devices: 7.12 us -> 23 us  [exchange(): lax.all_to_all(x, ('row', 'col'), split_axis=0, concat_axis=0, tiled=True)]
    all_to_all x4, starting transfers between devices: 28.9 us -> 19.6 us  [exchange(): lax.all_to_all(x, ('row', 'col'), split_axis=0, concat_axis=0, tiled=True)]
    all_to_all x3, blocking collectives: 97.5 us -> 94.6 us  [exchange(): lax.all_to_all(x, ('row', 'col'), split_axis=0, concat_axis=0, tiled=True)]
  transfers between devices with their start and end apart: 4 -> 4, of which waited for: 4 -> 4; matrix products, arithmetic and copies ran while one was open for 0% -> 0% of each run, Pallas kernels for 15% -> 10%
where the time goes in v4:
time: 195 us; the launch traced here: 194 us
  blocking collectives  94.6 us (49%)
  Pallas kernels  53.9 us (28%)
  waiting for transfers between devices  23 us (12%)
  starting transfers between devices  19.6 us (10%)
  local copies, waits for them, and re-layouts  2.39 us (1%)
    all_to_all x3, blocking collectives, exchange(): lax.all_to_all(x, ('row', 'col'), split_axis=0, concat_axis=0, tiled=True)  94.6 us
    pallas_call x12, Pallas kernels, placed(): run(*(pltpu.with_memory_space_constraint(x, pltpu.HBM) if k == 'h' else x...  53.9 us
    all_to_all x4, waiting for transfers between devices, exchange(): lax.all_to_all(x, ('row', 'col'), split_axis=0, concat_axis=0, tiled=True)  23 us
    all_to_all x4, starting transfers between devices, exchange(): lax.all_to_all(x, ('row', 'col'), split_axis=0, concat_axis=0, tiled=True)  19.6 us
  transfers between devices with their start and end apart: 4, of which 4 were waited for; matrix products, arithmetic and copies ran while one was open for 0% of the time, Pallas kernels for 10%

profile of v4, /device:TPU:1, one launch (start us, length us, event | category | flops | bytes accessed | tf_op | source)
XLA Modules:
  0.0 194.2 jit_solution(3218758669255136299)
XLA Ops:
  0.6 0.0 copy-start
  0.6 1.2 copy-done
  1.9 1.1 copy-done.1
  2.9 3.8 %shard_map.109 = bf16[128,64,128]{2,1,0:T(8,128)(2,1)S(1)} custom-call(bf16[64,64,128]{2,1,0:T(8,128)(2,1)S(1)} %copy-done, bf16[37,64,128]{2,1,0:T(8,128)(2,1)S(1)} %copy-done.1), custom_call_target="tpu_custom_call" | custom-call | tf_op jit(solution)/shard_map/pallas_call | solution.py:619
  6.8 0.0 copy-start.3
  6.8 41.5 %all_to_all.62.r_hbm = bf16[128,64,128]{2,1,0:T(8,128)(2,1)} all-to-all(bf16[128,64,128]{2,1,0:T(8,128)(2,1)S(1)} %shard_map.109), channel_id=1, replica_groups=mesh['row'=8,'col'=16] {'row','col'}, dimensions={0} | all-to-all | bytes 4194304 | tf_op jit(solution)/shard_map/all_to_all | solution.py:634
  48.3 0.0 copy-done.3
  48.3 4.1 %shard_map.110 = (f32[64,64,128]{2,1,0:T(8,128)S(1)}, f32[128,128]{1,0:T(8,128)S(1)}, bf16[64,192,128]{2,1,0:T(8,128)(2,1)}) custom-call(bf16[128,64,128]{2,1,0:T(8,128)(2,1)} %all_to_all.62.r_hbm, bf16[9,64,64]{2,1,0:T(8,128)(2,1)S(1)} %copy-done.3), custom_call_target="tpu_custom_call" | custom-call | tf_op jit(solution)/shard_map/pallas_call | solution.py:619
  52.4 15.5 %all_to_all.63 = f32[128,1,128]{2,1,0:T(1,128)S(1)} all-to-all(f32[128,1,128]{2,1,0:T(1,128)S(1)} %bitcast.25), channel_id=1, replica_groups=mesh['row'=8,'col'=16] {'row','col'}, dimensions={0} | all-to-all | bytes 131072 | tf_op jit(solution)/shard_map/all_to_all | solution.py:634
  67.9 0.0 copy-done.2
  67.9 4.4 %shard_map.111 = (f32[64,64,128]{2,1,0:T(8,128)}, f32[128,128]{1,0:T(8,128)}, bf16[64,192,128]{2,1,0:T(8,128)(2,1)}) custom-call(f32[64,64,128]{2,1,0:T(8,128)S(1)} %get-tuple-element.33.act_ref.act1_ref, f32[128,128]{1,0:T(8,128)S(1)} %bitcast.18, bf16[9,64,64]{2,1,0:T(8,128)(2,1)S(1)} %copy-done.2), custom_call_target="tpu_custom_call" | custom-call | tf_op jit(solution)/shard_map/pallas_call | solution.py:619
  72.4 4.4 %all-to-all-start.2 = ((f32[128,1,128]{2,1,0:T(1,128)}), f32[128,1,128]{2,1,0:T(1,128)S(1)}, u32[]{:S(2)}, u32[]{:S(2)}) async-start(f32[128,1,128]{2,1,0:T(1,128)} %bitcast.4), calls=%async_computation.2 | async-start | bytes 131072 | tf_op jit(solution)/shard_map/all_to_all | solution.py:634
  76.8 0.0 copy-done.5
  76.8 0.0 copy-done.4
  76.8 4.6 %shard_map.112.sym_ref = bf16[64,40,128]{2,1,0:T(8,128)(2,1)S(1)} custom-call(s32[1]{0:T(128)} %bitcast.6.flag_ref, bf16[128,64,128]{2,1,0:T(8,128)(2,1)} %all_to_all.62.r_hbm), custom_call_target="tpu_custom_call" | custom-call | tf_op jit(solution)/shard_map/pallas_call | solution.py:619
  81.5 4.8 %all-to-all-done.2 = f32[128,1,128]{2,1,0:T(1,128)S(1)} async-done(((f32[128,1,128]{2,1,0:T(1,128)}), f32[128,1,128]{2,1,0:T(1,128)S(1)}, u32[]{:S(2)}, u32[]{:S(2)}) %all-to-all-start.2) | async-done | bytes 65568 | tf_op jit(solution)/shard_map/all_to_all | solution.py:634
  86.3 0.1 broadcast_in_dim.2.bias_ref
  86.4 4.6 %shard_map.113 = (f32[64,64,128]{2,1,0:T(8,128)}, f32[128,128]{1,0:T(8,128)}, f32[64,40,128]{2,1,0:T(8,128)}, f32[40,128]{1,0:T(8,128)S(1)}) custom-call(f32[64,64,128]{2,1,0:T(8,128)} %get-tuple-element.35.act_hbm, f32[128,128]{1,0:T(8,128)S(1)} %bitcast.21, bf16[64,192,128]{2,1,0:T(8,128)(2,1)} %get-tuple-element.38.taps_hbm, ...), custom_call_target="tpu_custom_call" | custom-call | tf_op jit(solution)/shard_map/pallas_call | solution.py:619
  91.0 4.9 %all-to-all-start.3 = ((f32[128,1,128]{2,1,0:T(1,128)}), f32[128,1,128]{2,1,0:T(1,128)S(1)}, u32[]{:S(2)}, u32[]{:S(2)}) async-start(f32[128,1,128]{2,1,0:T(1,128)} %bitcast.8), calls=%async_computation.3 | async-start | bytes 131072 | tf_op jit(solution)/shard_map/all_to_all | solution.py:634
  95.9 5.6 %shard_map.114.big_in = bf16[128,72,128]{2,1,0:T(8,128)(2,1)} custom-call(s32[1]{0:T(128)} %bitcast.6.flag_ref, f32[64,40,128]{2,1,0:T(8,128)} %get-tuple-element.42.raw_hbm), custom_call_target="tpu_custom_call" | custom-call | tf_op jit(solution)/shard_map/pallas_call | solution.py:619
  101.5 3.9 %all-to-all-done.3 = f32[128,1,128]{2,1,0:T(1,128)S(1)} async-done(((f32[128,1,128]{2,1,0:T(1,128)}), f32[128,1,128]{2,1,0:T(1,128)S(1)}, u32[]{:S(2)}, u32[]{:S(2)}) %all-to-all-start.3) | async-done | bytes 65568 | tf_op jit(solution)/shard_map/all_to_all | solution.py:634
  105.4 5.7 %shard_map.115 = (f32[64,64,128]{2,1,0:T(8,128)}, f32[128,128]{1,0:T(8,128)}, bf16[66,64,128]{2,1,0:T(8,128)(2,1)}) custom-call(f32[64,64,128]{2,1,0:T(8,128)} %get-tuple-element.35.act_hbm, f32[128,128]{1,0:T(8,128)S(1)} %bitcast.22, f32[64,64,128]{2,1,0:T(8,128)} %get-tuple-element.40.grad_hbm, f32[128,128]{1,0:T(8,128)S(1)} %bitcast.24, ...), custom_call_target="tpu_custom_call" | custom-call | tf_op jit(solution)/shard_map/pallas_call | solution.py:619
  111.2 5.9 %all-to-all-start.4 = ((f32[128,1,128]{2,1,0:T(1,128)}), f32[128,1,128]{2,1,0:T(1,128)S(1)}, u32[]{:S(2)}, u32[]{:S(2)}) async-start(f32[128,1,128]{2,1,0:T(1,128)} %bitcast.11), calls=%async_computation.4 | async-start | bytes 131072 | tf_op jit(solution)/shard_map/all_to_all | solution.py:634
  117.0 3.6 %shard_map.116.terms_ref = f32[384,128]{1,0:T(8,128)S(1)} custom-call(bf16[66,64,128]{2,1,0:T(8,128)(2,1)} %get-tuple-element.46.u_hbm, bf16[64,192,128]{2,1,0:T(8,128)(2,1)} %get-tuple-element.47.taps_hbm, f32[40,128]{1,0:T(8,128)S(1)} %get-tuple-element.48.term_ref), custom_call_target="tpu_custom_call" | custom-call | tf_op jit(solution)/shard_map/pallas_call | solution.py:619
  120.7 5.9 %all-to-all-done.4 = f32[128,1,128]{2,1,0:T(1,128)S(1)} async-done(((f32[128,1,128]{2,1,0:T(1,128)}), f32[128,1,128]{2,1,0:T(1,128)S(1)}, u32[]{:S(2)}, u32[]{:S(2)}) %all-to-all-start.4) | async-done | bytes 65568 | tf_op jit(solution)/shard_map/all_to_all | solution.py:634
  126.6 5.9 %shard_map.117 = (f32[128,8,128]{2,1,0:T(8,128)}, bf16[64,192,128]{2,1,0:T(8,128)(2,1)}) custom-call(f32[64,64,128]{2,1,0:T(8,128)} %get-tuple-element.44.grad_hbm, f32[128,128]{1,0:T(8,128)S(1)} %bitcast.23, f32[64,64,128]{2,1,0:T(8,128)S(1)} %get-tuple-element.33.act_ref.act1_ref, f32[128,128]{1,0:T(8,128)S(1)} %bitcast.20, ...), custom_call_target="tpu_custom_call" | custom-call | tf_op jit(solution)/shard_map/pallas_call | solution.py:619
  132.4 4.4 %all-to-all-start.5 = ((f32[128,8,128]{2,1,0:T(8,128)}), f32[128,8,128]{2,1,0:T(8,128)S(1)}, u32[]{:S(2)}, u32[]{:S(2)}) async-start(f32[128,8,128]{2,1,0:T(8,128)} %get-tuple-element.51), calls=%async_computation.5 | async-start | bytes 1048576 | tf_op jit(solution)/shard_map/all_to_all | solution.py:634
  136.8 5.2 %shard_map.118.big_in = bf16[128,72,128]{2,1,0:T(8,128)(2,1)} custom-call(bf16[64,192,128]{2,1,0:T(8,128)(2,1)} %get-tuple-element.52.utaps_hbm, bf16[9,64,64]{2,1,0:T(8,128)(2,1)S(1)} %copy-done.3, f32[64,64,128]{2,1,0:T(8,128)} %get-tuple-element.40.grad_hbm, bf16[128,72,128]{2,1,0:T(8,128)(2,1)} %shard_map.114.big_in), custom_call_target="tpu_custom_call", output_to_operand_aliasing={{}: (3, {})} | custom-call | tf_op jit(solution)/shard_map/pallas_call | solution.py:619
  142.1 8.3 %all-to-all-done.5.r_ref = f32[128,8,128]{2,1,0:T(8,128)S(1)} async-done(((f32[128,8,128]{2,1,0:T(8,128)}), f32[128,8,128]{2,1,0:T(8,128)S(1)}, u32[]{:S(2)}, u32[]{:S(2)}) %all-to-all-start.5) | async-done | bytes 524320 | tf_op jit(solution)/shard_map/all_to_all | solution.py:634
  150.4 0.9 shard_map.119
  151.3 37.5 %all_to_all.64.r_ref = bf16[128,72,128]{2,1,0:T(8,128)(2,1)S(1)} all-to-all(bf16[128,72,128]{2,1,0:T(8,128)(2,1)} %shard_map.119), channel_id=1, replica_groups=mesh['row'=8,'col'=16] {'row','col'}, dimensions={0} | all-to-all | bytes 4718592 | tf_op jit(solution)/shard_map/all_to_all | solution.py:634
  188.9 5.4 %shard_map.120 = (bf16[64,64,128]{2,1,0:T(8,128)(2,1)}, bf16[37,64,128]{2,1,0:T(8,128)(2,1)}, f32[9,64,64]{2,1,0:T(8,128)}, f32[9,64,64]{2,1,0:T(8,128)}, f32[37,64]{1,0:T(8,128)}, /*index=5*/f32[1,37]{1,0:T(1,128)}) custom-call(bf16[128,72,128]{2,1,0:T(8,128)(2,1)S(1)} %all_to_all.64.r_ref), custom_call_target="tpu_custom_call" | custom-call | tf_op jit(solution)/shard_map/pallas_call | solution.py:619
  (6 shorter events, 0.0 us)
Async XLA Ops:
  0.6 1.2 copy-start
  1.9 1.1 copy-start.1
  6.8 41.5 %copy-start.3 = (bf16[9,64,64]{2,1,0:T(8,128)(2,1)S(1)}, bf16[9,64,64]{2,1,0:T(8,128)(2,1)}, u32[]{:S(2)}) copy-start(bf16[9,64,64]{2,1,0:T(8,128)(2,1)} %w_ref.7) | copy-start | bytes 221188
  48.3 19.6 %copy-start.2 = (bf16[9,64,64]{2,1,0:T(8,128)(2,1)S(1)}, bf16[9,64,64]{2,1,0:T(8,128)(2,1)}, u32[]{:S(2)}) copy-start(bf16[9,64,64]{2,1,0:T(8,128)(2,1)} %w_ref.6) | copy-start | bytes 221188
  48.3 28.5 %copy-start.5 = (f32[37]{0:T(128)S(1)}, f32[37]{0:T(128)}, u32[]{:S(2)}) copy-start(f32[37]{0:T(128)} %param.10) | copy-start | bytes 448
  48.3 28.5 %copy-start.4 = (bf16[37,64]{1,0:T(8,128)(2,1)S(1)}, bf16[37,64]{1,0:T(8,128)(2,1)}, u32[]{:S(2)}) copy-start(bf16[37,64]{1,0:T(8,128)(2,1)} %param.9) | copy-start | bytes 14212
  72.4 13.9 %all-to-all-start.2 = ((f32[128,1,128]{2,1,0:T(1,128)}), f32[128,1,128]{2,1,0:T(1,128)S(1)}, u32[]{:S(2)}, u32[]{:S(2)}) async-start(f32[128,1,128]{2,1,0:T(1,128)} %bitcast.4), calls=%async_computation.2 | async-start | bytes 131072 | tf_op jit(solution)/shard_map/all_to_all | solution.py:634
  91.0 14.5 %all-to-all-start.3 = ((f32[128,1,128]{2,1,0:T(1,128)}), f32[128,1,128]{2,1,0:T(1,128)S(1)}, u32[]{:S(2)}, u32[]{:S(2)}) async-start(f32[128,1,128]{2,1,0:T(1,128)} %bitcast.8), calls=%async_computation.3 | async-start | bytes 131072 | tf_op jit(solution)/shard_map/all_to_all | solution.py:634
  111.2 15.4 %all-to-all-start.4 = ((f32[128,1,128]{2,1,0:T(1,128)}), f32[128,1,128]{2,1,0:T(1,128)S(1)}, u32[]{:S(2)}, u32[]{:S(2)}) async-start(f32[128,1,128]{2,1,0:T(1,128)} %bitcast.11), calls=%async_computation.4 | async-start | bytes 131072 | tf_op jit(solution)/shard_map/all_to_all | solution.py:634
  132.4 18.0 %all-to-all-start.5 = ((f32[128,8,128]{2,1,0:T(8,128)}), f32[128,8,128]{2,1,0:T(8,128)S(1)}, u32[]{:S(2)}, u32[]{:S(2)}) async-start(f32[128,8,128]{2,1,0:T(8,128)} %get-tuple-element.51), calls=%async_computation.5 | async-start | bytes 1048576 | tf_op jit(solution)/shard_map/all_to_all | solution.py:634

commit v5 on v4

--- a/solution.py
+++ b/solution.py
@@ -18,7 +18,6 @@
 BINS = 37
 CELLS = float(1024 * 1024)
 OWN = float(64 * 128)
-WIDE = 24
 PARTS = 4
 
 
@@ -73,55 +72,63 @@
 def pack_kernel(f_ref, c_ref, o_ref, f_s, c_s):
     order = class_order()
     f_s[...] = f_ref[...].astype(F32)
+    for a in range(STEP):
+        parts = []
+        for h in range(2):
+            x = jnp.concatenate([f_s[:, 32 * h + a, :], f_s[:, 32 * h + 16 + a, :]], axis=0)
+            parts.append(dot_nt(order, x.astype(BF16)))
+        for b in range(STEP):
+            dest, slot = PLACE[(a, b)]
+            tile = jnp.concatenate([p[8 * b : 8 * b + 8] for p in parts], axis=0)
+            o_ref[dest, 16 * slot : 16 * slot + 16, :] = tile.astype(BF16)
     c_s[0:BINS] = c_ref[...].astype(F32)
     c_s[BINS:40] = jnp.zeros((40 - BINS, GRID, 128), F32)
-    pad = jnp.zeros((WIDE, 128), F32)
-
-    def feature(j):
-        return f_s[:, j, :]
-
-    def bins(j):
-        return jnp.concatenate([c_s[:, j, :], pad], axis=0)
-
-    for first, get in ((0, feature), (32, bins)):
-        for a in range(STEP):
-            parts = []
-            for h in range(2):
-                x = jnp.concatenate([get(32 * h + a), get(32 * h + 16 + a)], axis=0)
-                parts.append(dot_nt(order, x.astype(BF16)))
-            for b in range(STEP):
-                dest, slot = PLACE[(a, b)]
-                tile = jnp.concatenate([p[8 * b : 8 * b + 8] for p in parts], axis=0)
-                at = first + 16 * slot
-                o_ref[dest, at : at + 16, :] = tile.astype(BF16)
+    o_ref[:, 48:56, :] = jnp.zeros((DEVICES, 8, 128), BF16)
+    for a in range(STEP):
+        bins = [c_s[:, 16 * low + a, :] for low in range(4)]
+        x = jnp.concatenate([v[:32] for v in bins], axis=0)
+        main = dot_nt(order, x.astype(BF16))
+        x = jnp.concatenate([v[32:] for v in bins] * 2 + [jnp.zeros((64, 128), F32)], axis=0)
+        rest = dot_nt(order, x.astype(BF16))
+        for b in range(STEP):
+            dest, slot = PLACE[(a, b)]
+            span = slice(8 * b, 8 * b + 8)
+            at = 32 + 8 * slot
+            o_ref[dest, at : at + 8, :] = main[span].astype(BF16)
+            lanes = slice(32 * slot, 32 * slot + 32)
+            o_ref[dest, 48:56, lanes] = rest[span, lanes].astype(BF16)
 
 
 def last_kernel(r_ref, f_ref, l_ref, first_ref, second_ref, head_ref, bias_ref, f_s, c_s):
     back = class_order()
-
-    def feature(j, x):
-        f_s[:, j, :] = x
-
-    def bins(j, x):
-        c_s[:, j, :] = x[:40]
-
-    for first, put in ((0, feature), (32, bins)):
-        for a in range(STEP):
-            rows = [[], []]
-            for b in range(STEP):
-                src, slot = PLACE[(a, b)]
-                at = first + 16 * slot
-                tile = r_ref[src, at : at + 16, :].astype(F32)
-                rows[0].append(tile[:8])
-                rows[1].append(tile[8:])
-            for h in range(2):
-                z = jnp.concatenate(rows[h], axis=0)
-                x = dot(z.T.astype(BF16), back)
-                put(32 * h + a, x[:64])
-                put(32 * h + 16 + a, x[64:])
+    for a in range(STEP):
+        rows = [[], []]
+        for b in range(STEP):
+            src, slot = PLACE[(a, b)]
+            tile = r_ref[src, 16 * slot : 16 * slot + 16, :].astype(F32)
+            rows[0].append(tile[:8])
+            rows[1].append(tile[8:])
+        for h in range(2):
+            z = jnp.concatenate(rows[h], axis=0)
+            x = dot(z.T.astype(BF16), back)
+            f_s[:, 32 * h + a, :] = x[:64]
+            f_s[:, 32 * h + 16 + a, :] = x[64:]
     f_ref[...] = f_s[...].astype(BF16)
+    for a in range(STEP):
+        main, rest = [], []
+        for b in range(STEP):
+            src, slot = PLACE[(a, b)]
+            at = 32 + 8 * slot
+            main.append(r_ref[src, at : at + 8, :].astype(F32))
+            tile = r_ref[src, 48:56, :].astype(F32)
+            rest.append(pltpu.roll(tile, 96, 1) if slot else tile)
+        x = dot(jnp.concatenate(main, axis=0).T.astype(BF16), back)
+        y = dot(jnp.concatenate(rest, axis=0).T[:32].astype(BF16), back)
+        for low in range(4):
+            c_s[0:32, 16 * low + a, :] = x[32 * low : 32 * low + 32]
+            c_s[32:40, 16 * low + a, :] = y[8 * low : 8 * low + 8]
     l_ref[...] = c_s[0:BINS].astype(BF16)
-    tail = r_ref[:, 64:72, :].astype(F32) * (1.0 / 1024)
+    tail = r_ref[:, 56:64, :].astype(F32) * (1.0 / 1024)
 
     def fill(at, out_ref):
         low, mid, high = tail[:, at], tail[:, at + 1], tail[:, at + 2]
@@ -179,6 +186,51 @@
     lax.fori_loop(0, COLS, step, 0, unroll=8)
 
 
+def collect_bins(r_ref, put):
+    unit = eye(128)
+    lane = iota((32, 128), 1)
+
+    def step(col, carry):
+        main = [
+            r_ref[r * COLS + col, 8 * slot : 8 * slot + 8, :].astype(F32)
+            for slot in range(2)
+            for r in range(ROWS)
+        ]
+        rest = [r_ref[r * COLS + col, 16:24, :].astype(F32) for r in range(ROWS)] * 2
+        x = dot_nt(unit, jnp.concatenate(main, axis=0).astype(BF16))
+        y = dot_nt(unit, jnp.concatenate(rest, axis=0).astype(BF16))
+        y = jnp.where(lane < 64, y[:32], y[32:64])
+        for low in range(4):
+            put(
+                4 * col + low,
+                jnp.concatenate([x[32 * low : 32 * low + 32], y[8 * low : 8 * low + 8]], axis=0),
+            )
+        return carry
+
+    lax.fori_loop(0, COLS, step, 0, unroll=8)
+
+
+def spread_bins(o_ref, get):
+    unit = eye(128)
+    lane = iota((8, 128), 1)
+
+    def step(col, carry):
+        bins = [get(4 * col + low) for low in range(4)]
+        x = jnp.concatenate([v[:32] for v in bins], axis=0)
+        main = dot_nt(unit, x.astype(BF16))
+        x = jnp.concatenate([v[32:] for v in bins] * 2 + [jnp.zeros((64, 128), F32)], axis=0)
+        rest = dot_nt(unit, x.astype(BF16))
+        for r in range(ROWS):
+            for slot in range(2):
+                at = 64 * slot + 8 * r
+                o_ref[r * COLS + col, 8 * slot : 8 * slot + 8, :] = main[at : at + 8].astype(BF16)
+            tile = jnp.where(lane < 32, rest[8 * r : 8 * r + 8], rest[64 + 8 * r : 72 + 8 * r])
+            o_ref[r * COLS + col, 16:24, :] = tile.astype(BF16)
+        return carry
+
+    lax.fori_loop(0, COLS, step, 0, unroll=8)
+
+
 def put_taps(dst_ref, at, v):
     lane = iota((CH, 128), 1) % GRID
     dst_ref[at, 0:64, :] = jnp.where(lane == 0, 0.0, pltpu.roll(v, 1, 1)).astype(BF16)
@@ -337,7 +389,7 @@
         put_taps(taps_ref, j, v)
 
     collect(r_ref, 0, put)
-    out = pltpu.make_async_copy(taps_ref, taps_out, sem_out)
+    out = pltpu.make_async_copy(taps_ref.at[:, 64:128, :], taps_out, sem_out)
     out.start()
 
     def emit(j, v, total):
@@ -350,14 +402,14 @@
 
 
 def sym_kernel(flag_ref, r_hbm, sym_ref, r_ref, x_ref, k_ref, sem):
-    cells = pltpu.make_async_copy(r_hbm.at[:, 32:64, :], r_ref, sem)
+    cells = pltpu.make_async_copy(r_hbm.at[:, 32:56, :], r_ref, sem)
     cells.start()
     cells.wait()
 
     def put(j, v):
-        x_ref[j] = v[:40]
-
-    collect(r_ref, 0, put)
+        x_ref[j] = v
+
+    collect_bins(r_ref, put)
     symmetric(x_ref, k_ref, flag_ref[0])
     sym_ref[...] = x_ref[...].astype(BF16)
 
@@ -367,9 +419,8 @@
     cells.start()
     cells.wait()
     symmetric(x_ref, k_ref, flag_ref[0])
-    pad = jnp.zeros((WIDE, 128), F32)
-    spread(o_ref, 0, lambda j: jnp.concatenate([x_ref[j], pad], axis=0).astype(BF16))
-    out = pltpu.make_async_copy(o_ref, big_ref.at[:, 32:64, :], sem_out)
+    spread_bins(o_ref, lambda j: x_ref[j])
+    out = pltpu.make_async_copy(o_ref, big_ref.at[:, 32:56, :], sem_out)
     out.start()
     out.wait()
 
@@ -383,7 +434,7 @@
         return carry
 
     lax.fori_loop(0, GRID, step, 0, unroll=8)
-    taps_copy = pltpu.make_async_copy(taps_ref, taps_hbm, sem_taps)
+    taps_copy = pltpu.make_async_copy(taps_ref.at[:, 64:128, :], taps_hbm, sem_taps)
     taps_copy.start()
     outs = copies(out_ref, out_hbm, sem_out, ready)
 
@@ -405,12 +456,7 @@
     act_ref, mid_ref, grad_ref, raw_ref, sem_act, sem_mid, sem_grad, sem_raw
 ):
     acts = copies(act_hbm, act_ref, sem_act)
-    mids = [
-        pltpu.make_async_copy(
-            taps_hbm.at[whole(part), 64:128, :], mid_ref.at[whole(part)], sem_mid.at[part]
-        )
-        for part in range(PARTS)
-    ]
+    mids = copies(taps_hbm, mid_ref, sem_mid)
     for part in range(PARTS):
         acts[part].start()
         mids[part].start()
@@ -473,7 +519,8 @@
         normed = (act_ref[j] - mean) * inverse
         u = inverse * (grad_ref[j] - first_mean - normed * second_mean)
         u_ref[j + 1] = u.astype(BF16)
-        put_taps(utaps_ref, j, u)
+        if utaps_ref is not None:
+            put_taps(utaps_ref, j, u)
         return carry
 
     for part in range(PARTS):
@@ -520,13 +567,22 @@
     wait(outs)
 
 
-def terms_kernel(u_hbm, taps_hbm, term_ref, out_ref, u_ref, taps_ref, acc_ref, sem_u, sem_taps):
+def all_taps(mid_ref, taps_ref, first, last):
+    def step(j, carry):
+        put_taps(taps_ref, j, mid_ref[j].astype(F32))
+        return carry
+
+    lax.fori_loop(first, last, step, 0, unroll=8)
+
+
+def terms_kernel(u_hbm, taps_hbm, term_ref, out_ref, u_ref, mid_ref, taps_ref, acc_ref, sem_u, sem_taps):
+    taps_copy = pltpu.make_async_copy(taps_hbm, mid_ref, sem_taps)
+    taps_copy.start()
     u_copy = pltpu.make_async_copy(u_hbm, u_ref, sem_u)
     u_copy.start()
-    taps_copy = pltpu.make_async_copy(taps_hbm, taps_ref, sem_taps)
-    taps_copy.start()
+    taps_copy.wait()
+    all_taps(mid_ref, taps_ref, 0, GRID)
     u_copy.wait()
-    taps_copy.wait()
     weight_terms(u_ref, taps_ref, acc_ref)
     store_terms(acc_ref, out_ref)
     out_ref[288:328] = term_ref[...]
@@ -535,20 +591,21 @@
 
 def fifth_kernel(
     grad_hbm, table4_ref, act1_ref, table1_ref, taps_hbm, terms_ref,
-    part_ref, utaps_hbm,
-    grad_ref, taps_ref, utaps_ref, u_ref, acc_ref, buf_ref, sem_grad, sem_taps, sem_out
+    part_ref, u_hbm,
+    grad_ref, mid_ref, taps_ref, u_ref, acc_ref, buf_ref, sem_grad, sem_taps, sem_out
 ):
+    taps_copy = pltpu.make_async_copy(taps_hbm, mid_ref, sem_taps)
+    taps_copy.start()
     grads = copies(grad_hbm, grad_ref, sem_grad)
     start(grads)
-    taps_copy = pltpu.make_async_copy(taps_hbm, taps_ref, sem_taps)
-    taps_copy.start()
+    taps_copy.wait()
+    all_taps(mid_ref, taps_ref, 0, GRID)
     norm_back(
-        act1_ref, moments(table1_ref), grad_ref, means(table4_ref), u_ref, utaps_ref,
+        act1_ref, moments(table1_ref), grad_ref, means(table4_ref), u_ref, None,
         lambda part: grads[part].wait(),
     )
-    out = pltpu.make_async_copy(utaps_ref, utaps_hbm, sem_out)
+    out = pltpu.make_async_copy(u_ref.at[1:65], u_hbm, sem_out)
     out.start()
-    taps_copy.wait()
     weight_terms(u_ref, taps_ref, acc_ref)
     store_terms(acc_ref, buf_ref)
     buf_ref[288:384] = jnp.zeros((96, 128), F32)
@@ -561,18 +618,19 @@
 
 
 def sixth_kernel(
-    utaps_hbm, w_ref, grad_hbm, big_in, big_ref,
-    utaps_ref, grad_ref, x_ref, w_s, o_ref, sem_taps, sem_grad, sem_out
+    u_hbm, w_ref, grad_hbm, big_in, big_ref,
+    u_ref, utaps_ref, grad_ref, x_ref, w_s, o_ref, sem_u, sem_grad, sem_out
 ):
-    taps = copies(utaps_hbm, utaps_ref, sem_taps)
+    us = copies(u_hbm, u_ref, sem_u)
     grads = copies(grad_hbm, grad_ref, sem_grad)
     for part in range(PARTS):
-        taps[part].start()
+        us[part].start()
         grads[part].start()
     stack_weights(w_ref, w_s, True)
 
     def before(part):
-        taps[part].wait()
+        us[part].wait()
+        all_taps(u_ref, utaps_ref, 16 * part, 16 * part + 16)
         grads[part].wait()
 
     def emit(j, v, carry):
@@ -593,7 +651,7 @@
 
     total = lax.fori_loop(1, DEVICES, step, r_ref[0], unroll=8)
     o_ref[...] = jnp.broadcast_to(total.astype(BF16)[None], o_ref.shape)
-    copy = pltpu.make_async_copy(o_ref, big_ref.at[:, 64:72, :], sem)
+    copy = pltpu.make_async_copy(o_ref, big_ref.at[:, 56:64, :], sem)
     copy.start()
     copy.wait()
 
@@ -643,7 +701,8 @@
 ACC = ((192, 192), F32)
 PART = ((DEVICES, 8, 128), F32)
 TERMS = ((384, 128), F32)
-BIG = ((DEVICES, 72, 128), BF16)
+BIG = ((DEVICES, 64, 128), BF16)
+PACKED_BINS = ((DEVICES, 24, 128), BF16)
 PACKED = ((DEVICES, 32, 128), BF16)
 PLANES = ((CH, GRID, 128), F32)
 BINF = ((GRID, 40, 128), F32)
@@ -657,17 +716,17 @@
     head = jnp.pad(head_weight, ((0, 3), (0, 0)))
     bias = jnp.broadcast_to(jnp.pad(head_bias, (0, 3))[:, None], (40, 128))
 
-    sent = call(pack_kernel, [((DEVICES, 64, 128), BF16)], "vv", [PLANES, BINK])(
+    sent = call(pack_kernel, [((DEVICES, 56, 128), BF16)], "vv", [PLANES, BINK])(
         features, cotangent
     )[0]
     cells = exchange(sent)
     act1, stat, taps = call(
-        first_kernel, [FIELD, STAT, hbm(TAPS)], "hv", [PACKED, TAPS, STACK], (0, 0)
+        first_kernel, [FIELD, STAT, hbm(HALF)], "hv", [PACKED, TAPS, STACK], (0, 0)
     )(cells, conv_first)
     table1 = exchange(stat)
-    sym = call(sym_kernel, [BINH], "sh", [PACKED, BINF, BINK], (0,))(flag, cells)[0]
+    sym = call(sym_kernel, [BINH], "sh", [PACKED_BINS, BINF, BINK], (0,))(flag, cells)[0]
     act2, stat, taps2 = call(
-        second_kernel, [hbm(FIELD), STAT, hbm(TAPS)], "vvv", [FIELD, TAPS, STACK], (0, PARTS)
+        second_kernel, [hbm(FIELD), STAT, hbm(HALF)], "vvv", [FIELD, TAPS, STACK], (0, PARTS)
     )(act1, table1, conv_second)
     table2 = exchange(stat)
     table2, sym = lax.optimization_barrier((table2, sym))
@@ -679,7 +738,7 @@
         (PARTS,) * 4,
     )(act2, table2, taps, sym, head, bias)
     table3 = exchange(stat)
-    big = call(logit_kernel, [hbm(BIG)], "sh", [BINF, BINK, PACKED], (0, 0))(flag, raw)[0]
+    big = call(logit_kernel, [hbm(BIG)], "sh", [BINF, BINK, PACKED_BINS], (0, 0))(flag, raw)[0]
     table3, big = lax.optimization_barrier((table3, big))
     grad1, stat, u2 = call(
         fourth_kernel,
@@ -689,13 +748,13 @@
         (PARTS, PARTS, PARTS, 0),
     )(act2, table2, grad, table3, act1, table1, conv_second)
     table4 = exchange(stat)
-    terms2 = call(terms_kernel, [TERMS], "hhv", [PADDED, TAPS, ACC], (0, 0))(u2, taps2, term)[0]
+    terms2 = call(terms_kernel, [TERMS], "hhv", [PADDED, HALF, TAPS, ACC], (0, 0))(u2, taps2, term)[0]
     table4, terms2 = lax.optimization_barrier((table4, terms2))
-    part, utaps = call(
+    part, u1 = call(
         fifth_kernel,
-        [PART, hbm(TAPS)],
+        [PART, hbm(HALF)],
         "hvvvhv",
-        [FIELD, TAPS, TAPS, PADDED, ACC, TERMS],
+        [FIELD, HALF, TAPS, PADDED, ACC, TERMS],
         (PARTS, 0, 0),
     )(grad1, table4, act1, table1, taps, terms2)
     got = exchange(part)
@@ -703,10 +762,10 @@
         sixth_kernel,
         [hbm(BIG)],
         "hvhh",
-        [TAPS, FIELD, HALF, STACK, PACKED],
+        [HALF, TAPS, FIELD, HALF, STACK, PACKED],
         (PARTS, PARTS, 0),
         {3: 0},
-    )(utaps, conv_first, grad, big)[0]
+    )(u1, conv_first, grad, big)[0]
     big = call(share_kernel, [hbm(BIG)], "vh", [((DEVICES, 8, 128), BF16)], (0,), {1: 0})(got, big)[0]
     result = exchange(big)
     input_grad, logits, first, second, head_grad, bias_grad = call(

time: 195 us -> 188 us (0.964)
  blocking collectives: 94.6 us -> 88.5 us
    all_to_all x3, blocking collectives: 94.6 us -> 88.5 us  [exchange(): lax.all_to_all(x, ('row', 'col'), split_axis=0, concat_axis=0, tiled=True)]
where the time goes in v5:
time: 188 us; the launch traced here: 187 us
  blocking collectives  88.5 us (47%)
  Pallas kernels  53.7 us (29%)
  waiting for transfers between devices  22.4 us (12%)
  starting transfers between devices  19.2 us (10%)
  local copies, waits for them, and re-layouts  2.39 us (1%)
    all_to_all x3, blocking collectives, exchange(): lax.all_to_all(x, ('row', 'col'), split_axis=0, concat_axis=0, tiled=True)  88.5 us
    pallas_call x12, Pallas kernels, placed(): run(*(pltpu.with_memory_space_constraint(x, pltpu.HBM) if k == 'h' else x...  53.7 us
    all_to_all x4, waiting for transfers between devices, exchange(): lax.all_to_all(x, ('row', 'col'), split_axis=0, concat_axis=0, tiled=True)  22.4 us
    all_to_all x4, starting transfers between devices, exchange(): lax.all_to_all(x, ('row', 'col'), split_axis=0, concat_axis=0, tiled=True)  19.2 us
  transfers between devices with their start and end apart: 4, of which 4 were waited for; matrix products, arithmetic and copies ran while one was open for 0% of the time, Pallas kernels for 10%

profile of v5, /device:TPU:1, one launch (start us, length us, event | category | flops | bytes accessed | tf_op | source)
XLA Modules:
  0.0 186.9 jit_solution(13310318269432711754)
XLA Ops:
  0.6 0.0 copy-start
  0.6 1.2 copy-done
  1.9 1.1 copy-done.1
  2.9 3.6 %shard_map.109 = bf16[128,56,128]{2,1,0:T(8,128)(2,1)S(1)} custom-call(bf16[64,64,128]{2,1,0:T(8,128)(2,1)S(1)} %copy-done, bf16[37,64,128]{2,1,0:T(8,128)(2,1)S(1)} %copy-done.1), custom_call_target="tpu_custom_call" | custom-call | tf_op jit(solution)/shard_map/pallas_call | solution.py:677
  6.6 0.0 copy-start.2
  6.6 38.6 %all_to_all.62.r_hbm = bf16[128,56,128]{2,1,0:T(8,128)(2,1)} all-to-all(bf16[128,56,128]{2,1,0:T(8,128)(2,1)S(1)} %shard_map.109), channel_id=1, replica_groups=mesh['row'=8,'col'=16] {'row','col'}, dimensions={0} | all-to-all | bytes 3670016 | tf_op jit(solution)/shard_map/all_to_all | solution.py:692
  45.1 0.0 copy-done.3
  45.1 4.0 %shard_map.110 = (f32[64,64,128]{2,1,0:T(8,128)S(1)}, f32[128,128]{1,0:T(8,128)S(1)}, bf16[64,64,128]{2,1,0:T(8,128)(2,1)}) custom-call(bf16[128,56,128]{2,1,0:T(8,128)(2,1)} %all_to_all.62.r_hbm, bf16[9,64,64]{2,1,0:T(8,128)(2,1)S(1)} %copy-done.3), custom_call_target="tpu_custom_call" | custom-call | tf_op jit(solution)/shard_map/pallas_call | solution.py:677
  49.1 15.2 %all_to_all.63 = f32[128,1,128]{2,1,0:T(1,128)S(1)} all-to-all(f32[128,1,128]{2,1,0:T(1,128)S(1)} %bitcast.25), channel_id=1, replica_groups=mesh['row'=8,'col'=16] {'row','col'}, dimensions={0} | all-to-all | bytes 131072 | tf_op jit(solution)/shard_map/all_to_all | solution.py:692
  64.3 0.0 copy-done.2
  64.3 3.9 %shard_map.111 = (f32[64,64,128]{2,1,0:T(8,128)}, f32[128,128]{1,0:T(8,128)}, bf16[64,64,128]{2,1,0:T(8,128)(2,1)}) custom-call(f32[64,64,128]{2,1,0:T(8,128)S(1)} %get-tuple-element.33.act_ref.act1_ref, f32[128,128]{1,0:T(8,128)S(1)} %bitcast.18, bf16[9,64,64]{2,1,0:T(8,128)(2,1)S(1)} %copy-done.2), custom_call_target="tpu_custom_call" | custom-call | tf_op jit(solution)/shard_map/pallas_call | solution.py:677
  68.2 4.4 %all-to-all-start.2 = ((f32[128,1,128]{2,1,0:T(1,128)}), f32[128,1,128]{2,1,0:T(1,128)S(1)}, u32[]{:S(2)}, u32[]{:S(2)}) async-start(f32[128,1,128]{2,1,0:T(1,128)} %bitcast.4), calls=%async_computation.2 | async-start | bytes 131072 | tf_op jit(solution)/shard_map/all_to_all | solution.py:692
  72.6 0.0 copy-done.5
  72.6 0.0 copy-done.4
  72.7 4.5 %shard_map.112.sym_ref = bf16[64,40,128]{2,1,0:T(8,128)(2,1)S(1)} custom-call(s32[1]{0:T(128)} %bitcast.6.flag_ref, bf16[128,56,128]{2,1,0:T(8,128)(2,1)} %all_to_all.62.r_hbm), custom_call_target="tpu_custom_call" | custom-call | tf_op jit(solution)/shard_map/pallas_call | solution.py:677
  77.2 4.9 %all-to-all-done.2 = f32[128,1,128]{2,1,0:T(1,128)S(1)} async-done(((f32[128,1,128]{2,1,0:T(1,128)}), f32[128,1,128]{2,1,0:T(1,128)S(1)}, u32[]{:S(2)}, u32[]{:S(2)}) %all-to-all-start.2) | async-done | bytes 65568 | tf_op jit(solution)/shard_map/all_to_all | solution.py:692
  82.1 0.1 broadcast_in_dim.2.bias_ref
  82.2 4.6 %shard_map.113 = (f32[64,64,128]{2,1,0:T(8,128)}, f32[128,128]{1,0:T(8,128)}, f32[64,40,128]{2,1,0:T(8,128)}, f32[40,128]{1,0:T(8,128)S(1)}) custom-call(f32[64,64,128]{2,1,0:T(8,128)} %get-tuple-element.35.act_hbm, f32[128,128]{1,0:T(8,128)S(1)} %bitcast.21, bf16[64,64,128]{2,1,0:T(8,128)(2,1)} %get-tuple-element.38.taps_hbm, ...), custom_call_target="tpu_custom_call" | custom-call | tf_op jit(solution)/shard_map/pallas_call | solution.py:677
  86.8 4.8 %all-to-all-start.3 = ((f32[128,1,128]{2,1,0:T(1,128)}), f32[128,1,128]{2,1,0:T(1,128)S(1)}, u32[]{:S(2)}, u32[]{:S(2)}) async-start(f32[128,1,128]{2,1,0:T(1,128)} %bitcast.8), calls=%async_computation.3 | async-start | bytes 131072 | tf_op jit(solution)/shard_map/all_to_all | solution.py:692
  91.6 5.3 %shard_map.114.big_in = bf16[128,64,128]{2,1,0:T(8,128)(2,1)} custom-call(s32[1]{0:T(128)} %bitcast.6.flag_ref, f32[64,40,128]{2,1,0:T(8,128)} %get-tuple-element.42.raw_hbm), custom_call_target="tpu_custom_call" | custom-call | tf_op jit(solution)/shard_map/pallas_call | solution.py:677
  96.9 4.2 %all-to-all-done.3 = f32[128,1,128]{2,1,0:T(1,128)S(1)} async-done(((f32[128,1,128]{2,1,0:T(1,128)}), f32[128,1,128]{2,1,0:T(1,128)S(1)}, u32[]{:S(2)}, u32[]{:S(2)}) %all-to-all-start.3) | async-done | bytes 65568 | tf_op jit(solution)/shard_map/all_to_all | solution.py:692
  101.2 5.8 %shard_map.115 = (f32[64,64,128]{2,1,0:T(8,128)}, f32[128,128]{1,0:T(8,128)}, bf16[66,64,128]{2,1,0:T(8,128)(2,1)}) custom-call(f32[64,64,128]{2,1,0:T(8,128)} %get-tuple-element.35.act_hbm, f32[128,128]{1,0:T(8,128)S(1)} %bitcast.22, f32[64,64,128]{2,1,0:T(8,128)} %get-tuple-element.40.grad_hbm, f32[128,128]{1,0:T(8,128)S(1)} %bitcast.24, ...), custom_call_target="tpu_custom_call" | custom-call | tf_op jit(solution)/shard_map/pallas_call | solution.py:677
  106.9 5.5 %all-to-all-start.4 = ((f32[128,1,128]{2,1,0:T(1,128)}), f32[128,1,128]{2,1,0:T(1,128)S(1)}, u32[]{:S(2)}, u32[]{:S(2)}) async-start(f32[128,1,128]{2,1,0:T(1,128)} %bitcast.11), calls=%async_computation.4 | async-start | bytes 131072 | tf_op jit(solution)/shard_map/all_to_all | solution.py:692
  112.5 3.8 %shard_map.116.terms_ref = f32[384,128]{1,0:T(8,128)S(1)} custom-call(bf16[66,64,128]{2,1,0:T(8,128)(2,1)} %get-tuple-element.46.u_hbm, bf16[64,64,128]{2,1,0:T(8,128)(2,1)} %get-tuple-element.47.taps_hbm, f32[40,128]{1,0:T(8,128)S(1)} %get-tuple-element.48.term_ref), custom_call_target="tpu_custom_call" | custom-call | tf_op jit(solution)/shard_map/pallas_call | solution.py:677
  116.3 5.8 %all-to-all-done.4 = f32[128,1,128]{2,1,0:T(1,128)S(1)} async-done(((f32[128,1,128]{2,1,0:T(1,128)}), f32[128,1,128]{2,1,0:T(1,128)S(1)}, u32[]{:S(2)}, u32[]{:S(2)}) %all-to-all-start.4) | async-done | bytes 65568 | tf_op jit(solution)/shard_map/all_to_all | solution.py:692
  122.0 6.1 %shard_map.117 = (f32[128,8,128]{2,1,0:T(8,128)}, bf16[64,64,128]{2,1,0:T(8,128)(2,1)}) custom-call(f32[64,64,128]{2,1,0:T(8,128)} %get-tuple-element.44.grad_hbm, f32[128,128]{1,0:T(8,128)S(1)} %bitcast.23, f32[64,64,128]{2,1,0:T(8,128)S(1)} %get-tuple-element.33.act_ref.act1_ref, f32[128,128]{1,0:T(8,128)S(1)} %bitcast.20, ...), custom_call_target="tpu_custom_call" | custom-call | tf_op jit(solution)/shard_map/pallas_call | solution.py:677
  128.1 4.4 %all-to-all-start.5 = ((f32[128,8,128]{2,1,0:T(8,128)}), f32[128,8,128]{2,1,0:T(8,128)S(1)}, u32[]{:S(2)}, u32[]{:S(2)}) async-start(f32[128,8,128]{2,1,0:T(8,128)} %get-tuple-element.51), calls=%async_computation.5 | async-start | bytes 1048576 | tf_op jit(solution)/shard_map/all_to_all | solution.py:692
  132.5 6.1 %shard_map.118.big_in = bf16[128,64,128]{2,1,0:T(8,128)(2,1)} custom-call(bf16[64,64,128]{2,1,0:T(8,128)(2,1)} %get-tuple-element.52.u_hbm, bf16[9,64,64]{2,1,0:T(8,128)(2,1)S(1)} %copy-done.3, f32[64,64,128]{2,1,0:T(8,128)} %get-tuple-element.40.grad_hbm, bf16[128,64,128]{2,1,0:T(8,128)(2,1)} %shard_map.114.big_in), custom_call_target="tpu_custom_call", output_to_operand_aliasing={{}: (3, {})} | custom-call | tf_op jit(solution)/shard_map/pallas_call | solution.py:677
  138.6 7.5 %all-to-all-done.5.r_ref = f32[128,8,128]{2,1,0:T(8,128)S(1)} async-done(((f32[128,8,128]{2,1,0:T(8,128)}), f32[128,8,128]{2,1,0:T(8,128)S(1)}, u32[]{:S(2)}, u32[]{:S(2)}) %all-to-all-start.5) | async-done | bytes 524320 | tf_op jit(solution)/shard_map/all_to_all | solution.py:692
  146.0 1.0 shard_map.119
  147.0 34.7 %all_to_all.64.r_ref = bf16[128,64,128]{2,1,0:T(8,128)(2,1)S(1)} all-to-all(bf16[128,64,128]{2,1,0:T(8,128)(2,1)} %shard_map.119), channel_id=1, replica_groups=mesh['row'=8,'col'=16] {'row','col'}, dimensions={0} | all-to-all | bytes 4194304 | tf_op jit(solution)/shard_map/all_to_all | solution.py:692
  181.7 5.2 %shard_map.120 = (bf16[64,64,128]{2,1,0:T(8,128)(2,1)}, bf16[37,64,128]{2,1,0:T(8,128)(2,1)}, f32[9,64,64]{2,1,0:T(8,128)}, f32[9,64,64]{2,1,0:T(8,128)}, f32[37,64]{1,0:T(8,128)}, /*index=5*/f32[1,37]{1,0:T(1,128)}) custom-call(bf16[128,64,128]{2,1,0:T(8,128)(2,1)S(1)} %all_to_all.64.r_ref), custom_call_target="tpu_custom_call" | custom-call | tf_op jit(solution)/shard_map/pallas_call | solution.py:677
  (6 shorter events, 0.0 us)
Async XLA Ops:
  0.6 1.2 copy-start
  1.9 1.1 copy-start.1
  6.5 38.6 %copy-start.3 = (bf16[9,64,64]{2,1,0:T(8,128)(2,1)S(1)}, bf16[9,64,64]{2,1,0:T(8,128)(2,1)}, u32[]{:S(2)}) copy-start(bf16[9,64,64]{2,1,0:T(8,128)(2,1)} %w_ref.7) | copy-start | bytes 221188
  6.6 57.8 %copy-start.2 = (bf16[9,64,64]{2,1,0:T(8,128)(2,1)S(1)}, bf16[9,64,64]{2,1,0:T(8,128)(2,1)}, u32[]{:S(2)}) copy-start(bf16[9,64,64]{2,1,0:T(8,128)(2,1)} %w_ref.6) | copy-start | bytes 221188
  45.1 27.5 %copy-start.5 = (f32[37]{0:T(128)S(1)}, f32[37]{0:T(128)}, u32[]{:S(2)}) copy-start(f32[37]{0:T(128)} %param.10) | copy-start | bytes 448
  45.1 27.5 %copy-start.4 = (bf16[37,64]{1,0:T(8,128)(2,1)S(1)}, bf16[37,64]{1,0:T(8,128)(2,1)}, u32[]{:S(2)}) copy-start(bf16[37,64]{1,0:T(8,128)(2,1)} %param.9) | copy-start | bytes 14212
  68.2 13.9 %all-to-all-start.2 = ((f32[128,1,128]{2,1,0:T(1,128)}), f32[128,1,128]{2,1,0:T(1,128)S(1)}, u32[]{:S(2)}, u32[]{:S(2)}) async-start(f32[128,1,128]{2,1,0:T(1,128)} %bitcast.4), calls=%async_computation.2 | async-start | bytes 131072 | tf_op jit(solution)/shard_map/all_to_all | solution.py:692
  86.8 14.4 %all-to-all-start.3 = ((f32[128,1,128]{2,1,0:T(1,128)}), f32[128,1,128]{2,1,0:T(1,128)S(1)}, u32[]{:S(2)}, u32[]{:S(2)}) async-start(f32[128,1,128]{2,1,0:T(1,128)} %bitcast.8), calls=%async_computation.3 | async-start | bytes 131072 | tf_op jit(solution)/shard_map/all_to_all | solution.py:692
  106.9 15.1 %all-to-all-start.4 = ((f32[128,1,128]{2,1,0:T(1,128)}), f32[128,1,128]{2,1,0:T(1,128)S(1)}, u32[]{:S(2)}, u32[]{:S(2)}) async-start(f32[128,1,128]{2,1,0:T(1,128)} %bitcast.11), calls=%async_computation.4 | async-start | bytes 131072 | tf_op jit(solution)/shard_map/all_to_all | solution.py:692
  128.1 18.0 %all-to-all-start.5 = ((f32[128,8,128]{2,1,0:T(8,128)}), f32[128,8,128]{2,1,0:T(8,128)S(1)}, u32[]{:S(2)}, u32[]{:S(2)}) async-start(f32[128,8,128]{2,1,0:T(8,128)} %get-tuple-element.51), calls=%async_computation.5 | async-start | bytes 1048576 | tf_op jit(solution)/shard_map/all_to_all | solution.py:692

commit v6 on v5

--- a/solution.py
+++ b/solution.py
@@ -69,8 +69,15 @@
     return jnp.where(z > 0, 1.0, jnp.exp(jnp.minimum(z, 0.0)))
 
 
-def pack_kernel(f_ref, c_ref, o_ref, f_s, c_s):
+def pack_kernel(f_hbm, c_hbm, o_ref, f_ref, c_ref, f_s, c_s, sem_f, sem_c):
+    f_copy = pltpu.make_async_copy(f_hbm, f_ref, sem_f)
+    f_copy.start()
+    c_copy = pltpu.make_async_copy(c_hbm, c_ref, sem_c)
+    c_copy.start()
     order = class_order()
+    o_ref[:, 48:56, :] = jnp.zeros((DEVICES, 8, 128), BF16)
+    c_s[BINS:40] = jnp.zeros((40 - BINS, GRID, 128), F32)
+    f_copy.wait()
     f_s[...] = f_ref[...].astype(F32)
     for a in range(STEP):
         parts = []
@@ -81,9 +88,8 @@
             dest, slot = PLACE[(a, b)]
             tile = jnp.concatenate([p[8 * b : 8 * b + 8] for p in parts], axis=0)
             o_ref[dest, 16 * slot : 16 * slot + 16, :] = tile.astype(BF16)
+    c_copy.wait()
     c_s[0:BINS] = c_ref[...].astype(F32)
-    c_s[BINS:40] = jnp.zeros((40 - BINS, GRID, 128), F32)
-    o_ref[:, 48:56, :] = jnp.zeros((DEVICES, 8, 128), BF16)
     for a in range(STEP):
         bins = [c_s[:, 16 * low + a, :] for low in range(4)]
         x = jnp.concatenate([v[:32] for v in bins], axis=0)
@@ -99,7 +105,9 @@
             o_ref[dest, 48:56, lanes] = rest[span, lanes].astype(BF16)
 
 
-def last_kernel(r_ref, f_ref, l_ref, first_ref, second_ref, head_ref, bias_ref, f_s, c_s):
+def last_kernel(
+    r_ref, f_hbm, l_hbm, first_ref, second_ref, head_ref, bias_ref, f_ref, l_ref, f_s, c_s, sem_f, sem_l
+):
     back = class_order()
     for a in range(STEP):
         rows = [[], []]
@@ -114,6 +122,8 @@
             f_s[:, 32 * h + a, :] = x[:64]
             f_s[:, 32 * h + 16 + a, :] = x[64:]
     f_ref[...] = f_s[...].astype(BF16)
+    f_copy = pltpu.make_async_copy(f_ref, f_hbm, sem_f)
+    f_copy.start()
     for a in range(STEP):
         main, rest = [], []
         for b in range(STEP):
@@ -128,6 +138,8 @@
             c_s[0:32, 16 * low + a, :] = x[32 * low : 32 * low + 32]
             c_s[32:40, 16 * low + a, :] = y[8 * low : 8 * low + 8]
     l_ref[...] = c_s[0:BINS].astype(BF16)
+    l_copy = pltpu.make_async_copy(l_ref, l_hbm, sem_l)
+    l_copy.start()
     tail = r_ref[:, 56:64, :].astype(F32) * (1.0 / 1024)
 
     def fill(at, out_ref):
@@ -146,6 +158,8 @@
     high = fill(3, second_ref)
     head_ref[...] = high[32 : 32 + BINS, :64]
     bias_ref[...] = jnp.broadcast_to(high[:, 64:65], (128, 128)).T[0:1, 32 : 32 + BINS]
+    f_copy.wait()
+    l_copy.wait()
 
 
 def collect(r_ref, first, put):
@@ -318,7 +332,7 @@
         acc_ref[...] += dot_nt(jnp.concatenate(lhs, axis=1), jnp.concatenate(rhs, axis=1))
         return carry
 
-    lax.fori_loop(0, GRID // 4, step, 0, unroll=8)
+    lax.fori_loop(0, GRID // 4, step, 0, unroll=16)
 
 
 def own_row(first, second):
@@ -355,7 +369,7 @@
         off = act_ref[j] - mean
         return acc + off * off
 
-    square = lax.fori_loop(0, GRID, step, jnp.zeros((CH, 128), F32), unroll=8)
+    square = lax.fori_loop(0, GRID, step, jnp.zeros((CH, 128), F32), unroll=16)
     return own_row(total, square)
 
 
@@ -433,7 +447,7 @@
         put_taps(taps_ref, j, elu((act_ref[j] - mean) * inverse))
         return carry
 
-    lax.fori_loop(0, GRID, step, 0, unroll=8)
+    lax.fori_loop(0, GRID, step, 0, unroll=16)
     taps_copy = pltpu.make_async_copy(taps_ref.at[:, 64:128, :], taps_hbm, sem_taps)
     taps_copy.start()
     outs = copies(out_ref, out_hbm, sem_out, ready)
@@ -525,7 +539,7 @@
 
     for part in range(PARTS):
         before(part)
-        lax.fori_loop(16 * part, 16 * part + 16, step, 0, unroll=8)
+        lax.fori_loop(16 * part, 16 * part + 16, step, 0, unroll=16)
 
 
 def fourth_kernel(
@@ -572,7 +586,7 @@
         put_taps(taps_ref, j, mid_ref[j].astype(F32))
         return carry
 
-    lax.fori_loop(first, last, step, 0, unroll=8)
+    lax.fori_loop(first, last, step, 0, unroll=16)
 
 
 def terms_kernel(u_hbm, taps_hbm, term_ref, out_ref, u_ref, mid_ref, taps_ref, acc_ref, sem_u, sem_taps):
@@ -598,6 +612,11 @@
     taps_copy.start()
     grads = copies(grad_hbm, grad_ref, sem_grad)
     start(grads)
+    for p in range(3):
+        part_ref[:, 3 + p, :] = terms_ref[128 * p : 128 * p + 128]
+    for p in range(6, 8):
+        part_ref[:, p, :] = jnp.zeros((128, 128), F32)
+    buf_ref[288:384] = jnp.zeros((96, 128), F32)
     taps_copy.wait()
     all_taps(mid_ref, taps_ref, 0, GRID)
     norm_back(
@@ -608,12 +627,8 @@
     out.start()
     weight_terms(u_ref, taps_ref, acc_ref)
     store_terms(acc_ref, buf_ref)
-    buf_ref[288:384] = jnp.zeros((96, 128), F32)
     for p in range(3):
         part_ref[:, p, :] = buf_ref[128 * p : 128 * p + 128]
-        part_ref[:, 3 + p, :] = terms_ref[128 * p : 128 * p + 128]
-    for p in range(6, 8):
-        part_ref[:, p, :] = jnp.zeros((128, 128), F32)
     out.wait()
 
 
@@ -705,6 +720,8 @@
 PACKED_BINS = ((DEVICES, 24, 128), BF16)
 PACKED = ((DEVICES, 32, 128), BF16)
 PLANES = ((CH, GRID, 128), F32)
+CELLS_OUT = ((CH, GRID, 128), BF16)
+BINS_OUT = ((BINS, GRID, 128), BF16)
 BINF = ((GRID, 40, 128), F32)
 BINH = ((GRID, 40, 128), BF16)
 BINK = ((40, GRID, 128), F32)
@@ -716,9 +733,9 @@
     head = jnp.pad(head_weight, ((0, 3), (0, 0)))
     bias = jnp.broadcast_to(jnp.pad(head_bias, (0, 3))[:, None], (40, 128))
 
-    sent = call(pack_kernel, [((DEVICES, 56, 128), BF16)], "vv", [PLANES, BINK])(
-        features, cotangent
-    )[0]
+    sent = call(
+        pack_kernel, [((DEVICES, 56, 128), BF16)], "hh", [CELLS_OUT, BINS_OUT, PLANES, BINK], (0, 0)
+    )(features, cotangent)[0]
     cells = exchange(sent)
     act1, stat, taps = call(
         first_kernel, [FIELD, STAT, hbm(HALF)], "hv", [PACKED, TAPS, STACK], (0, 0)
@@ -771,15 +788,16 @@
     input_grad, logits, first, second, head_grad, bias_grad = call(
         last_kernel,
         [
-            ((CH, GRID, 128), BF16),
-            ((BINS, GRID, 128), BF16),
+            hbm(CELLS_OUT),
+            hbm(BINS_OUT),
             ((9, CH, CH), F32),
             ((9, CH, CH), F32),
             ((BINS, CH), F32),
             ((1, BINS), F32),
         ],
         "v",
-        [PLANES, BINK],
+        [CELLS_OUT, BINS_OUT, PLANES, BINK],
+        (0, 0),
     )(result)
     return logits, input_grad, first, second, head_grad, bias_grad.reshape(BINS)
 

time: 188 us -> 187 us (level)
  local copies, waits for them, and re-layouts: 2.39 us -> 0.1 us
    unnamed x12 -> x8, local copies, waits for them, and re-layouts: 2.3 us -> 0.02 us
where the time goes in v6:
time: 187 us; the launch traced here: 186 us
  blocking collectives  88.5 us (47%)
  Pallas kernels  54.4 us (29%)
  waiting for transfers between devices  23.2 us (12%)
  starting transfers between devices  19.2 us (10%)
    all_to_all x3, blocking collectives, exchange(): lax.all_to_all(x, ('row', 'col'), split_axis=0, concat_axis=0, tiled=True)  88.5 us
    pallas_call x12, Pallas kernels, placed(): run(*(pltpu.with_memory_space_constraint(x, pltpu.HBM) if k == 'h' else x...  54.4 us
    all_to_all x4, waiting for transfers between devices, exchange(): lax.all_to_all(x, ('row', 'col'), split_axis=0, concat_axis=0, tiled=True)  23.2 us
    all_to_all x4, starting transfers between devices, exchange(): lax.all_to_all(x, ('row', 'col'), split_axis=0, concat_axis=0, tiled=True)  19.2 us
  transfers between devices with their start and end apart: 4, of which 4 were waited for; matrix products, arithmetic and copies ran while one was open for 0% of the time, Pallas kernels for 10%

profile of v6, /device:TPU:1, one launch (start us, length us, event | category | flops | bytes accessed | tf_op | source)
XLA Modules:
  0.0 186.3 jit_solution(1719865641827581750)
XLA Ops:
  0.6 4.9 %shard_map.109 = bf16[128,56,128]{2,1,0:T(8,128)(2,1)S(1)} custom-call(bf16[64,64,128]{2,1,0:T(8,128)(2,1)} %f_hbm.1, bf16[37,64,128]{2,1,0:T(8,128)(2,1)} %c_hbm.1), custom_call_target="tpu_custom_call" | custom-call | tf_op jit(solution)/shard_map/pallas_call | solution.py:692
  5.6 0.0 copy-start.1
  5.6 0.0 copy-start
  5.6 38.6 %all_to_all.62.r_hbm = bf16[128,56,128]{2,1,0:T(8,128)(2,1)} all-to-all(bf16[128,56,128]{2,1,0:T(8,128)(2,1)S(1)} %shard_map.109), channel_id=1, replica_groups=mesh['row'=8,'col'=16] {'row','col'}, dimensions={0} | all-to-all | bytes 3670016 | tf_op jit(solution)/shard_map/all_to_all | solution.py:707
  44.1 0.0 copy-done.1
  44.1 0.0 copy-start.3
  44.2 0.0 copy-start.2
  44.2 4.0 %shard_map.110 = (f32[64,64,128]{2,1,0:T(8,128)S(1)}, f32[128,128]{1,0:T(8,128)S(1)}, bf16[64,64,128]{2,1,0:T(8,128)(2,1)}) custom-call(bf16[128,56,128]{2,1,0:T(8,128)(2,1)} %all_to_all.62.r_hbm, bf16[9,64,64]{2,1,0:T(8,128)(2,1)S(1)} %copy-done.1), custom_call_target="tpu_custom_call" | custom-call | tf_op jit(solution)/shard_map/pallas_call | solution.py:692
  48.1 15.2 %all_to_all.63 = f32[128,1,128]{2,1,0:T(1,128)S(1)} all-to-all(f32[128,1,128]{2,1,0:T(1,128)S(1)} %bitcast.25), channel_id=1, replica_groups=mesh['row'=8,'col'=16] {'row','col'}, dimensions={0} | all-to-all | bytes 131072 | tf_op jit(solution)/shard_map/all_to_all | solution.py:707
  63.3 0.0 copy-done
  63.3 3.7 %shard_map.111 = (f32[64,64,128]{2,1,0:T(8,128)}, f32[128,128]{1,0:T(8,128)}, bf16[64,64,128]{2,1,0:T(8,128)(2,1)}) custom-call(f32[64,64,128]{2,1,0:T(8,128)S(1)} %get-tuple-element.33.act_ref.act1_ref, f32[128,128]{1,0:T(8,128)S(1)} %bitcast.18, bf16[9,64,64]{2,1,0:T(8,128)(2,1)S(1)} %copy-done), custom_call_target="tpu_custom_call" | custom-call | tf_op jit(solution)/shard_map/pallas_call | solution.py:692
  67.1 4.4 %all-to-all-start.2 = ((f32[128,1,128]{2,1,0:T(1,128)}), f32[128,1,128]{2,1,0:T(1,128)S(1)}, u32[]{:S(2)}, u32[]{:S(2)}) async-start(f32[128,1,128]{2,1,0:T(1,128)} %bitcast.4), calls=%async_computation.2 | async-start | bytes 131072 | tf_op jit(solution)/shard_map/all_to_all | solution.py:707
  71.5 0.0 copy-done.3
  71.5 0.0 copy-done.2
  71.5 4.5 %shard_map.112.sym_ref = bf16[64,40,128]{2,1,0:T(8,128)(2,1)S(1)} custom-call(s32[1]{0:T(128)} %bitcast.6.flag_ref, bf16[128,56,128]{2,1,0:T(8,128)(2,1)} %all_to_all.62.r_hbm), custom_call_target="tpu_custom_call" | custom-call | tf_op jit(solution)/shard_map/pallas_call | solution.py:692
  76.1 4.9 %all-to-all-done.2 = f32[128,1,128]{2,1,0:T(1,128)S(1)} async-done(((f32[128,1,128]{2,1,0:T(1,128)}), f32[128,1,128]{2,1,0:T(1,128)S(1)}, u32[]{:S(2)}, u32[]{:S(2)}) %all-to-all-start.2) | async-done | bytes 65568 | tf_op jit(solution)/shard_map/all_to_all | solution.py:707
  81.0 0.1 broadcast_in_dim.2.bias_ref
  81.1 4.6 %shard_map.113 = (f32[64,64,128]{2,1,0:T(8,128)}, f32[128,128]{1,0:T(8,128)}, f32[64,40,128]{2,1,0:T(8,128)}, f32[40,128]{1,0:T(8,128)S(1)}) custom-call(f32[64,64,128]{2,1,0:T(8,128)} %get-tuple-element.35.act_hbm, f32[128,128]{1,0:T(8,128)S(1)} %bitcast.21, bf16[64,64,128]{2,1,0:T(8,128)(2,1)} %get-tuple-element.38.taps_hbm, ...), custom_call_target="tpu_custom_call" | custom-call | tf_op jit(solution)/shard_map/pallas_call | solution.py:692
  85.7 4.8 %all-to-all-start.3 = ((f32[128,1,128]{2,1,0:T(1,128)}), f32[128,1,128]{2,1,0:T(1,128)S(1)}, u32[]{:S(2)}, u32[]{:S(2)}) async-start(f32[128,1,128]{2,1,0:T(1,128)} %bitcast.8), calls=%async_computation.3 | async-start | bytes 131072 | tf_op jit(solution)/shard_map/all_to_all | solution.py:707
  90.5 5.3 %shard_map.114.big_in = bf16[128,64,128]{2,1,0:T(8,128)(2,1)} custom-call(s32[1]{0:T(128)} %bitcast.6.flag_ref, f32[64,40,128]{2,1,0:T(8,128)} %get-tuple-element.42.raw_hbm), custom_call_target="tpu_custom_call" | custom-call | tf_op jit(solution)/shard_map/pallas_call | solution.py:692
  95.8 4.2 %all-to-all-done.3 = f32[128,1,128]{2,1,0:T(1,128)S(1)} async-done(((f32[128,1,128]{2,1,0:T(1,128)}), f32[128,1,128]{2,1,0:T(1,128)S(1)}, u32[]{:S(2)}, u32[]{:S(2)}) %all-to-all-start.3) | async-done | bytes 65568 | tf_op jit(solution)/shard_map/all_to_all | solution.py:707
  100.0 5.6 %shard_map.115 = (f32[64,64,128]{2,1,0:T(8,128)}, f32[128,128]{1,0:T(8,128)}, bf16[66,64,128]{2,1,0:T(8,128)(2,1)}) custom-call(f32[64,64,128]{2,1,0:T(8,128)} %get-tuple-element.35.act_hbm, f32[128,128]{1,0:T(8,128)S(1)} %bitcast.22, f32[64,64,128]{2,1,0:T(8,128)} %get-tuple-element.40.grad_hbm, f32[128,128]{1,0:T(8,128)S(1)} %bitcast.24, ...), custom_call_target="tpu_custom_call" | custom-call | tf_op jit(solution)/shard_map/pallas_call | solution.py:692
  105.6 5.5 %all-to-all-start.4 = ((f32[128,1,128]{2,1,0:T(1,128)}), f32[128,1,128]{2,1,0:T(1,128)S(1)}, u32[]{:S(2)}, u32[]{:S(2)}) async-start(f32[128,1,128]{2,1,0:T(1,128)} %bitcast.11), calls=%async_computation.4 | async-start | bytes 131072 | tf_op jit(solution)/shard_map/all_to_all | solution.py:707
  111.2 3.3 %shard_map.116.terms_ref = f32[384,128]{1,0:T(8,128)S(1)} custom-call(bf16[66,64,128]{2,1,0:T(8,128)(2,1)} %get-tuple-element.46.u_hbm, bf16[64,64,128]{2,1,0:T(8,128)(2,1)} %get-tuple-element.47.taps_hbm, f32[40,128]{1,0:T(8,128)S(1)} %get-tuple-element.48.term_ref), custom_call_target="tpu_custom_call" | custom-call | tf_op jit(solution)/shard_map/pallas_call | solution.py:692
  114.4 6.2 %all-to-all-done.4 = f32[128,1,128]{2,1,0:T(1,128)S(1)} async-done(((f32[128,1,128]{2,1,0:T(1,128)}), f32[128,1,128]{2,1,0:T(1,128)S(1)}, u32[]{:S(2)}, u32[]{:S(2)}) %all-to-all-start.4) | async-done | bytes 65568 | tf_op jit(solution)/shard_map/all_to_all | solution.py:707
  120.7 5.9 %shard_map.117 = (f32[128,8,128]{2,1,0:T(8,128)}, bf16[64,64,128]{2,1,0:T(8,128)(2,1)}) custom-call(f32[64,64,128]{2,1,0:T(8,128)} %get-tuple-element.44.grad_hbm, f32[128,128]{1,0:T(8,128)S(1)} %bitcast.23, f32[64,64,128]{2,1,0:T(8,128)S(1)} %get-tuple-element.33.act_ref.act1_ref, f32[128,128]{1,0:T(8,128)S(1)} %bitcast.20, ...), custom_call_target="tpu_custom_call" | custom-call | tf_op jit(solution)/shard_map/pallas_call | solution.py:692
  126.6 4.4 %all-to-all-start.5 = ((f32[128,8,128]{2,1,0:T(8,128)}), f32[128,8,128]{2,1,0:T(8,128)S(1)}, u32[]{:S(2)}, u32[]{:S(2)}) async-start(f32[128,8,128]{2,1,0:T(8,128)} %get-tuple-element.51), calls=%async_computation.5 | async-start | bytes 1048576 | tf_op jit(solution)/shard_map/all_to_all | solution.py:707
  131.0 5.8 %shard_map.118.big_in = bf16[128,64,128]{2,1,0:T(8,128)(2,1)} custom-call(bf16[64,64,128]{2,1,0:T(8,128)(2,1)} %get-tuple-element.52.u_hbm, bf16[9,64,64]{2,1,0:T(8,128)(2,1)S(1)} %copy-done.1, f32[64,64,128]{2,1,0:T(8,128)} %get-tuple-element.40.grad_hbm, bf16[128,64,128]{2,1,0:T(8,128)(2,1)} %shard_map.114.big_in), custom_call_target="tpu_custom_call", output_to_operand_aliasing={{}: (3, {})} | custom-call | tf_op jit(solution)/shard_map/pallas_call | solution.py:692
  136.8 7.8 %all-to-all-done.5.r_ref = f32[128,8,128]{2,1,0:T(8,128)S(1)} async-done(((f32[128,8,128]{2,1,0:T(8,128)}), f32[128,8,128]{2,1,0:T(8,128)S(1)}, u32[]{:S(2)}, u32[]{:S(2)}) %all-to-all-start.5) | async-done | bytes 524320 | tf_op jit(solution)/shard_map/all_to_all | solution.py:707
  144.6 1.0 shard_map.119
  145.5 34.7 %all_to_all.64.r_ref = bf16[128,64,128]{2,1,0:T(8,128)(2,1)S(1)} all-to-all(bf16[128,64,128]{2,1,0:T(8,128)(2,1)} %shard_map.119), channel_id=1, replica_groups=mesh['row'=8,'col'=16] {'row','col'}, dimensions={0} | all-to-all | bytes 4194304 | tf_op jit(solution)/shard_map/all_to_all | solution.py:707
  180.2 5.9 %shard_map.120 = (bf16[64,64,128]{2,1,0:T(8,128)(2,1)}, bf16[37,64,128]{2,1,0:T(8,128)(2,1)}, f32[9,64,64]{2,1,0:T(8,128)}, f32[9,64,64]{2,1,0:T(8,128)}, f32[37,64]{1,0:T(8,128)}, /*index=5*/f32[1,37]{1,0:T(1,128)}) custom-call(bf16[128,64,128]{2,1,0:T(8,128)(2,1)S(1)} %all_to_all.64.r_ref), custom_call_target="tpu_custom_call" | custom-call | tf_op jit(solution)/shard_map/pallas_call | solution.py:692
  (2 shorter events, 0.0 us)
Async XLA Ops:
  5.6 38.6 %copy-start.1 = (bf16[9,64,64]{2,1,0:T(8,128)(2,1)S(1)}, bf16[9,64,64]{2,1,0:T(8,128)(2,1)}, u32[]{:S(2)}) copy-start(bf16[9,64,64]{2,1,0:T(8,128)(2,1)} %w_ref.7) | copy-start | bytes 221188
  5.6 57.7 %copy-start = (bf16[9,64,64]{2,1,0:T(8,128)(2,1)S(1)}, bf16[9,64,64]{2,1,0:T(8,128)(2,1)}, u32[]{:S(2)}) copy-start(bf16[9,64,64]{2,1,0:T(8,128)(2,1)} %w_ref.6) | copy-start | bytes 221188
  44.1 27.3 %copy-start.3 = (f32[37]{0:T(128)S(1)}, f32[37]{0:T(128)}, u32[]{:S(2)}) copy-start(f32[37]{0:T(128)} %param.10) | copy-start | bytes 448
  44.2 27.4 %copy-start.2 = (bf16[37,64]{1,0:T(8,128)(2,1)S(1)}, bf16[37,64]{1,0:T(8,128)(2,1)}, u32[]{:S(2)}) copy-start(bf16[37,64]{1,0:T(8,128)(2,1)} %param.9) | copy-start | bytes 14212
  67.1 13.9 %all-to-all-start.2 = ((f32[128,1,128]{2,1,0:T(1,128)}), f32[128,1,128]{2,1,0:T(1,128)S(1)}, u32[]{:S(2)}, u32[]{:S(2)}) async-start(f32[128,1,128]{2,1,0:T(1,128)} %bitcast.4), calls=%async_computation.2 | async-start | bytes 131072 | tf_op jit(solution)/shard_map/all_to_all | solution.py:707
  85.7 14.4 %all-to-all-start.3 = ((f32[128,1,128]{2,1,0:T(1,128)}), f32[128,1,128]{2,1,0:T(1,128)S(1)}, u32[]{:S(2)}, u32[]{:S(2)}) async-start(f32[128,1,128]{2,1,0:T(1,128)} %bitcast.8), calls=%async_computation.3 | async-start | bytes 131072 | tf_op jit(solution)/shard_map/all_to_all | solution.py:707
  105.6 15.1 %all-to-all-start.4 = ((f32[128,1,128]{2,1,0:T(1,128)}), f32[128,1,128]{2,1,0:T(1,128)S(1)}, u32[]{:S(2)}, u32[]{:S(2)}) async-start(f32[128,1,128]{2,1,0:T(1,128)} %bitcast.11), calls=%async_computation.4 | async-start | bytes 131072 | tf_op jit(solution)/shard_map/all_to_all | solution.py:707
  126.6 18.0 %all-to-all-start.5 = ((f32[128,8,128]{2,1,0:T(8,128)}), f32[128,8,128]{2,1,0:T(8,128)S(1)}, u32[]{:S(2)}, u32[]{:S(2)}) async-start(f32[128,8,128]{2,1,0:T(8,128)} %get-tuple-element.51), calls=%async_computation.5 | async-start | bytes 1048576 | tf_op jit(solution)/shard_map/all_to_all | solution.py:707
